TPU v7x, 512 devices: a whole 4x8x8 slice. The times are simulated.
512 devices in a mesh: expert: 32 (over y, x), tensor: 16 (over z, core).
Axes of the slice: x: 4, y: 8, z: 8, core: 2. Of those that a mesh axis runs over, the one named last changes fastest.
Arguments:
- residual: bfloat16 [2048, 7168], P('expert', 'tensor'), may hold values from -40 to 40
- attn_parts: bfloat16 [16, 2048, 7168], P('tensor', 'expert'), may hold values from -2 to 2
- norm_gain: bfloat16 [7168], P('tensor'), may hold values from 0.099609375 to 1.8984375
- routes: int32 [2048, 8], P('expert'), may hold values from 0 to 31, all different within a row; in each aligned block of 64 rows (0 to 63, 64 to 127, ...) at most 24 rows name the same one
- route_weights: float32 [2048, 8], P('expert'), may hold values from 0.05 to 0.6
- w_gate: bfloat16 [32, 7168, 2048], P('expert', None, 'tensor'), may hold values from -0.06023809 to 0.06023809
- w_gate_q: bfloat16 [32, 7168, 2048], P('expert', None, 'tensor'), may hold values from -0.09567226 to 0.09567226
Outputs:
- token_error: float32 [2048], P('expert')
- expert_error: float32 [32], P('expert')
- hess_diag: float32 [32, 7168], P('expert', 'tensor')
Inputs may be any that keep to these rules, and one draw needn't show every extreme that they name: `routes`: no expert is named by more than 24 of the rows of one device, and in every draw some expert is named by exactly 24 of them; the 8 experts of a token are distinct; every expert is named by some token.
All inputs are finite; a program needn't handle non-finite values.
Results may differ from a plain program's by a relative error of at most 0.0023.
Values may be sent and summed in bfloat16 or wider, within the bound.
A program may use at most 64 MiB of HBM per device.

v0:
```python
import jax
import jax.numpy as jnp
from jax import lax
from jax.sharding import PartitionSpec as P

D = 7168
FF = 2048
CAP = 24


epsilon = 1e-06


def per_device(residual, attn_parts, norm_gain, routes, route_weights, w_gate, w_gate_q):
    n_expert = lax.axis_size("expert")
    tok_count = residual.shape[0]
    local_cols = residual.shape[1]
    top_count = routes.shape[1]
    gain_wide = norm_gain.astype(jnp.float32)[None, :]
    summed = lax.psum_scatter(
        attn_parts[0].astype(jnp.float32).astype(jnp.bfloat16),
        "tensor",
        scatter_dimension=1,
        tiled=True,
    ).astype(jnp.float32)
    hidden = residual.astype(jnp.float32) + summed
    squares = lax.psum(jnp.sum(hidden * hidden, axis=1), "tensor")
    scaling = lax.rsqrt(squares / D + epsilon)
    normed = (hidden * scaling[:, None] * gain_wide).astype(jnp.bfloat16)
    expert_ids = jnp.arange(n_expert, dtype=jnp.int32)
    flat_routes = routes.reshape(-1)
    one_hot = (flat_routes[:, None] == expert_ids[None, :]).astype(jnp.int32)
    earlier = jnp.cumsum(one_hot, axis=0) - one_hot
    slot_index = jnp.sum(earlier * one_hot, axis=1)
    target = flat_routes * CAP + slot_index
    load_counts = jnp.sum(one_hot, axis=0)
    slot_ids = jnp.arange(n_expert * CAP, dtype=jnp.int32)
    placing = (slot_ids[:, None] == target[None, :]).reshape(n_expert * CAP, tok_count, top_count)
    dispatch = jnp.sum(placing.astype(jnp.int32), axis=2).astype(jnp.bfloat16)
    count_send = load_counts.astype(jnp.bfloat16).reshape(n_expert, 1)
    weight_full = w_gate[0]
    weight_quant = w_gate_q[0]
    outgoing = jnp.dot(dispatch, normed, preferred_element_type=jnp.float32).astype(jnp.bfloat16)
    outgoing = outgoing.reshape(n_expert, CAP, local_cols)
    arrived, arrived_counts = (
        lax.all_to_all(outgoing, "expert", split_axis=0, concat_axis=0, tiled=True),
        lax.all_to_all(count_send, "expert", split_axis=0, concat_axis=0, tiled=True),
    )
    own_block = arrived.reshape(n_expert * CAP, local_cols)
    column_block = lax.all_gather(own_block, "tensor", axis=1, tiled=True)
    full_acc = jnp.dot(column_block, weight_full, preferred_element_type=jnp.float32)
    quant_acc = jnp.dot(column_block, weight_quant, preferred_element_type=jnp.float32)
    block_squares = jnp.einsum("rc,rc->c", own_block, own_block, preferred_element_type=jnp.float32)
    total_load = jnp.sum(arrived_counts.astype(jnp.float32))
    hess_local = 2.0 * block_squares / total_load
    difference = full_acc - quant_acc
    err_part = (jnp.sum(difference * difference, axis=1) / FF).reshape(n_expert, CAP)
    pow_part = (jnp.sum(full_acc * full_acc, axis=1) / FF).reshape(n_expert, CAP)
    err_slots, pow_slots = lax.psum((err_part, pow_part), "tensor")
    expert_total = jnp.sum(err_slots) / (jnp.sum(pow_slots) + epsilon)
    back_err, back_pow = (
        lax.all_to_all(err_slots, "expert", split_axis=0, concat_axis=0, tiled=True),
        lax.all_to_all(pow_slots, "expert", split_axis=0, concat_axis=0, tiled=True),
    )
    token_err = jnp.take(back_err.reshape(-1), target).reshape(tok_count, top_count)
    token_pow = jnp.take(back_pow.reshape(-1), target).reshape(tok_count, top_count)
    ratios = token_err / (token_pow + epsilon)
    token_error = jnp.sum(route_weights * ratios, axis=1)
    return (token_error, expert_total.reshape(1), hess_local.reshape(1, local_cols))


def solution(mesh):
    placed = (
        P("expert", "tensor"),
        P("tensor", "expert", None),
        P("tensor"),
        P("expert", None),
        P("expert", None),
        P("expert", None, "tensor"),
        P("expert", None, "tensor"),
    )
    return jax.shard_map(
        per_device,
        mesh=mesh,
        in_specs=placed,
        out_specs=(P("expert"), P("expert"), P("expert", "tensor")),
        check_vma=False,
    )
```

profile of v0, /device:TPU:1, one launch (start us, length us, event | category | flops | bytes accessed | tf_op | source)
XLA Modules:
  0.0 300.3 jit_solution(2115498877063809150)
XLA Ops:
  7.2 2.7 copy.57
  10.1 0.1 copy.40
  10.2 0.1 eq.40
  10.3 0.1 eq.44
  10.4 1.2 reduce-window.6
  11.6 0.2 slice_reduce_fusion
  11.8 0.2 convert_reduce_fusion.1
  12.0 0.1 reduce_sum.93
  12.1 0.1 copy.44
  12.2 0.5 convert_reduce_fusion
  12.8 63.0 %reduce-scatter.4.cloned.1.call-done = bf16[448,64]{1,0:T(8,128)(2,1)} async-done(((bf16[7168,64]{1,0:T(8,128)(2,1)}), bf16[448,64]{1,0:T(8,128)(2,1)}) %reduce-scatter.4.cloned.1.call-update) | async-done | bytes 57360
  75.7 1.0 copy.58
  76.7 0.1 multiply_reduce_fusion.1
  76.9 26.5 %psum.21 = f32[64]{0:T(128)S(1)} all-reduce(f32[64]{0:T(128)S(1)} %multiply_reduce_fusion.1), channel_id=1, replica_groups=mesh['expert'=32,'tensor'=16] {'tensor'}, use_global_device_ids=true, to_apply=%region_6.7 | all-reduce | flops 64 | bytes 512 | tf_op jit(solution)/shard_map/psum | solution.py:27
  103.4 0.5 convolution_convert_fusion
  103.8 0.3 copy.45
  104.1 30.1 %all_to_all.29 = bf16[32,24,448]{2,1,0:T(8,128)(2,1)S(1)} all-to-all(bf16[32,24,448]{2,1,0:T(8,128)(2,1)S(1)} %bitcast.49), channel_id=1, replica_groups=mesh['expert'=32,'tensor'=16] {'expert'}, dimensions={0} | all-to-all | bytes 1376256 | tf_op jit(solution)/shard_map/all_to_all | solution.py:46
  134.2 1.1 copy.46
  135.4 0.7 copy.50
  136.1 5.8 %all-to-all-start.3 = ((bf16[32,1,1]{2,1,0:T(2,128)(2,1)}), bf16[32,1,1]{2,1,0:T(2,128)(2,1)S(1)}, u32[]{:S(2)}, u32[]{:S(2)}) async-start(bf16[32,1,1]{2,1,0:T(2,128)(2,1)} %copy.50), calls=%async_computation.3 | async-start | bytes 32768 | tf_op jit(solution)/shard_map/all_to_all | solution.py:47
  141.9 0.1 copy.49
  142.0 8.5 %all-to-all-done.3 = bf16[32,1,1]{2,1,0:T(2,128)(2,1)S(1)} async-done(((bf16[32,1,1]{2,1,0:T(2,128)(2,1)}), bf16[32,1,1]{2,1,0:T(2,128)(2,1)S(1)}, u32[]{:S(2)}, u32[]{:S(2)}) %all-to-all-start.3) | async-done | bytes 96 | tf_op jit(solution)/shard_map/all_to_all | solution.py:47
  150.5 0.6 convert_reduce_fusion.2
  151.1 51.8 %all-gather.2.cloned.1.call-done = bf16[768,7168]{0,1:T(8,128)(2,1)} async-done(((bf16[768,448]{0,1:T(8,128)(2,1)}), bf16[768,7168]{0,1:T(8,128)(2,1)}) %all-gather.2.cloned.1.call-update) | async-done | bytes 11010064 | tf_op jit(solution)/shard_map/all_gather | solution.py:50
  202.9 6.0 %multiply_reduce_fusion = (f32[768]{0:T(1024)S(1)}, f32[768,128]{0,1:T(8,128)S(1)}) fusion(bf16[768,7168]{0,1:T(8,128)(2,1)} %all-gather.2.cloned.1.call-done, bf16[1,7168,128]{2,1,0:T(8,128)(2,1)S(1)} %copy-done), kind=kOutput, calls=%fused_computation.14 | convolution fusion | flops 1409481984 | bytes 13241344 | tf_op jit(solution)/shard_map/dot_general | solution.py:51
  209.0 1.2 copy-done.5
  210.2 0.5 copy-done.6
  210.7 1.8 fusion.11
  212.5 0.1 div.34
  212.6 0.1 div.36
  212.7 43.4 %all-reduce = (f32[32,24]{1,0:T(8,128)}, f32[32,24]{1,0:T(8,128)}) all-reduce(f32[32,24]{1,0:T(8,128)S(1)} %div.36, f32[32,24]{1,0:T(8,128)S(1)} %div.34), channel_id=1, replica_groups=mesh['expert'=32,'tensor'=16] {'tensor'}, use_global_device_ids=true, to_apply=%region_10.12 | all-reduce | flops 1536 | bytes 12288 | tf_op jit(solution)/shard_map/psum | solution.py:59
  256.1 9.3 %all-to-all-start.1 = ((f32[32,1,24]{2,1,0:T(1,128)}), f32[32,1,24]{2,1,0:T(1,128)S(1)}, u32[]{:S(2)}, u32[]{:S(2)}) async-start(f32[32,1,24]{2,1,0:T(1,128)} %bitcast.9), calls=%async_computation.1 | async-start | bytes 32768 | tf_op jit(solution)/shard_map/all_to_all | solution.py:62
  265.4 0.3 fusion.4
  265.7 8.2 %all-to-all-done.1 = f32[32,1,24]{2,1,0:T(1,128)S(1)} async-done(((f32[32,1,24]{2,1,0:T(1,128)}), f32[32,1,24]{2,1,0:T(1,128)S(1)}, u32[]{:S(2)}, u32[]{:S(2)}) %all-to-all-start.1) | async-done | bytes 3104 | tf_op jit(solution)/shard_map/all_to_all | solution.py:62
  273.8 3.9 %all-to-all-start.2 = ((f32[32,1,24]{2,1,0:T(1,128)}), f32[32,1,24]{2,1,0:T(1,128)S(1)}, u32[]{:S(2)}, u32[]{:S(2)}) async-start(f32[32,1,24]{2,1,0:T(1,128)} %bitcast.11), calls=%async_computation.2 | async-start | bytes 32768 | tf_op jit(solution)/shard_map/all_to_all | solution.py:63
  277.7 1.2 multiply_divide_fusion
  278.9 1.3 reduce_sum.99
  280.2 1.3 reduce_sum.100
  282.9 0.5 broadcast.60
  283.4 0.7 reduce.12
  284.1 0.1 reshape.113
  284.2 2.1 all-to-all-done.2
  286.3 0.7 reduce.11
  287.0 0.1 reshape.114
  287.1 2.3 gather_fusion
  289.3 2.3 gather_fusion.1
  291.7 0.1 div.38
  291.8 0.6 multiply_reduce_fusion.2
  (29 shorter events, 0.3 us)
Async XLA Ops:
  7.2 195.8 %copy-start = (bf16[1,7168,128]{2,1,0:T(8,128)(2,1)S(1)}, bf16[1,7168,128]{2,1,0:T(8,128)(2,1)}, u32[]{:S(2)}) copy-start(bf16[1,7168,128]{2,1,0:T(8,128)(2,1)} %param.14) | copy-start | bytes 5505028
  7.2 68.6 %reduce-scatter.4.cloned.1.call-start = ((), (), s32[]{:S(2)}) async-start(), calls=%async_computation.6 | async-start | bytes 1949696
  7.2 2.8 copy-start.2
  7.2 3.1 %copy-start.4 = (bf16[448]{0:T(512)(128)(2,1)S(1)}, bf16[448]{0:T(512)(128)(2,1)}, u32[]{:S(2)}) copy-start(bf16[448]{0:T(512)(128)(2,1)} %param.11) | copy-start | bytes 2692
  10.0 66.7 %copy-start.1 = (bf16[64,448]{1,0:T(8,128)(2,1)S(1)}, bf16[64,448]{1,0:T(8,128)(2,1)}, u32[]{:S(2)}) copy-start(bf16[64,448]{1,0:T(8,128)(2,1)} %param.9) | copy-start | bytes 172036
  10.0 192.9 %all-gather.2.cloned.1.call-start = ((), (), s32[]{:S(2)}) async-start(), calls=%async_computation.5 | async-start | bytes 11698176 | tf_op jit(solution)/shard_map/all_gather | solution.py:50
  104.1 37.8 %copy-start.3 = (f32[64,8]{0,1:T(8,128)S(1)}, f32[64,8]{0,1:T(8,128)}, u32[]{:S(2)}) copy-start(f32[64,8]{0,1:T(8,128)} %param.13) | copy-start | bytes 6148
  136.1 14.4 %all-to-all-start.3 = ((bf16[32,1,1]{2,1,0:T(2,128)(2,1)}), bf16[32,1,1]{2,1,0:T(2,128)(2,1)S(1)}, u32[]{:S(2)}, u32[]{:S(2)}) async-start(bf16[32,1,1]{2,1,0:T(2,128)(2,1)} %copy.50), calls=%async_computation.3 | async-start | bytes 32768 | tf_op jit(solution)/shard_map/all_to_all | solution.py:47
  202.9 7.3 %copy-start.5 = (bf16[768,7168]{0,1:T(8,128)(2,1)S(1)}, bf16[768,7168]{0,1:T(8,128)(2,1)}, u32[]{:S(2)}) copy-start(bf16[768,7168]{0,1:T(8,128)(2,1)} %all-gather.2.cloned.1.call-done) | copy-start | bytes 33030148
  202.9 7.8 %copy-start.6 = (bf16[1,7168,128]{2,1,0:T(8,128)(2,1)S(1)}, bf16[1,7168,128]{2,1,0:T(8,128)(2,1)}, u32[]{:S(2)}) copy-start(bf16[1,7168,128]{2,1,0:T(8,128)(2,1)} %param.15) | copy-start | bytes 5505028
  256.1 17.7 %all-to-all-start.1 = ((f32[32,1,24]{2,1,0:T(1,128)}), f32[32,1,24]{2,1,0:T(1,128)S(1)}, u32[]{:S(2)}, u32[]{:S(2)}) async-start(f32[32,1,24]{2,1,0:T(1,128)} %bitcast.9), calls=%async_computation.1 | async-start | bytes 32768 | tf_op jit(solution)/shard_map/all_to_all | solution.py:62
  273.8 12.4 %all-to-all-start.2 = ((f32[32,1,24]{2,1,0:T(1,128)}), f32[32,1,24]{2,1,0:T(1,128)S(1)}, u32[]{:S(2)}, u32[]{:S(2)}) async-start(f32[32,1,24]{2,1,0:T(1,128)} %bitcast.11), calls=%async_computation.2 | async-start | bytes 32768 | tf_op jit(solution)/shard_map/all_to_all | solution.py:63
Sparse Core Ops, SparseCore 0:
  10.9 64.8 reduce-scatter.3
  135.5 67.3 all-gather.1
where the time goes:
time: 305 us; the launch traced here: 300 us
  waiting for transfers between devices  134 us (44%)
  blocking collectives  100 us (33%)
  starting transfers between devices  19 us (6%)
  between operations  16.7 us (5%)
  local copies, waits for them, and re-layouts  13.9 us (5%)
  other arithmetic  8.86 us (3%)
  matrix products  8.28 us (3%)
    unnamed x3, waiting for transfers between devices  63 us
    all_gather x1, waiting for transfers between devices, per_device(): column_block = lax.all_gather(own_block, 'tensor', axis=1, tiled=True)  51.8 us
    psum x1, blocking collectives, per_device(): err_slots, pow_slots = lax.psum((err_part, pow_part), 'tensor')  43.4 us
    all_to_all x1, blocking collectives, per_device(): lax.all_to_all(outgoing, 'expert', split_axis=0, concat_axis=0, tiled=True)  30.1 us
    psum x1, blocking collectives, per_device(): squares = lax.psum(jnp.sum(hidden * hidden, axis=1), 'tensor')  26.5 us
    all_to_all x1, starting transfers between devices, per_device(): lax.all_to_all(err_slots, 'expert', split_axis=0, concat_axis=0, tiled=True)  9.27 us
    all_to_all x1, waiting for transfers between devices, per_device(): lax.all_to_all(count_send, 'expert', split_axis=0, concat_axis=0, tiled=T...  8.47 us
    all_to_all x1, waiting for transfers between devices, per_device(): lax.all_to_all(err_slots, 'expert', split_axis=0, concat_axis=0, tiled=True)  8.16 us
  transfers between devices with their start and end apart: 5, of which 5 were waited for; matrix products, arithmetic and copies ran while one was open for 3% of the time, Pallas kernels for 0%

commit v1 on v0

v1 whole, which is shorter than its diff:
```python
import jax
import jax.numpy as jnp
from jax import lax
from jax.sharding import PartitionSpec as P

D = 7168
FF = 2048
CAP = 24


epsilon = 1e-06


def per_device(residual, attn_parts, norm_gain, routes, route_weights, w_gate, w_gate_q):
    n_expert = lax.axis_size("expert")
    tok_count = residual.shape[0]
    local_cols = residual.shape[1]
    top_count = routes.shape[1]
    gain_local = norm_gain.astype(jnp.float32)[None, :]
    gain_full = lax.all_gather(norm_gain, "tensor", tiled=True).astype(jnp.float32)[None, :]
    summed = lax.psum_scatter(
        attn_parts[0].astype(jnp.float32).astype(jnp.bfloat16),
        "tensor",
        scatter_dimension=1,
        tiled=True,
    ).astype(jnp.float32)
    hidden = (residual.astype(jnp.float32) + summed).astype(jnp.bfloat16)
    expert_ids = jnp.arange(n_expert, dtype=jnp.int32)
    flat_routes = routes.reshape(-1)
    one_hot = (flat_routes[:, None] == expert_ids[None, :]).astype(jnp.int32)
    earlier = jnp.cumsum(one_hot, axis=0) - one_hot
    slot_index = jnp.sum(earlier * one_hot, axis=1)
    target = flat_routes * CAP + slot_index
    load_counts = jnp.sum(one_hot, axis=0)
    slot_ids = jnp.arange(n_expert * CAP, dtype=jnp.int32)
    placing = (slot_ids[:, None] == target[None, :]).reshape(n_expert * CAP, tok_count, top_count)
    dispatch = jnp.sum(placing.astype(jnp.int32), axis=2).astype(jnp.bfloat16)
    outgoing = jnp.dot(dispatch, hidden, preferred_element_type=jnp.float32).astype(jnp.bfloat16)
    outgoing = outgoing.reshape(n_expert, CAP, local_cols)
    count_rows = jnp.broadcast_to(load_counts.astype(jnp.bfloat16)[:, None, None], (n_expert, 1, local_cols))
    outgoing = jnp.concatenate([outgoing, count_rows], axis=1)
    arrived = lax.all_to_all(outgoing, "expert", split_axis=0, concat_axis=0, tiled=True)
    arrived_counts = arrived[:, CAP, 0].astype(jnp.float32)
    own_block = arrived[:, :CAP, :].reshape(n_expert * CAP, local_cols)
    column_block = lax.all_gather(own_block, "tensor", axis=1, tiled=True)
    wide = column_block.astype(jnp.float32)
    scaling = lax.rsqrt(jnp.sum(wide * wide, axis=1, keepdims=True) / D + epsilon)
    normed = (wide * scaling * gain_full).astype(jnp.bfloat16)
    normed_local = (own_block.astype(jnp.float32) * scaling * gain_local).astype(jnp.bfloat16)
    full_acc = jnp.dot(normed, w_gate[0], preferred_element_type=jnp.float32)
    quant_acc = jnp.dot(normed, w_gate_q[0], preferred_element_type=jnp.float32)
    block_squares = jnp.einsum("rc,rc->c", normed_local, normed_local, preferred_element_type=jnp.float32)
    total_load = jnp.sum(arrived_counts)
    hess_local = 2.0 * block_squares / total_load
    difference = full_acc - quant_acc
    err_part = (jnp.sum(difference * difference, axis=1) / FF).reshape(n_expert, 1, CAP)
    pow_part = (jnp.sum(full_acc * full_acc, axis=1) / FF).reshape(n_expert, 1, CAP)
    slots = lax.psum(jnp.concatenate([err_part, pow_part], axis=1), "tensor")
    expert_total = jnp.sum(slots[:, 0]) / (jnp.sum(slots[:, 1]) + epsilon)
    back = lax.all_to_all(slots, "expert", split_axis=0, concat_axis=0, tiled=True)
    token_err = jnp.take(back[:, 0].reshape(-1), target).reshape(tok_count, top_count)
    token_pow = jnp.take(back[:, 1].reshape(-1), target).reshape(tok_count, top_count)
    ratios = token_err / (token_pow + epsilon)
    token_error = jnp.sum(route_weights * ratios, axis=1)
    return (token_error, expert_total.reshape(1), hess_local.reshape(1, local_cols))


def solution(mesh):
    placed = (
        P("expert", "tensor"),
        P("tensor", "expert", None),
        P("tensor"),
        P("expert", None),
        P("expert", None),
        P("expert", None, "tensor"),
        P("expert", None, "tensor"),
    )
    return jax.shard_map(
        per_device,
        mesh=mesh,
        in_specs=placed,
        out_specs=(P("expert"), P("expert"), P("expert", "tensor")),
        check_vma=False,
    )
```

time: 305 us -> 280 us (0.918)
  waiting for transfers between devices: 134 us -> 86.9 us
  blocking collectives: 100 us -> 128 us
  starting transfers between devices: 19 us -> 9.27 us
  other arithmetic: 8.86 us -> 14.1 us
    unnamed x0 -> x1, blocking collectives: none -> 51.5 us
    all_gather x1, waiting for transfers between devices: 51.8 us -> 18.4 us  [per_device(): column_block = lax.all_gather(own_block, 'tensor', axis=1, tiled=True)]
    psum x2 -> x1, blocking collectives: 69.9 us -> 43.4 us  [per_device(): slots = lax.psum(jnp.concatenate([err_part, pow_part], axis=1), 'tensor')]
    all_to_all x3 -> x1, waiting for transfers between devices: 18.7 us -> 5.55 us  [per_device(): lax.all_to_all(slots, 'expert', split_axis=0, concat_axis=0, tiled=True)]
    all_to_all x3 -> x1, starting transfers between devices: 18.9 us -> 9.19 us  [per_device(): lax.all_to_all(slots, 'expert', split_axis=0, concat_axis=0, tiled=True)]
    reduce_sum x5 -> x4, other arithmetic: 3.56 us -> 8.76 us  [the longest x1 6.51 us: per_device(): jnp.sum(wide * wide, axis=1, keepdims=True) / D + epsilon]
    unnamed x18 -> x25, local copies, waits for them, and re-layouts: 5.66 us -> 6.44 us
  transfers between devices with their start and end apart: 5 -> 3, of which waited for: 5 -> 3; matrix products, arithmetic and copies ran while one was open for 3% -> 3% of each run, Pallas kernels for 0% -> 0%
where the time goes in v1:
time: 280 us; the launch traced here: 277 us
  blocking collectives  128 us (46%)
  waiting for transfers between devices  86.9 us (31%)
  between operations  17.4 us (6%)
  local copies, waits for them, and re-layouts  14.4 us (5%)
  other arithmetic  14.1 us (5%)
  starting transfers between devices  9.27 us (3%)
  matrix products  7.03 us (3%)
    unnamed x3, waiting for transfers between devices  63 us
    unnamed x1, blocking collectives  51.5 us
    psum x1, blocking collectives, per_device(): slots = lax.psum(jnp.concatenate([err_part, pow_part], axis=1), 'tensor')  43.4 us
    all_to_all x1, blocking collectives, per_device(): lax.all_to_all(outgoing, 'expert', split_axis=0, concat_axis=0, tiled=True)  32.7 us
    all_gather x1, waiting for transfers between devices, per_device(): column_block = lax.all_gather(own_block, 'tensor', axis=1, tiled=True)  18.4 us
    all_to_all x1, starting transfers between devices, per_device(): lax.all_to_all(slots, 'expert', split_axis=0, concat_axis=0, tiled=True)  9.19 us
    reduce_sum x1, other arithmetic, per_device(): jnp.sum(wide * wide, axis=1, keepdims=True) / D + epsilon  6.51 us
    unnamed x25, local copies, waits for them, and re-layouts  6.44 us
  transfers between devices with their start and end apart: 3, of which 3 were waited for; matrix products, arithmetic and copies ran while one was open for 3% of the time, Pallas kernels for 0%

profile of v1, /device:TPU:1, one launch (start us, length us, event | category | flops | bytes accessed | tf_op | source)
XLA Modules:
  0.0 276.8 jit_solution(10890716168880705273)
XLA Ops:
  7.2 0.0 reduce-scatter.4.cloned.1.call-start
  7.2 2.8 copy.51
  10.0 0.0 all-gather.2.cloned.1.call-start
  10.1 0.1 copy.36
  10.2 0.1 eq.40
  10.3 0.1 eq.44
  10.4 1.2 reduce-window.6
  11.5 0.2 slice_reduce_fusion
  11.8 0.2 fusion.28
  11.9 0.1 reduce_sum.93
  12.0 0.1 copy.39
  12.1 0.1 copy.40
  12.2 0.5 convert_reduce_fusion
  12.7 63.0 %reduce-scatter.4.cloned.1.call-done = bf16[448,64]{1,0:T(8,128)(2,1)} async-done(((bf16[7168,64]{1,0:T(8,128)(2,1)}), bf16[448,64]{1,0:T(8,128)(2,1)}) %reduce-scatter.4.cloned.1.call-update) | async-done | bytes 57360
  75.7 1.0 copy.52
  76.7 0.4 convolution_convert_fusion
  77.1 0.3 copy.41
  77.4 0.1 broadcast_in_dim.6
  77.5 0.2 pad_maximum_fusion
  77.7 32.7 %all_to_all.10 = bf16[32,25,448]{2,1,0:T(8,128)(2,1)S(1)} all-to-all(bf16[32,25,448]{2,1,0:T(8,128)(2,1)S(1)} %pad_maximum_fusion), channel_id=1, replica_groups=mesh['expert'=32,'tensor'=16] {'expert'}, dimensions={0} | all-to-all | bytes 1433600 | tf_op jit(solution)/shard_map/all_to_all | solution.py:42
  110.4 1.0 copy-done.3
  111.4 0.1 slice.37
  111.5 1.2 copy.42
  112.7 1.3 dynamic-slice
  114.7 0.3 dynamic-update-slice
  114.9 51.5 %all-reduce = bf16[7168]{0:T(1024)(128)(2,1)S(1)} all-reduce(bf16[7168]{0:T(1024)(128)(2,1)S(1)} %dynamic-update-slice), channel_id=1, replica_groups=mesh['expert'=32,'tensor'=16] {'tensor'}, use_global_device_ids=true, to_apply=%add | all-reduce | flops 7168 | bytes 28672
  166.4 0.1 copy.44
  166.5 1.5 fusion.30
  168.0 18.4 %all-gather.2.cloned.1.call-done = bf16[768,7168]{0,1:T(8,128)(2,1)} async-done(((bf16[768,448]{0,1:T(8,128)(2,1)}), bf16[768,7168]{0,1:T(8,128)(2,1)}) %all-gather.2.cloned.1.call-update) | async-done | bytes 11010064 | tf_op jit(solution)/shard_map/all_gather | solution.py:45
  186.4 6.5 %fusion = f32[768]{0:T(1024)S(1)} fusion(bf16[768,7168]{0,1:T(8,128)(2,1)} %all-gather.2.cloned.1.call-done), kind=kLoop, calls=%fused_computation.4 | loop fusion | flops 16514304 | bytes 11013120 | tf_op jit(solution)/shard_map/reduce_sum | solution.py:47
  192.9 1.5 fusion.9
  194.4 3.3 %multiply_reduce_fusion = (f32[768]{0:T(1024)S(1)}, f32[768,128]{0,1:T(8,128)S(1)}) fusion(bf16[1,7168,128]{2,1,0:T(8,128)(2,1)S(1)} %copy-done, bf16[768,7168]{0,1:T(8,128)(2,1)S(1)} %copy-done.1, f32[7168]{0:T(1024)S(1)} %convert_element_type.66, f32[768]{0:T(1024)S(1)} %add_rsqrt_fusion), kind=kOutput, calls=%fused_computation.22 | convolution fusion | flops 1431502080 | bytes 13273088 | tf_op jit(solution)/shard_map/dot_general | solution.py:50
  197.7 3.3 %fusion.20 = f32[768]{0:T(1024)S(1)} fusion(f32[768,128]{0,1:T(8,128)S(1)} %get-tuple-element.11, bf16[1,7168,128]{2,1,0:T(8,128)(2,1)S(1)} %copy-done.8, bf16[768,7168]{0,1:T(8,128)(2,1)S(1)} %copy-done.1, f32[7168]{0:T(1024)S(1)} %convert_element_type.66, f32[768]{0:T(1024)S(1)} %add_rsqrt_fusion), kind=kOutput, calls=%fused_computation.19 | convolution fusion | flops 1431600384 | bytes 13273088 | tf_op jit(solution)/shard_map/dot_general | solution.py:51
  201.1 0.1 div.34
  201.2 0.1 div.36
  201.3 43.4 %psum.7 = f32[32,2,24]{2,0,1:T(8,128)S(1)} all-reduce(f32[32,2,24]{2,0,1:T(8,128)S(1)} %pad_maximum_fusion.1), channel_id=1, replica_groups=mesh['expert'=32,'tensor'=16] {'tensor'}, use_global_device_ids=true, to_apply=%region_9.10 | all-reduce | flops 1536 | bytes 12288 | tf_op jit(solution)/shard_map/psum | solution.py:58
  244.7 0.6 copy.43
  245.3 9.2 %all-to-all-start.1 = ((f32[32,2,24]{2,1,0:T(2,128)}), f32[32,2,24]{2,1,0:T(2,128)S(1)}, u32[]{:S(2)}, u32[]{:S(2)}) async-start(f32[32,2,24]{2,1,0:T(2,128)} %copy.43), calls=%async_computation.1 | async-start | bytes 65536 | tf_op jit(solution)/shard_map/all_to_all | solution.py:60
  254.5 1.2 multiply_divide_fusion
  255.8 0.6 slice_reduce_fusion.1
  257.7 5.6 %all-to-all-done.1 = f32[32,2,24]{2,1,0:T(2,128)S(1)} async-done(((f32[32,2,24]{2,1,0:T(2,128)}), f32[32,2,24]{2,1,0:T(2,128)S(1)}, u32[]{:S(2)}, u32[]{:S(2)}) %all-to-all-start.1) | async-done | bytes 6176 | tf_op jit(solution)/shard_map/all_to_all | solution.py:60
  263.2 0.1 slice_reduce_fusion.4
  263.3 0.1 reshape_squeeze.6
  263.4 0.1 reshape_squeeze.7
  263.5 2.3 gather_fusion
  265.8 2.3 gather_fusion.1
  268.1 0.1 div.38
  268.2 0.6 multiply_reduce_fusion.1
  (34 shorter events, 0.2 us)
Async XLA Ops:
  7.2 187.2 %copy-start = (bf16[1,7168,128]{2,1,0:T(8,128)(2,1)S(1)}, bf16[1,7168,128]{2,1,0:T(8,128)(2,1)}, u32[]{:S(2)}) copy-start(bf16[1,7168,128]{2,1,0:T(8,128)(2,1)} %param.14) | copy-start | bytes 5505028
  7.2 68.6 %reduce-scatter.4.cloned.1.call-start = ((), (), s32[]{:S(2)}) async-start(), calls=%async_computation.4 | async-start | bytes 1949696
  7.2 2.8 %copy-start.5 = (s32[64,8]{0,1:T(8,128)S(1)}, s32[64,8]{0,1:T(8,128)}, u32[]{:S(2)}) copy-start(s32[64,8]{0,1:T(8,128)} %param.12) | copy-start | bytes 6148
  10.0 66.7 %copy-start.4 = (bf16[64,448]{1,0:T(8,128)(2,1)S(1)}, bf16[64,448]{1,0:T(8,128)(2,1)}, u32[]{:S(2)}) copy-start(bf16[64,448]{1,0:T(8,128)(2,1)} %param.9) | copy-start | bytes 172036
  10.0 176.4 %all-gather.2.cloned.1.call-start = ((), (), s32[]{:S(2)}) async-start(), calls=%async_computation.3 | async-start | bytes 11698176 | tf_op jit(solution)/shard_map/all_gather | solution.py:45
  110.4 1.0 copy-start.3
  111.4 1.3 copy-start.7
  111.4 55.0 %copy-start.6 = (f32[64,8]{0,1:T(8,128)S(1)}, f32[64,8]{0,1:T(8,128)}, u32[]{:S(2)}) copy-start(f32[64,8]{0,1:T(8,128)} %param.13) | copy-start | bytes 6148
  111.5 56.5 %copy-start.2 = (bf16[32,24,448]{2,1,0:T(8,128)(2,1)}, bf16[32,24,448]{2,1,0:T(8,128)(2,1)S(1)}, u32[]{:S(2)}) copy-start(bf16[32,24,448]{2,1,0:T(8,128)(2,1)S(1)} %slice.37) | copy-start | bytes 2064388
  186.4 8.0 %copy-start.1 = (bf16[768,7168]{0,1:T(8,128)(2,1)S(1)}, bf16[768,7168]{0,1:T(8,128)(2,1)}, u32[]{:S(2)}) copy-start(bf16[768,7168]{0,1:T(8,128)(2,1)} %all-gather.2.cloned.1.call-done) | copy-start | bytes 33030148
  194.4 3.3 %copy-start.8 = (bf16[1,7168,128]{2,1,0:T(8,128)(2,1)S(1)}, bf16[1,7168,128]{2,1,0:T(8,128)(2,1)}, u32[]{:S(2)}) copy-start(bf16[1,7168,128]{2,1,0:T(8,128)(2,1)} %param.15) | copy-start | bytes 5505028
  245.3 17.9 %all-to-all-start.1 = ((f32[32,2,24]{2,1,0:T(2,128)}), f32[32,2,24]{2,1,0:T(2,128)S(1)}, u32[]{:S(2)}, u32[]{:S(2)}) async-start(f32[32,2,24]{2,1,0:T(2,128)} %copy.43), calls=%async_computation.1 | async-start | bytes 65536 | tf_op jit(solution)/shard_map/all_to_all | solution.py:60
Sparse Core Ops, SparseCore 0:
  10.8 64.8 reduce-scatter.3
  112.8 73.5 all-gather.1

commit v2 on v1

--- a/solution.py
+++ b/solution.py
@@ -1,6 +1,8 @@
 import jax
 import jax.numpy as jnp
 from jax import lax
+from jax.experimental import pallas as pl
+from jax.experimental.pallas import tpu as pltpu
 from jax.sharding import PartitionSpec as P
 
 D = 7168
@@ -10,9 +12,54 @@
 
 epsilon = 1e-06
 
+MESH_ID = pl.DeviceIdType.MESH
+
+
+def exchange(x, axis, n, cid, gather):
+    block = x.shape if gather else x.shape[1:]
+
+    def kernel(x_ref, o_ref, local_sem, send_sem, recv_sem):
+        me = lax.axis_index(axis)
+        barrier = pltpu.get_barrier_semaphore()
+        for k in range(1, n):
+            pl.semaphore_signal(barrier, inc=1, device_id={axis: lax.rem(me + k, n)}, device_id_type=MESH_ID)
+        pl.semaphore_wait(barrier, n - 1)
+        local = pltpu.make_async_copy(x_ref if gather else x_ref.at[me], o_ref.at[me], local_sem)
+        local.start()
+        copies = []
+        for k in range(1, n):
+            peer = lax.rem(me + k, n)
+            copy = pltpu.make_async_remote_copy(
+                src_ref=x_ref if gather else x_ref.at[peer],
+                dst_ref=o_ref.at[me],
+                send_sem=send_sem.at[k],
+                recv_sem=recv_sem.at[k],
+                device_id={axis: peer},
+                device_id_type=MESH_ID,
+            )
+            copy.start()
+            copies.append(copy)
+        local.wait()
+        for copy in copies:
+            copy.wait()
+
+    return pl.pallas_call(
+        kernel,
+        out_shape=jax.ShapeDtypeStruct((n,) + tuple(block), x.dtype),
+        in_specs=[pl.BlockSpec(memory_space=pltpu.VMEM)],
+        out_specs=pl.BlockSpec(memory_space=pltpu.VMEM),
+        scratch_shapes=[
+            pltpu.SemaphoreType.DMA(()),
+            pltpu.SemaphoreType.DMA((n,)),
+            pltpu.SemaphoreType.DMA((n,)),
+        ],
+        compiler_params=pltpu.CompilerParams(collective_id=cid, has_side_effects=True),
+    )(x)
+
 
 def per_device(residual, attn_parts, norm_gain, routes, route_weights, w_gate, w_gate_q):
     n_expert = lax.axis_size("expert")
+    n_tensor = lax.axis_size("tensor")
     tok_count = residual.shape[0]
     local_cols = residual.shape[1]
     top_count = routes.shape[1]
@@ -55,9 +102,10 @@
     difference = full_acc - quant_acc
     err_part = (jnp.sum(difference * difference, axis=1) / FF).reshape(n_expert, 1, CAP)
     pow_part = (jnp.sum(full_acc * full_acc, axis=1) / FF).reshape(n_expert, 1, CAP)
-    slots = lax.psum(jnp.concatenate([err_part, pow_part], axis=1), "tensor")
+    partial = jnp.concatenate([err_part, pow_part], axis=1)
+    slots = jnp.sum(exchange(partial, "tensor", n_tensor, 0, True), axis=0)
     expert_total = jnp.sum(slots[:, 0]) / (jnp.sum(slots[:, 1]) + epsilon)
-    back = lax.all_to_all(slots, "expert", split_axis=0, concat_axis=0, tiled=True)
+    back = exchange(slots, "expert", n_expert, 1, False)
     token_err = jnp.take(back[:, 0].reshape(-1), target).reshape(tok_count, top_count)
     token_pow = jnp.take(back[:, 1].reshape(-1), target).reshape(tok_count, top_count)
     ratios = token_err / (token_pow + epsilon)

time: 280 us -> 254 us (0.907)
  blocking collectives: 128 us -> 84.2 us
  Pallas kernels: 0 us -> 31.4 us
  starting transfers between devices: 9.27 us -> 0.08 us
  waiting for transfers between devices: 86.9 us -> 81.4 us
    psum x1 -> x0, blocking collectives: 43.4 us -> none  [per_device(): slots = lax.psum(jnp.concatenate([err_part, pow_part], axis=1), 'tensor')]
    pallas_call x0 -> x2, Pallas kernels: none -> 31.4 us  [exchange(): pl.pallas_call(kernel, out_shape=jax.ShapeDtypeStruct((n,) + tuple(block)...]
    all_to_all x1 -> x0, starting transfers between devices: 9.19 us -> none  [per_device(): lax.all_to_all(slots, 'expert', split_axis=0, concat_axis=0, tiled=True)]
    all_to_all x1 -> x0, waiting for transfers between devices: 5.55 us -> none  [per_device(): lax.all_to_all(slots, 'expert', split_axis=0, concat_axis=0, tiled=True)]
    unnamed x25 -> x27, local copies, waits for them, and re-layouts: 6.44 us -> 7.17 us
  transfers between devices with their start and end apart: 3 -> 2, of which waited for: 3 -> 2; matrix products, arithmetic and copies ran while one was open for 3% -> 2% of each run, Pallas kernels for 0% -> 0%
where the time goes in v2:
time: 254 us; the launch traced here: 253 us
  blocking collectives  84.2 us (33%)
  waiting for transfers between devices  81.4 us (32%)
  Pallas kernels  31.4 us (12%)
  between operations  17.4 us (7%)
  other arithmetic  16 us (6%)
  local copies, waits for them, and re-layouts  15.3 us (6%)
  matrix products  7.01 us (3%)
    unnamed x3, waiting for transfers between devices  63 us
    unnamed x1, blocking collectives  51.5 us
    all_to_all x1, blocking collectives, per_device(): lax.all_to_all(outgoing, 'expert', split_axis=0, concat_axis=0, tiled=True)  32.7 us
    pallas_call x2, Pallas kernels, exchange(): pl.pallas_call(kernel, out_shape=jax.ShapeDtypeStruct((n,) + tuple(block)...  31.4 us
    all_gather x1, waiting for transfers between devices, per_device(): column_block = lax.all_gather(own_block, 'tensor', axis=1, tiled=True)  18.4 us
    unnamed x27, local copies, waits for them, and re-layouts  7.17 us
    reduce_sum x1, other arithmetic, per_device(): jnp.sum(wide * wide, axis=1, keepdims=True) / D + epsilon  6.51 us
  transfers between devices with their start and end apart: 2, of which 2 were waited for; matrix products, arithmetic and copies ran while one was open for 2% of the time, Pallas kernels for 0%

profile of v2, /device:TPU:1, one launch (start us, length us, event | category | flops | bytes accessed | tf_op | source)
XLA Modules:
  0.0 252.9 jit_solution(10433368375570952430)
XLA Ops:
  7.2 2.8 %copy.56 = bf16[64,7168]{0,1:T(8,128)(2,1)} copy(bf16[64,7168]{1,0:T(8,128)(2,1)} %bitcast.44) | data formatting | bytes 1835008
  10.0 0.0 all-gather.2.cloned.1.call-start
  10.1 0.1 copy.40
  10.2 0.1 eq.40
  10.3 0.1 eq.44
  10.4 1.2 reduce-window.6
  11.5 0.2 slice_reduce_fusion
  11.8 0.2 fusion.28
  11.9 0.1 reduce_sum.102
  12.0 0.1 copy.43
  12.1 0.1 copy.44
  12.2 0.5 convert_reduce_fusion
  12.7 63.0 %reduce-scatter.4.cloned.1.call-done = bf16[448,64]{1,0:T(8,128)(2,1)} async-done(((bf16[7168,64]{1,0:T(8,128)(2,1)}), bf16[448,64]{1,0:T(8,128)(2,1)}) %reduce-scatter.4.cloned.1.call-update) | async-done | bytes 57360
  75.7 1.0 copy.57
  76.7 0.4 convolution_convert_fusion
  77.1 0.3 copy.45
  77.4 0.1 broadcast_in_dim.6
  77.5 0.2 pad_maximum_fusion
  77.7 32.7 %all_to_all.5 = bf16[32,25,448]{2,1,0:T(8,128)(2,1)S(1)} all-to-all(bf16[32,25,448]{2,1,0:T(8,128)(2,1)S(1)} %pad_maximum_fusion), channel_id=1, replica_groups=mesh['expert'=32,'tensor'=16] {'expert'}, dimensions={0} | all-to-all | bytes 1433600 | tf_op jit(solution)/shard_map/all_to_all | solution.py:89
  110.4 1.0 copy-done.3
  111.4 0.1 slice.37
  111.5 1.2 copy.46
  112.7 1.3 dynamic-slice
  114.7 0.3 dynamic-update-slice
  114.9 51.5 %all-reduce = bf16[7168]{0:T(1024)(128)(2,1)S(1)} all-reduce(bf16[7168]{0:T(1024)(128)(2,1)S(1)} %dynamic-update-slice), channel_id=1, replica_groups=mesh['expert'=32,'tensor'=16] {'tensor'}, use_global_device_ids=true, to_apply=%add | all-reduce | flops 7168 | bytes 28672
  166.4 0.1 copy.49
  166.5 1.5 fusion.30
  168.0 18.4 %all-gather.2.cloned.1.call-done = bf16[768,7168]{0,1:T(8,128)(2,1)} async-done(((bf16[768,448]{0,1:T(8,128)(2,1)}), bf16[768,7168]{0,1:T(8,128)(2,1)}) %all-gather.2.cloned.1.call-update) | async-done | bytes 11010064 | tf_op jit(solution)/shard_map/all_gather | solution.py:92
  186.4 6.5 %fusion = f32[768]{0:T(1024)S(1)} fusion(bf16[768,7168]{0,1:T(8,128)(2,1)} %all-gather.2.cloned.1.call-done), kind=kLoop, calls=%fused_computation.4 | loop fusion | flops 16514304 | bytes 11013120 | tf_op jit(solution)/shard_map/reduce_sum | solution.py:94
  192.9 0.7 copy-done.1
  193.6 3.3 %multiply_reduce_fusion = (f32[768]{0:T(1024)S(1)}, f32[768,128]{0,1:T(8,128)S(1)}) fusion(bf16[1,7168,128]{2,1,0:T(8,128)(2,1)S(1)} %copy-done, bf16[768,7168]{0,1:T(8,128)(2,1)S(1)} %copy-done.1, f32[7168]{0:T(1024)S(1)} %convert_element_type.66, f32[768]{0:T(1024)S(1)} %add_rsqrt_fusion), kind=kOutput, calls=%fused_computation.22 | convolution fusion | flops 1431502080 | bytes 13273088 | tf_op jit(solution)/shard_map/dot_general | solution.py:97
  197.0 3.3 %fusion.20 = f32[768]{0:T(1024)S(1)} fusion(f32[768,128]{0,1:T(8,128)S(1)} %get-tuple-element.11, bf16[1,7168,128]{2,1,0:T(8,128)(2,1)S(1)} %copy-done.9, bf16[768,7168]{0,1:T(8,128)(2,1)S(1)} %copy-done.1, f32[7168]{0:T(1024)S(1)} %convert_element_type.66, f32[768]{0:T(1024)S(1)} %add_rsqrt_fusion), kind=kOutput, calls=%fused_computation.19 | convolution fusion | flops 1431600384 | bytes 13273088 | tf_op jit(solution)/shard_map/dot_general | solution.py:98
  200.3 0.1 div.34
  200.4 0.1 div.36
  200.5 0.6 pad_maximum_fusion.1.x_ref
  201.1 18.9 %shard_map.94 = f32[16,32,2,24]{3,2,1,0:T(2,128)} custom-call(f32[32,2,24]{2,1,0:T(2,128)} %pad_maximum_fusion.1.x_ref), custom_call_target="tpu_custom_call" | custom-call | tf_op jit(solution)/shard_map/pallas_call | solution.py:46
  220.0 1.3 reduce_sum.108.x_ref
  221.3 0.6 slice_reduce_fusion.1
  221.9 12.6 %shard_map.95 = f32[32,2,24]{2,1,0:T(2,128)} custom-call(f32[32,2,24]{2,1,0:T(2,128)} %copy-done.4), custom_call_target="tpu_custom_call" | custom-call | tf_op jit(solution)/shard_map/pallas_call | solution.py:46
  234.5 1.5 fusion.9
  236.0 0.9 slice_reduce_fusion.4
  236.9 0.1 reshape_squeeze.6
  237.0 0.1 reshape_squeeze.7
  237.1 2.3 gather_fusion
  239.4 2.3 gather_fusion.1
  241.7 0.1 div.38
  241.8 1.2 multiply_divide_fusion
  244.3 0.6 multiply_reduce_fusion.1
  (35 shorter events, 0.2 us)
Async XLA Ops:
  7.2 185.7 %copy-start = (bf16[1,7168,128]{2,1,0:T(8,128)(2,1)S(1)}, bf16[1,7168,128]{2,1,0:T(8,128)(2,1)}, u32[]{:S(2)}) copy-start(bf16[1,7168,128]{2,1,0:T(8,128)(2,1)} %param.14) | copy-start | bytes 5505028
  7.2 68.6 %reduce-scatter.4.cloned.1.call-start = ((), (), s32[]{:S(2)}) async-start(), calls=%async_computation.3 | async-start | bytes 1949696
  7.2 2.8 %copy-start.6 = (s32[64,8]{0,1:T(8,128)S(1)}, s32[64,8]{0,1:T(8,128)}, u32[]{:S(2)}) copy-start(s32[64,8]{0,1:T(8,128)} %param.12) | copy-start | bytes 6148
  10.0 66.7 %copy-start.5 = (bf16[64,448]{1,0:T(8,128)(2,1)S(1)}, bf16[64,448]{1,0:T(8,128)(2,1)}, u32[]{:S(2)}) copy-start(bf16[64,448]{1,0:T(8,128)(2,1)} %param.9) | copy-start | bytes 172036
  10.0 176.4 %all-gather.2.cloned.1.call-start = ((), (), s32[]{:S(2)}) async-start(), calls=%async_computation.2 | async-start | bytes 11698176 | tf_op jit(solution)/shard_map/all_gather | solution.py:92
  110.4 1.0 copy-start.3
  111.4 1.3 copy-start.8
  111.4 55.0 %copy-start.7 = (f32[64,8]{0,1:T(8,128)S(1)}, f32[64,8]{0,1:T(8,128)}, u32[]{:S(2)}) copy-start(f32[64,8]{0,1:T(8,128)} %param.13) | copy-start | bytes 6148
  111.5 56.6 %copy-start.2 = (bf16[32,24,448]{2,1,0:T(8,128)(2,1)}, bf16[32,24,448]{2,1,0:T(8,128)(2,1)S(1)}, u32[]{:S(2)}) copy-start(bf16[32,24,448]{2,1,0:T(8,128)(2,1)S(1)} %slice.37) | copy-start | bytes 2064388
  186.4 7.3 %copy-start.1 = (bf16[768,7168]{0,1:T(8,128)(2,1)S(1)}, bf16[768,7168]{0,1:T(8,128)(2,1)}, u32[]{:S(2)}) copy-start(bf16[768,7168]{0,1:T(8,128)(2,1)} %all-gather.2.cloned.1.call-done) | copy-start | bytes 33030148
  193.6 3.3 %copy-start.9 = (bf16[1,7168,128]{2,1,0:T(8,128)(2,1)S(1)}, bf16[1,7168,128]{2,1,0:T(8,128)(2,1)}, u32[]{:S(2)}) copy-start(bf16[1,7168,128]{2,1,0:T(8,128)(2,1)} %param.15) | copy-start | bytes 5505028
  221.3 0.7 copy-start.4
Sparse Core Ops, SparseCore 0:
  10.8 64.8 reduce-scatter.3
  112.8 73.5 all-gather.1

commit v3 on v1

--- a/solution.py
+++ b/solution.py
@@ -1,6 +1,8 @@
 import jax
 import jax.numpy as jnp
 from jax import lax
+from jax.experimental import pallas as pl
+from jax.experimental.pallas import tpu as pltpu
 from jax.sharding import PartitionSpec as P
 
 D = 7168
@@ -10,20 +12,74 @@
 
 epsilon = 1e-06
 
+MESH_ID = pl.DeviceIdType.MESH
+
+
+def exchange(arrays, axis, n, cid):
+    count = len(arrays)
+    modes = [gather for _, gather in arrays]
+
+    def kernel(*refs):
+        x_refs = refs[:count]
+        o_refs = refs[count:2 * count]
+        local_sem, send_sem, recv_sem = refs[2 * count:]
+        me = lax.axis_index(axis)
+        barrier = pltpu.get_barrier_semaphore()
+        for k in range(1, n):
+            pl.semaphore_signal(barrier, inc=1, device_id={axis: lax.rem(me + k, n)}, device_id_type=MESH_ID)
+        pl.semaphore_wait(barrier, n - 1)
+        copies = []
+        for a in range(count):
+            x_ref, o_ref, gather = x_refs[a], o_refs[a], modes[a]
+            local = pltpu.make_async_copy(x_ref if gather else x_ref.at[me], o_ref.at[me], local_sem.at[a])
+            local.start()
+            copies.append(local)
+        for k in range(1, n):
+            peer = lax.rem(me + k, n)
+            for a in range(count):
+                x_ref, o_ref, gather = x_refs[a], o_refs[a], modes[a]
+                copy = pltpu.make_async_remote_copy(
+                    src_ref=x_ref if gather else x_ref.at[peer],
+                    dst_ref=o_ref.at[me],
+                    send_sem=send_sem.at[a, k],
+                    recv_sem=recv_sem.at[a, k],
+                    device_id={axis: peer},
+                    device_id_type=MESH_ID,
+                )
+                copy.start()
+                copies.append(copy)
+        for copy in copies:
+            copy.wait()
+
+    out_shape = [
+        jax.ShapeDtypeStruct((n,) + tuple(x.shape if gather else x.shape[1:]), x.dtype)
+        for x, gather in arrays
+    ]
+    return pl.pallas_call(
+        kernel,
+        out_shape=out_shape,
+        in_specs=[pl.BlockSpec(memory_space=pltpu.VMEM)] * count,
+        out_specs=[pl.BlockSpec(memory_space=pltpu.VMEM)] * count,
+        scratch_shapes=[
+            pltpu.SemaphoreType.DMA((count,)),
+            pltpu.SemaphoreType.DMA((count, n)),
+            pltpu.SemaphoreType.DMA((count, n)),
+        ],
+        compiler_params=pltpu.CompilerParams(collective_id=cid, has_side_effects=True),
+    )(*[x for x, _ in arrays])
+
 
 def per_device(residual, attn_parts, norm_gain, routes, route_weights, w_gate, w_gate_q):
     n_expert = lax.axis_size("expert")
+    n_tensor = lax.axis_size("tensor")
     tok_count = residual.shape[0]
     local_cols = residual.shape[1]
     top_count = routes.shape[1]
     gain_local = norm_gain.astype(jnp.float32)[None, :]
-    gain_full = lax.all_gather(norm_gain, "tensor", tiled=True).astype(jnp.float32)[None, :]
-    summed = lax.psum_scatter(
-        attn_parts[0].astype(jnp.float32).astype(jnp.bfloat16),
-        "tensor",
-        scatter_dimension=1,
-        tiled=True,
-    ).astype(jnp.float32)
+    column_parts = attn_parts[0].reshape(tok_count, n_tensor, local_cols).transpose(1, 0, 2)
+    parts_in, gain_in = exchange([(column_parts, False), (norm_gain.reshape(1, local_cols), True)], "tensor", n_tensor, 0)
+    gain_full = gain_in.reshape(1, n_tensor * local_cols).astype(jnp.float32)
+    summed = jnp.sum(parts_in.astype(jnp.float32), axis=0)
     hidden = (residual.astype(jnp.float32) + summed).astype(jnp.bfloat16)
     expert_ids = jnp.arange(n_expert, dtype=jnp.int32)
     flat_routes = routes.reshape(-1)
@@ -39,7 +95,7 @@
     outgoing = outgoing.reshape(n_expert, CAP, local_cols)
     count_rows = jnp.broadcast_to(load_counts.astype(jnp.bfloat16)[:, None, None], (n_expert, 1, local_cols))
     outgoing = jnp.concatenate([outgoing, count_rows], axis=1)
-    arrived = lax.all_to_all(outgoing, "expert", split_axis=0, concat_axis=0, tiled=True)
+    (arrived,) = exchange([(outgoing, False)], "expert", n_expert, 1)
     arrived_counts = arrived[:, CAP, 0].astype(jnp.float32)
     own_block = arrived[:, :CAP, :].reshape(n_expert * CAP, local_cols)
     column_block = lax.all_gather(own_block, "tensor", axis=1, tiled=True)
@@ -55,9 +111,11 @@
     difference = full_acc - quant_acc
     err_part = (jnp.sum(difference * difference, axis=1) / FF).reshape(n_expert, 1, CAP)
     pow_part = (jnp.sum(full_acc * full_acc, axis=1) / FF).reshape(n_expert, 1, CAP)
-    slots = lax.psum(jnp.concatenate([err_part, pow_part], axis=1), "tensor")
+    partial = jnp.concatenate([err_part, pow_part], axis=1)
+    (gathered,) = exchange([(partial, True)], "tensor", n_tensor, 2)
+    slots = jnp.sum(gathered, axis=0)
     expert_total = jnp.sum(slots[:, 0]) / (jnp.sum(slots[:, 1]) + epsilon)
-    back = lax.all_to_all(slots, "expert", split_axis=0, concat_axis=0, tiled=True)
+    (back,) = exchange([(slots, False)], "expert", n_expert, 3)
     token_err = jnp.take(back[:, 0].reshape(-1), target).reshape(tok_count, top_count)
     token_pow = jnp.take(back[:, 1].reshape(-1), target).reshape(tok_count, top_count)
     ratios = token_err / (token_pow + epsilon)

time: 280 us -> 235 us (0.84)
  blocking collectives: 128 us -> 0 us
  Pallas kernels: 0 us -> 105 us
  waiting for transfers between devices: 86.9 us -> 69.6 us
  starting transfers between devices: 9.27 us -> 0.04 us
  other arithmetic: 14.1 us -> 19.2 us
    pallas_call x0 -> x4, Pallas kernels: none -> 105 us  [exchange(): pl.pallas_call(kernel, out_shape=out_shape, in_specs=[pl.BlockSpec(memory...]
    unnamed x3 -> x1, waiting for transfers between devices: 63 us -> 0.02 us
    unnamed x1 -> x0, blocking collectives: 51.5 us -> none
    all_gather x1, waiting for transfers between devices: 18.4 us -> 69.6 us  [per_device(): column_block = lax.all_gather(own_block, 'tensor', axis=1, tiled=True)]
    psum x1 -> x0, blocking collectives: 43.4 us -> none  [per_device(): slots = lax.psum(jnp.concatenate([err_part, pow_part], axis=1), 'tensor')]
    all_to_all x1 -> x0, blocking collectives: 32.7 us -> none  [per_device(): lax.all_to_all(outgoing, 'expert', split_axis=0, concat_axis=0, tiled=True)]
    all_to_all x1 -> x0, starting transfers between devices: 9.19 us -> none  [per_device(): lax.all_to_all(slots, 'expert', split_axis=0, concat_axis=0, tiled=True)]
    all_to_all x1 -> x0, waiting for transfers between devices: 5.55 us -> none  [per_device(): lax.all_to_all(slots, 'expert', split_axis=0, concat_axis=0, tiled=True)]
  transfers between devices with their start and end apart: 3 -> 1, of which waited for: 3 -> 1; matrix products, arithmetic and copies ran while one was open for 3% -> 1% of each run, Pallas kernels for 0% -> 0%
where the time goes in v3:
time: 235 us; the launch traced here: 234 us
  Pallas kernels  105 us (45%)
  waiting for transfers between devices  69.6 us (30%)
  other arithmetic  19.2 us (8%)
  between operations  16.8 us (7%)
  local copies, waits for them, and re-layouts  16.3 us (7%)
  matrix products  7.01 us (3%)
    pallas_call x4, Pallas kernels, exchange(): pl.pallas_call(kernel, out_shape=out_shape, in_specs=[pl.BlockSpec(memory...  105 us
    all_gather x1, waiting for transfers between devices, per_device(): column_block = lax.all_gather(own_block, 'tensor', axis=1, tiled=True)  69.6 us
    reduce_sum x1, other arithmetic, per_device(): jnp.sum(wide * wide, axis=1, keepdims=True) / D + epsilon  6.51 us
  transfers between devices with their start and end apart: 1, of which 1 were waited for; matrix products, arithmetic and copies ran while one was open for 1% of the time, Pallas kernels for 0%

profile of v3, /device:TPU:1, one launch (start us, length us, event | category | flops | bytes accessed | tf_op | source)
XLA Modules:
  0.0 234.0 jit_solution(15396661411774820187)
XLA Ops:
  7.2 0.9 copy.44
  8.1 0.1 eq.40
  8.2 0.1 eq.44
  8.3 1.3 reshape.118.refs_1_
  9.6 1.2 reduce-window.6
  10.7 0.2 slice_reduce_fusion
  11.0 0.2 fusion.28
  11.2 0.1 reduce_sum.111
  11.3 0.1 copy.47
  11.3 0.7 multiply_add_fusion
  12.0 0.1 copy.48
  12.1 0.5 convert_reduce_fusion.1
  12.6 2.4 %reshape_squeeze.9 = bf16[64,16,448]{2,1,0:T(8,128)(2,1)S(1)} reshape(bf16[1,64,7168]{2,1,0:T(8,128)(2,1)} %param.10) | data formatting | bytes 1835008 | tf_op jit(solution)/shard_map/reshape;squeeze | solution.py:79
  15.0 1.6 copy.64
  16.6 39.3 %shard_map.94 = (bf16[16,64,448]{2,1,0:T(8,128)(2,1)}, bf16[16,1,448]{2,1,0:T(2,128)(2,1)}) custom-call(bf16[16,64,448]{2,1,0:T(8,128)(2,1)} %bitcast.41, bf16[1,448]{1,0:T(2,128)(2,1)} %reshape.118.refs_1_), custom_call_target="tpu_custom_call" | custom-call | tf_op jit(solution)/shard_map/pallas_call | solution.py:58
  55.9 1.4 convert_reduce_fusion
  57.3 0.4 convolution_convert_fusion
  57.7 0.3 copy.50
  58.0 0.1 broadcast_in_dim.6
  58.1 1.2 pad_maximum_fusion.refs_0_
  59.3 34.4 %shard_map.95 = bf16[32,25,448]{2,1,0:T(8,128)(2,1)} custom-call(bf16[32,25,448]{2,1,0:T(8,128)(2,1)} %pad_maximum_fusion.refs_0_), custom_call_target="tpu_custom_call" | custom-call | tf_op jit(solution)/shard_map/pallas_call | solution.py:58
  93.7 1.2 slice.26
  95.0 1.2 copy.51
  96.2 0.1 copy.54
  96.3 0.1 convert_reduce_fusion.3
  96.4 0.1 reshape.123
  96.5 1.5 convert_reduce_fusion.4
  98.0 69.6 %all-gather.2.cloned.1.call-done = bf16[768,7168]{0,1:T(8,128)(2,1)} async-done(((bf16[768,448]{0,1:T(8,128)(2,1)}), bf16[768,7168]{0,1:T(8,128)(2,1)}) %all-gather.2.cloned.1.call-update) | async-done | bytes 11010064 | tf_op jit(solution)/shard_map/all_gather | solution.py:101
  167.5 6.5 %fusion = f32[768]{0:T(1024)S(1)} fusion(bf16[768,7168]{0,1:T(8,128)(2,1)} %all-gather.2.cloned.1.call-done), kind=kLoop, calls=%fused_computation.4 | loop fusion | flops 16514304 | bytes 11013120 | tf_op jit(solution)/shard_map/reduce_sum | solution.py:103
  174.1 0.7 copy-done.1
  174.8 3.3 %multiply_reduce_fusion = (f32[768]{0:T(1024)S(1)}, f32[768,128]{0,1:T(8,128)S(1)}) fusion(bf16[1,7168,128]{2,1,0:T(8,128)(2,1)S(1)} %copy-done, bf16[768,7168]{0,1:T(8,128)(2,1)S(1)} %copy-done.1, f32[7168]{0:T(1024)S(1)} %reshape.123, f32[768]{0:T(1024)S(1)} %add_rsqrt_fusion), kind=kOutput, calls=%fused_computation.24 | convolution fusion | flops 1431502080 | bytes 13273088 | tf_op jit(solution)/shard_map/dot_general | solution.py:106
  178.1 3.3 %fusion.20 = f32[768]{0:T(1024)S(1)} fusion(f32[768,128]{0,1:T(8,128)S(1)} %get-tuple-element.15, bf16[1,7168,128]{2,1,0:T(8,128)(2,1)S(1)} %copy-done.8, bf16[768,7168]{0,1:T(8,128)(2,1)S(1)} %copy-done.1, f32[7168]{0:T(1024)S(1)} %reshape.123, f32[768]{0:T(1024)S(1)} %add_rsqrt_fusion), kind=kOutput, calls=%fused_computation.20 | convolution fusion | flops 1431600384 | bytes 13273088 | tf_op jit(solution)/shard_map/dot_general | solution.py:107
  181.5 0.1 div.34
  181.6 0.1 div.36
  181.6 0.6 pad_maximum_fusion.1.refs_0_
  182.3 18.8 %shard_map.96 = f32[16,32,2,24]{3,2,1,0:T(2,128)} custom-call(f32[32,2,24]{2,1,0:T(2,128)} %pad_maximum_fusion.1.refs_0_), custom_call_target="tpu_custom_call" | custom-call | tf_op jit(solution)/shard_map/pallas_call | solution.py:58
  201.1 1.3 reduce_sum.118.refs_0_
  202.4 0.6 slice_reduce_fusion.1
  203.0 12.6 %shard_map.97 = f32[32,2,24]{2,1,0:T(2,128)} custom-call(f32[32,2,24]{2,1,0:T(2,128)} %copy-done.3), custom_call_target="tpu_custom_call" | custom-call | tf_op jit(solution)/shard_map/pallas_call | solution.py:58
  215.6 1.5 fusion.9
  217.1 0.9 slice_reduce_fusion.4
  218.1 0.1 reshape_squeeze.10
  218.1 0.1 reshape_squeeze.11
  218.2 2.3 gather_fusion
  220.5 2.3 gather_fusion.1
  222.8 0.1 div.38
  222.9 1.2 multiply_divide_fusion
  225.4 0.6 multiply_reduce_fusion.1
  (30 shorter events, 0.2 us)
Async XLA Ops:
  7.2 166.9 %copy-start = (bf16[1,7168,128]{2,1,0:T(8,128)(2,1)S(1)}, bf16[1,7168,128]{2,1,0:T(8,128)(2,1)}, u32[]{:S(2)}) copy-start(bf16[1,7168,128]{2,1,0:T(8,128)(2,1)} %param.14) | copy-start | bytes 5505028
  7.2 160.4 %all-gather.2.cloned.1.call-start = ((), (), s32[]{:S(2)}) async-start(), calls=%async_computation | async-start | bytes 11698176 | tf_op jit(solution)/shard_map/all_gather | solution.py:101
  16.6 40.7 %copy-start.4 = (bf16[64,448]{1,0:T(8,128)(2,1)S(1)}, bf16[64,448]{1,0:T(8,128)(2,1)}, u32[]{:S(2)}) copy-start(bf16[64,448]{1,0:T(8,128)(2,1)} %param.9) | copy-start | bytes 172036
  93.7 2.5 %copy-start.7 = (bf16[448]{0:T(512)(128)(2,1)S(1)}, bf16[448]{0:T(512)(128)(2,1)}, u32[]{:S(2)}) copy-start(bf16[448]{0:T(512)(128)(2,1)} %param.11) | copy-start | bytes 2692
  93.7 2.5 %copy-start.6 = (f32[64,8]{0,1:T(8,128)S(1)}, f32[64,8]{0,1:T(8,128)}, u32[]{:S(2)}) copy-start(f32[64,8]{0,1:T(8,128)} %param.13) | copy-start | bytes 6148
  93.7 2.6 %copy-start.5 = (bf16[16,1,448]{2,1,0:T(2,128)(2,1)S(1)}, bf16[16,1,448]{2,1,0:T(2,128)(2,1)}, u32[]{:S(2)}) copy-start(bf16[16,1,448]{2,1,0:T(2,128)(2,1)} %get-tuple-element.7) | copy-start | bytes 43012
  94.9 3.0 %copy-start.2 = (bf16[32,24,448]{2,1,0:T(8,128)(2,1)}, bf16[32,24,448]{2,1,0:T(8,128)(2,1)S(1)}, u32[]{:S(2)}) copy-start(bf16[32,24,448]{2,1,0:T(8,128)(2,1)S(1)} %slice.26) | copy-start | bytes 2064388
  167.5 7.3 %copy-start.1 = (bf16[768,7168]{0,1:T(8,128)(2,1)S(1)}, bf16[768,7168]{0,1:T(8,128)(2,1)}, u32[]{:S(2)}) copy-start(bf16[768,7168]{0,1:T(8,128)(2,1)} %all-gather.2.cloned.1.call-done) | copy-start | bytes 33030148
  174.8 3.3 %copy-start.8 = (bf16[1,7168,128]{2,1,0:T(8,128)(2,1)S(1)}, bf16[1,7168,128]{2,1,0:T(8,128)(2,1)}, u32[]{:S(2)}) copy-start(bf16[1,7168,128]{2,1,0:T(8,128)(2,1)} %param.15) | copy-start | bytes 5505028
  202.4 0.7 copy-start.3
Sparse Core Ops, SparseCore 0:
  96.3 71.2 all-gather.1

commit v4 on v3

--- a/solution.py
+++ b/solution.py
@@ -92,12 +92,13 @@
     placing = (slot_ids[:, None] == target[None, :]).reshape(n_expert * CAP, tok_count, top_count)
     dispatch = jnp.sum(placing.astype(jnp.int32), axis=2).astype(jnp.bfloat16)
     outgoing = jnp.dot(dispatch, hidden, preferred_element_type=jnp.float32).astype(jnp.bfloat16)
-    outgoing = outgoing.reshape(n_expert, CAP, local_cols)
-    count_rows = jnp.broadcast_to(load_counts.astype(jnp.bfloat16)[:, None, None], (n_expert, 1, local_cols))
+    lane_rows = CAP * local_cols // 128
+    outgoing = outgoing.reshape(n_expert, lane_rows, 128)
+    count_rows = jnp.broadcast_to(load_counts.astype(jnp.bfloat16)[:, None, None], (n_expert, 1, 128))
     outgoing = jnp.concatenate([outgoing, count_rows], axis=1)
     (arrived,) = exchange([(outgoing, False)], "expert", n_expert, 1)
-    arrived_counts = arrived[:, CAP, 0].astype(jnp.float32)
-    own_block = arrived[:, :CAP, :].reshape(n_expert * CAP, local_cols)
+    arrived_counts = arrived[:, lane_rows, 0].astype(jnp.float32)
+    own_block = arrived[:, :lane_rows, :].reshape(n_expert * CAP, local_cols)
     column_block = lax.all_gather(own_block, "tensor", axis=1, tiled=True)
     wide = column_block.astype(jnp.float32)
     scaling = lax.rsqrt(jnp.sum(wide * wide, axis=1, keepdims=True) / D + epsilon)
@@ -109,11 +110,11 @@
     total_load = jnp.sum(arrived_counts)
     hess_local = 2.0 * block_squares / total_load
     difference = full_acc - quant_acc
-    err_part = (jnp.sum(difference * difference, axis=1) / FF).reshape(n_expert, 1, CAP)
-    pow_part = (jnp.sum(full_acc * full_acc, axis=1) / FF).reshape(n_expert, 1, CAP)
-    partial = jnp.concatenate([err_part, pow_part], axis=1)
+    err_part = jnp.sum(difference * difference, axis=1) / FF
+    pow_part = jnp.sum(full_acc * full_acc, axis=1) / FF
+    partial = jnp.concatenate([err_part, pow_part]).reshape(-1, 128)
     (gathered,) = exchange([(partial, True)], "tensor", n_tensor, 2)
-    slots = jnp.sum(gathered, axis=0)
+    slots = jnp.sum(gathered, axis=0).reshape(2, n_expert, CAP).transpose(1, 0, 2)
     expert_total = jnp.sum(slots[:, 0]) / (jnp.sum(slots[:, 1]) + epsilon)
     (back,) = exchange([(slots, False)], "expert", n_expert, 3)
     token_err = jnp.take(back[:, 0].reshape(-1), target).reshape(tok_count, top_count)

time: 235 us -> 221 us (0.940)
  Pallas kernels: 105 us -> 89.6 us
    pallas_call x4, Pallas kernels: 105 us -> 89.6 us  [exchange(): pl.pallas_call(kernel, out_shape=out_shape, in_specs=[pl.BlockSpec(memory...]
    reshape x1 -> x5, local copies, waits for them, and re-layouts: 1.18 us -> 4.26 us  [the longest x2 3.11 us: per_device(): own_block = arrived[:, :lane_rows, :].reshape(n_expert * CAP, local_cols)]
where the time goes in v4:
time: 221 us; the launch traced here: 220 us
  Pallas kernels  89.6 us (41%)
  waiting for transfers between devices  69.9 us (32%)
  other arithmetic  18.6 us (8%)
  local copies, waits for them, and re-layouts  18 us (8%)
  between operations  16.8 us (8%)
  matrix products  6.96 us (3%)
    pallas_call x4, Pallas kernels, exchange(): pl.pallas_call(kernel, out_shape=out_shape, in_specs=[pl.BlockSpec(memory...  89.6 us
    all_gather x1, waiting for transfers between devices, per_device(): column_block = lax.all_gather(own_block, 'tensor', axis=1, tiled=True)  69.8 us
    reduce_sum x1, other arithmetic, per_device(): jnp.sum(wide * wide, axis=1, keepdims=True) / D + epsilon  6.51 us
  transfers between devices with their start and end apart: 1, of which 1 were waited for; matrix products, arithmetic and copies ran while one was open for 1% of the time, Pallas kernels for 0%

profile of v4, /device:TPU:1, one launch (start us, length us, event | category | flops | bytes accessed | tf_op | source)
XLA Modules:
  0.0 219.9 jit_solution(974550788428254266)
XLA Ops:
  7.2 0.9 copy.41
  8.1 0.1 eq.40
  8.2 0.1 eq.44
  8.3 1.3 reshape.104.refs_1_
  9.6 1.2 reduce-window.6
  10.7 0.2 slice_reduce_fusion
  11.0 0.2 fusion.28
  11.2 0.1 reduce_sum.111
  11.3 0.1 copy.44
  11.3 0.7 multiply_add_fusion
  12.0 0.1 copy.45
  12.1 0.5 convert_reduce_fusion.1
  12.6 2.4 %reshape_squeeze.9 = bf16[64,16,448]{2,1,0:T(8,128)(2,1)S(1)} reshape(bf16[1,64,7168]{2,1,0:T(8,128)(2,1)} %param.10) | data formatting | bytes 1835008 | tf_op jit(solution)/shard_map/reshape;squeeze | solution.py:79
  15.0 1.6 copy.61
  16.6 39.2 %shard_map.94 = (bf16[16,64,448]{2,1,0:T(8,128)(2,1)}, bf16[16,1,448]{2,1,0:T(2,128)(2,1)}) custom-call(bf16[16,64,448]{2,1,0:T(8,128)(2,1)} %bitcast.43, bf16[1,448]{1,0:T(2,128)(2,1)} %reshape.104.refs_1_), custom_call_target="tpu_custom_call" | custom-call | tf_op jit(solution)/shard_map/pallas_call | solution.py:58
  55.8 1.4 convert_reduce_fusion
  57.2 0.4 convolution_convert_fusion
  57.6 0.3 copy.47
  57.9 1.0 reshape.105
  58.9 0.1 broadcast_in_dim.6
  59.0 0.9 pad_maximum_fusion.refs_0_
  60.0 27.4 %shard_map.95 = bf16[32,85,128]{2,1,0:T(8,128)(2,1)} custom-call(bf16[32,85,128]{2,1,0:T(8,128)(2,1)} %pad_maximum_fusion.refs_0_), custom_call_target="tpu_custom_call" | custom-call | tf_op jit(solution)/shard_map/pallas_call | solution.py:58
  87.4 2.0 reshape.106
  89.4 1.1 copy.48
  90.6 0.1 copy.50
  90.7 0.1 convert_reduce_fusion.3
  90.8 0.1 reshape.110
  90.9 1.5 convert_reduce_fusion.4
  92.5 69.8 %all-gather.2.cloned.1.call-done = bf16[768,7168]{0,1:T(8,128)(2,1)} async-done(((bf16[768,448]{0,1:T(8,128)(2,1)}), bf16[768,7168]{0,1:T(8,128)(2,1)}) %all-gather.2.cloned.1.call-update) | async-done | bytes 11010064 | tf_op jit(solution)/shard_map/all_gather | solution.py:102
  162.3 6.5 %fusion = f32[768]{0:T(1024)S(1)} fusion(bf16[768,7168]{0,1:T(8,128)(2,1)} %all-gather.2.cloned.1.call-done), kind=kLoop, calls=%fused_computation.4 | loop fusion | flops 16514304 | bytes 11013120 | tf_op jit(solution)/shard_map/reduce_sum | solution.py:104
  168.8 0.7 copy-done.1
  169.6 3.3 %multiply_reduce_fusion = (f32[768]{0:T(1024)S(1)}, f32[768,128]{0,1:T(8,128)S(1)}) fusion(bf16[1,7168,128]{2,1,0:T(8,128)(2,1)S(1)} %copy-done, bf16[768,7168]{0,1:T(8,128)(2,1)S(1)} %copy-done.1, f32[7168]{0:T(1024)S(1)} %reshape.110, f32[768]{0:T(1024)S(1)} %add_rsqrt_fusion), kind=kOutput, calls=%fused_computation.24 | convolution fusion | flops 1431502080 | bytes 13273088 | tf_op jit(solution)/shard_map/dot_general | solution.py:107
  172.8 3.3 %fusion.20 = f32[768]{0:T(1024)S(1)} fusion(f32[768,128]{0,1:T(8,128)S(1)} %get-tuple-element.15, bf16[1,7168,128]{2,1,0:T(8,128)(2,1)S(1)} %copy-done.8, bf16[768,7168]{0,1:T(8,128)(2,1)S(1)} %copy-done.1, f32[7168]{0:T(1024)S(1)} %reshape.110, f32[768]{0:T(1024)S(1)} %add_rsqrt_fusion), kind=kOutput, calls=%fused_computation.20 | convolution fusion | flops 1431600384 | bytes 13273088 | tf_op jit(solution)/shard_map/dot_general | solution.py:108
  176.2 0.6 pad_maximum_fusion.1.refs_0_
  176.8 10.4 %shard_map.96 = f32[16,12,128]{2,1,0:T(8,128)} custom-call(f32[12,128]{1,0:T(8,128)} %pad_maximum_fusion.1.refs_0_), custom_call_target="tpu_custom_call" | custom-call | tf_op jit(solution)/shard_map/pallas_call | solution.py:58
  187.2 0.9 reduce_sum.118
  188.1 0.1 reshape.107
  188.3 0.6 slice_reduce_fusion.1
  188.9 12.6 %shard_map.97 = f32[32,2,24]{2,1,0:T(2,128)} custom-call(f32[32,2,24]{2,1,0:T(2,128)} %bitcast.46), custom_call_target="tpu_custom_call" | custom-call | tf_op jit(solution)/shard_map/pallas_call | solution.py:58
  201.5 1.5 fusion.9
  203.0 0.9 slice_reduce_fusion.4
  203.9 0.1 reshape_squeeze.10
  204.0 0.1 reshape_squeeze.11
  204.1 2.3 %gather_fusion = f32[512]{0:T(512)S(1)} fusion(f32[768]{0:T(1024)S(1)} %reshape_squeeze.10, s32[1024]{0:T(1024)S(1)} %pad_clamp_fusion), kind=kCustom, calls=%fused_computation.clone | custom fusion | bytes 6144 | tf_op jit(solution)/shard_map/jit(_take)/gather | solution.py:120
  206.4 2.3 %gather_fusion.1 = f32[512]{0:T(512)S(1)} fusion(f32[768]{0:T(1024)S(1)} %reshape_squeeze.11, s32[1024]{0:T(1024)S(1)} %pad_clamp_fusion), kind=kCustom, calls=%fused_computation.1.clone | custom fusion | bytes 6144 | tf_op jit(solution)/shard_map/jit(_take)/gather | solution.py:121
  208.7 0.1 div.38
  208.8 1.2 multiply_divide_fusion
  211.3 0.6 multiply_reduce_fusion.1
  (30 shorter events, 0.2 us)
Async XLA Ops:
  7.2 161.7 %copy-start = (bf16[1,7168,128]{2,1,0:T(8,128)(2,1)S(1)}, bf16[1,7168,128]{2,1,0:T(8,128)(2,1)}, u32[]{:S(2)}) copy-start(bf16[1,7168,128]{2,1,0:T(8,128)(2,1)} %param.14) | copy-start | bytes 5505028
  7.2 155.1 %all-gather.2.cloned.1.call-start = ((), (), s32[]{:S(2)}) async-start(), calls=%async_computation | async-start | bytes 11698176 | tf_op jit(solution)/shard_map/all_gather | solution.py:102
  15.0 42.2 %copy-start.4 = (bf16[64,448]{1,0:T(8,128)(2,1)S(1)}, bf16[64,448]{1,0:T(8,128)(2,1)}, u32[]{:S(2)}) copy-start(bf16[64,448]{1,0:T(8,128)(2,1)} %param.9) | copy-start | bytes 172036
  87.4 3.2 %copy-start.7 = (bf16[448]{0:T(512)(128)(2,1)S(1)}, bf16[448]{0:T(512)(128)(2,1)}, u32[]{:S(2)}) copy-start(bf16[448]{0:T(512)(128)(2,1)} %param.11) | copy-start | bytes 2692
  87.4 3.2 %copy-start.6 = (f32[64,8]{0,1:T(8,128)S(1)}, f32[64,8]{0,1:T(8,128)}, u32[]{:S(2)}) copy-start(f32[64,8]{0,1:T(8,128)} %param.13) | copy-start | bytes 6148
  87.4 3.3 %copy-start.5 = (bf16[16,1,448]{2,1,0:T(2,128)(2,1)S(1)}, bf16[16,1,448]{2,1,0:T(2,128)(2,1)}, u32[]{:S(2)}) copy-start(bf16[16,1,448]{2,1,0:T(2,128)(2,1)} %get-tuple-element.7) | copy-start | bytes 43012
  89.4 3.0 %copy-start.2 = (bf16[768,448]{1,0:T(8,128)(2,1)}, bf16[768,448]{1,0:T(8,128)(2,1)S(1)}, u32[]{:S(2)}) copy-start(bf16[768,448]{1,0:T(8,128)(2,1)S(1)} %reshape.106) | copy-start | bytes 2064388
  162.3 7.3 %copy-start.1 = (bf16[768,7168]{0,1:T(8,128)(2,1)S(1)}, bf16[768,7168]{0,1:T(8,128)(2,1)}, u32[]{:S(2)}) copy-start(bf16[768,7168]{0,1:T(8,128)(2,1)} %all-gather.2.cloned.1.call-done) | copy-start | bytes 33030148
  169.6 3.3 %copy-start.8 = (bf16[1,7168,128]{2,1,0:T(8,128)(2,1)S(1)}, bf16[1,7168,128]{2,1,0:T(8,128)(2,1)}, u32[]{:S(2)}) copy-start(bf16[1,7168,128]{2,1,0:T(8,128)(2,1)} %param.15) | copy-start | bytes 5505028
  188.2 0.7 copy-start.3
Sparse Core Ops, SparseCore 0:
  90.7 71.5 all-gather.1

commit v5 on v4

--- a/solution.py
+++ b/solution.py
@@ -99,19 +99,37 @@
     (arrived,) = exchange([(outgoing, False)], "expert", n_expert, 1)
     arrived_counts = arrived[:, lane_rows, 0].astype(jnp.float32)
     own_block = arrived[:, :lane_rows, :].reshape(n_expert * CAP, local_cols)
-    column_block = lax.all_gather(own_block, "tensor", axis=1, tiled=True)
-    wide = column_block.astype(jnp.float32)
-    scaling = lax.rsqrt(jnp.sum(wide * wide, axis=1, keepdims=True) / D + epsilon)
-    normed = (wide * scaling * gain_full).astype(jnp.bfloat16)
-    normed_local = (own_block.astype(jnp.float32) * scaling * gain_local).astype(jnp.bfloat16)
-    full_acc = jnp.dot(normed, w_gate[0], preferred_element_type=jnp.float32)
-    quant_acc = jnp.dot(normed, w_gate_q[0], preferred_element_type=jnp.float32)
-    block_squares = jnp.einsum("rc,rc->c", normed_local, normed_local, preferred_element_type=jnp.float32)
+    halves = 2
+    half_rows = n_expert * CAP // halves
+    err_parts, pow_parts, square_parts = [], [], []
+    gathered_rows = [
+        lax.all_gather(own_block[h * half_rows:(h + 1) * half_rows], "tensor", axis=1, tiled=True)
+        for h in range(halves)
+    ]
+    for h in range(halves):
+        rows = own_block[h * half_rows:(h + 1) * half_rows]
+        column_block = gathered_rows[h]
+        if h > 0:
+            column_block, err_parts[-1], pow_parts[-1], square_parts[-1] = lax.optimization_barrier(
+                (column_block, err_parts[-1], pow_parts[-1], square_parts[-1])
+            )
+        wide = column_block.astype(jnp.float32)
+        scaling = lax.rsqrt(jnp.sum(wide * wide, axis=1, keepdims=True) / D + epsilon)
+        normed = (wide * scaling * gain_full).astype(jnp.bfloat16)
+        normed_local = (rows.astype(jnp.float32) * scaling * gain_local).astype(jnp.bfloat16)
+        full_acc = jnp.dot(normed, w_gate[0], preferred_element_type=jnp.float32)
+        quant_acc = jnp.dot(normed, w_gate_q[0], preferred_element_type=jnp.float32)
+        square_parts.append(jnp.einsum("rc,rc->c", normed_local, normed_local, preferred_element_type=jnp.float32))
+        difference = full_acc - quant_acc
+        err_parts.append(jnp.sum(difference * difference, axis=1) / FF)
+        pow_parts.append(jnp.sum(full_acc * full_acc, axis=1) / FF)
+    block_squares = square_parts[0]
+    for h in range(1, halves):
+        block_squares = block_squares + square_parts[h]
     total_load = jnp.sum(arrived_counts)
     hess_local = 2.0 * block_squares / total_load
-    difference = full_acc - quant_acc
-    err_part = jnp.sum(difference * difference, axis=1) / FF
-    pow_part = jnp.sum(full_acc * full_acc, axis=1) / FF
+    err_part = jnp.concatenate(err_parts)
+    pow_part = jnp.concatenate(pow_parts)
     partial = jnp.concatenate([err_part, pow_part]).reshape(-1, 128)
     (gathered,) = exchange([(partial, True)], "tensor", n_tensor, 2)
     slots = jnp.sum(gathered, axis=0).reshape(2, n_expert, CAP).transpose(1, 0, 2)

time: 221 us -> 237 us (1.072)
  waiting for transfers between devices: 69.9 us -> 82.4 us
  matrix products: 6.96 us -> 10.6 us
    all_gather x1 -> x2, waiting for transfers between devices: 69.8 us -> 82.4 us  [per_device(): lax.all_gather(own_block[h * half_rows:(h + 1) * half_rows], 'tensor', ax...]
    slice x1 -> x6, local copies, waits for them, and re-layouts: 0.22 us -> 3.83 us  [the longest x5 3.6 us: per_device(): own_block[h * half_rows:(h + 1) * half_rows]]
    reshape x2 -> x0, local copies, waits for them, and re-layouts: 3.11 us -> none  [per_device(): own_block = arrived[:, :lane_rows, :].reshape(n_expert * CAP, local_cols)]
    dot_general x1 -> x2, matrix products: 3.32 us -> 5.2 us  [per_device(): quant_acc = jnp.dot(normed, w_gate_q[0], preferred_element_type=jnp.float32)]
    dot_general x1 -> x2, matrix products: 3.26 us -> 4.98 us  [per_device(): full_acc = jnp.dot(normed, w_gate[0], preferred_element_type=jnp.float32)]
    reduce_sum x1 -> x2, other arithmetic: 6.51 us -> 7.92 us  [per_device(): jnp.sum(wide * wide, axis=1, keepdims=True) / D + epsilon]
  transfers between devices with their start and end apart: 1 -> 2, of which waited for: 1 -> 2; matrix products, arithmetic and copies ran while one was open for 1% -> 5% of each run, Pallas kernels for 0% -> 0%
where the time goes in v5:
time: 237 us
  Pallas kernels  89.7 us (38%)
  waiting for transfers between devices  82.4 us (35%)
  other arithmetic  18.9 us (8%)
  local copies, waits for them, and re-layouts  17.8 us (8%)
  between operations  16.8 us (7%)
  matrix products  10.6 us (4%)
    pallas_call x4, Pallas kernels, exchange(): pl.pallas_call(kernel, out_shape=out_shape, in_specs=[pl.BlockSpec(memory...  89.7 us
    all_gather x2, waiting for transfers between devices, per_device(): lax.all_gather(own_block[h * half_rows:(h + 1) * half_rows], 'tensor', ax...  82.4 us
    reduce_sum x2, other arithmetic, per_device(): jnp.sum(wide * wide, axis=1, keepdims=True) / D + epsilon  7.92 us
    dot_general x2, matrix products, per_device(): quant_acc = jnp.dot(normed, w_gate_q[0], preferred_element_type=jnp.float32)  5.2 us
    dot_general x2, matrix products, per_device(): full_acc = jnp.dot(normed, w_gate[0], preferred_element_type=jnp.float32)  4.98 us
  transfers between devices with their start and end apart: 2, of which 2 were waited for; matrix products, arithmetic and copies ran while one was open for 5% of the time, Pallas kernels for 0%

profile of v5, /device:TPU:1, one launch (start us, length us, event | category | flops | bytes accessed | tf_op | source)
XLA Modules:
  0.0 236.6 jit_solution(10914471568945225313)
XLA Ops:
  7.2 0.9 copy.43
  8.1 0.1 eq.40
  8.2 0.1 eq.44
  8.3 1.3 reshape.114.refs_1_
  9.6 1.2 reduce-window.6
  10.8 0.2 slice_reduce_fusion
  11.0 0.2 fusion.54
  11.3 0.7 multiply_add_fusion
  12.0 0.1 copy.47
  12.1 0.5 convert_reduce_fusion.1
  12.7 2.4 reshape_squeeze.9
  15.0 1.6 copy.70
  16.6 39.2 %shard_map.94 = (bf16[16,64,448]{2,1,0:T(8,128)(2,1)}, bf16[16,1,448]{2,1,0:T(2,128)(2,1)}) custom-call(bf16[16,64,448]{2,1,0:T(8,128)(2,1)} %bitcast.61, bf16[1,448]{1,0:T(2,128)(2,1)} %reshape.114.refs_1_), custom_call_target="tpu_custom_call" | custom-call | tf_op jit(solution)/shard_map/pallas_call | solution.py:58
  55.8 1.4 convert_reduce_fusion
  57.2 0.4 convolution_convert_fusion
  57.6 0.3 copy.49
  57.9 1.0 reshape.115
  59.0 0.1 broadcast_in_dim.6
  59.1 0.9 pad_maximum_fusion.refs_0_
  60.0 27.4 %shard_map.95 = bf16[32,85,128]{2,1,0:T(8,128)(2,1)} custom-call(bf16[32,85,128]{2,1,0:T(8,128)(2,1)} %pad_maximum_fusion.refs_0_), custom_call_target="tpu_custom_call" | custom-call | tf_op jit(solution)/shard_map/pallas_call | solution.py:58
  87.4 1.1 fusion.57
  88.6 0.3 slice.43
  88.9 0.9 copy.51
  89.9 0.2 all-gather.3.cloned.1.call-start
  90.1 0.3 slice.41
  90.4 0.9 copy.50
  91.5 0.1 convert_reduce_fusion.3
  91.7 1.5 convert_reduce_fusion.4
  93.2 44.1 %all-gather.5.cloned.1.call-done = bf16[384,7168]{0,1:T(8,128)(2,1)} async-done(((bf16[384,448]{0,1:T(8,128)(2,1)}), bf16[384,7168]{0,1:T(8,128)(2,1)}) %all-gather.5.cloned.1.call-update) | async-done | bytes 5505040 | tf_op jit(solution)/shard_map/all_gather | solution.py:106
  137.2 4.0 %fusion = f32[384]{0:T(512)S(1)} fusion(bf16[384,7168]{0,1:T(8,128)(2,1)} %all-gather.5.cloned.1.call-done), kind=kLoop, calls=%fused_computation.6 | loop fusion | flops 8257152 | bytes 5506560 | tf_op jit(solution)/shard_map/reduce_sum | solution.py:117
  141.2 0.2 fusion.49
  141.5 2.5 %multiply_reduce_fusion.1 = (f32[384]{0:T(512)S(1)}, f32[384,128]{0,1:T(8,128)S(1)}) fusion(bf16[1,7168,128]{2,1,0:T(8,128)(2,1)S(1)} %copy-done, bf16[384,7168]{0,1:T(8,128)(2,1)S(1)} %copy-done.2, f32[7168]{0:T(1024)S(1)} %reshape.119, f32[384]{0:T(512)S(1)} %add_rsqrt_fusion.1), kind=kOutput, calls=%fused_computation.41 | convolution fusion | flops 715751040 | bytes 7568384 | tf_op jit(solution)/shard_map/dot_general | solution.py:120
  144.0 2.5 %fusion.43 = f32[384]{0:T(512)S(1)} fusion(f32[384,128]{0,1:T(8,128)S(1)} %get-tuple-element.25, bf16[1,7168,128]{2,1,0:T(8,128)(2,1)S(1)} %copy-done.8, bf16[384,7168]{0,1:T(8,128)(2,1)S(1)} %copy-done.2, f32[7168]{0:T(1024)S(1)} %reshape.119, f32[384]{0:T(512)S(1)} %add_rsqrt_fusion.1), kind=kOutput, calls=%fused_computation.29 | convolution fusion | flops 715800192 | bytes 7568384 | tf_op jit(solution)/shard_map/dot_general | solution.py:121
  146.5 38.3 %all-gather.3.cloned.1.call-done = bf16[384,7168]{0,1:T(8,128)(2,1)} async-done(((bf16[384,448]{0,1:T(8,128)(2,1)}), bf16[384,7168]{0,1:T(8,128)(2,1)}) %all-gather.3.cloned.1.call-update) | async-done | bytes 5505040 | tf_op jit(solution)/shard_map/all_gather | solution.py:106
  184.8 4.0 %fusion.3 = f32[384]{0:T(512)S(1)} fusion(bf16[384,7168]{0,1:T(8,128)(2,1)} %all-gather.3.cloned.1.call-done), kind=kLoop, calls=%fused_computation.9 | loop fusion | flops 8257152 | bytes 5506560 | tf_op jit(solution)/shard_map/reduce_sum | solution.py:117
  188.8 0.2 fusion.48
  189.0 2.5 %multiply_reduce_fusion = (f32[384]{0:T(512)S(1)}, f32[384,128]{0,1:T(8,128)S(1)}) fusion(bf16[1,7168,128]{2,1,0:T(8,128)(2,1)S(1)} %copy-done, bf16[384,7168]{0,1:T(8,128)(2,1)S(1)} %copy-done.1, f32[384]{0:T(512)S(1)} %add_rsqrt_fusion, f32[7168]{0:T(1024)S(1)} %reshape.119), kind=kOutput, calls=%fused_computation.40 | convolution fusion | flops 715751040 | bytes 7568384 | tf_op jit(solution)/shard_map/dot_general | solution.py:120
  191.5 2.7 %fusion.38 = f32[384]{0:T(512)S(1)} fusion(f32[384,128]{0,1:T(8,128)S(1)} %get-tuple-element.27, bf16[1,7168,128]{2,1,0:T(8,128)(2,1)S(1)} %copy-done.9, bf16[384,7168]{0,1:T(8,128)(2,1)S(1)} %copy-done.1, f32[384]{0:T(512)S(1)} %add_rsqrt_fusion, f32[7168]{0:T(1024)S(1)} %reshape.119), kind=kOutput, calls=%fused_computation.28 | convolution fusion | flops 715800192 | bytes 7568384 | tf_op jit(solution)/shard_map/dot_general | solution.py:121
  194.2 0.6 pad_maximum_fusion.1.refs_0_
  194.9 10.5 %shard_map.96 = f32[16,12,128]{2,1,0:T(8,128)} custom-call(f32[12,128]{1,0:T(8,128)} %pad_maximum_fusion.1.refs_0_), custom_call_target="tpu_custom_call" | custom-call | tf_op jit(solution)/shard_map/pallas_call | solution.py:58
  205.4 0.9 reduce_sum.148
  206.4 0.6 slice_reduce_fusion.1
  207.1 12.6 %shard_map.97 = f32[32,2,24]{2,1,0:T(2,128)} custom-call(f32[32,2,24]{2,1,0:T(2,128)} %bitcast.63), custom_call_target="tpu_custom_call" | custom-call | tf_op jit(solution)/shard_map/pallas_call | solution.py:58
  219.7 0.9 slice_reduce_fusion.4
  220.8 2.3 gather_fusion
  223.1 2.3 gather_fusion.1
  226.8 0.6 multiply_reduce_fusion.2
  227.4 1.2 multiply_divide_fusion
  (45 shorter events, 0.9 us)
Async XLA Ops:
  7.2 134.3 %copy-start = (bf16[1,7168,128]{2,1,0:T(8,128)(2,1)S(1)}, bf16[1,7168,128]{2,1,0:T(8,128)(2,1)}, u32[]{:S(2)}) copy-start(bf16[1,7168,128]{2,1,0:T(8,128)(2,1)} %param.14) | copy-start | bytes 5505028
  7.2 50.0 %copy-start.4 = (bf16[64,448]{1,0:T(8,128)(2,1)S(1)}, bf16[64,448]{1,0:T(8,128)(2,1)}, u32[]{:S(2)}) copy-start(bf16[64,448]{1,0:T(8,128)(2,1)} %param.9) | copy-start | bytes 172036
  7.2 130.0 %all-gather.5.cloned.1.call-start = ((), (), s32[]{:S(2)}) async-start(), calls=%async_computation.1 | async-start | bytes 5849088 | tf_op jit(solution)/shard_map/all_gather | solution.py:106
  57.6 33.7 %copy-start.7 = (bf16[448]{0:T(512)(128)(2,1)S(1)}, bf16[448]{0:T(512)(128)(2,1)}, u32[]{:S(2)}) copy-start(bf16[448]{0:T(512)(128)(2,1)} %param.11) | copy-start | bytes 2692
  57.6 33.8 %copy-start.6 = (f32[64,8]{0,1:T(8,128)S(1)}, f32[64,8]{0,1:T(8,128)}, u32[]{:S(2)}) copy-start(f32[64,8]{0,1:T(8,128)} %param.13) | copy-start | bytes 6148
  57.6 33.8 %copy-start.5 = (bf16[16,1,448]{2,1,0:T(2,128)(2,1)S(1)}, bf16[16,1,448]{2,1,0:T(2,128)(2,1)}, u32[]{:S(2)}) copy-start(bf16[16,1,448]{2,1,0:T(2,128)(2,1)} %get-tuple-element.11) | copy-start | bytes 43012
  89.9 94.9 %all-gather.3.cloned.1.call-start = ((), (), s32[]{:S(2)}) async-start(), calls=%async_computation | async-start | bytes 5849088 | tf_op jit(solution)/shard_map/all_gather | solution.py:106
  137.2 4.2 %copy-start.2 = (bf16[384,7168]{0,1:T(8,128)(2,1)S(1)}, bf16[384,7168]{0,1:T(8,128)(2,1)}, u32[]{:S(2)}) copy-start(bf16[384,7168]{0,1:T(8,128)(2,1)} %all-gather.5.cloned.1.call-done) | copy-start | bytes 16515076
  141.4 2.5 %copy-start.8 = (bf16[1,7168,128]{2,1,0:T(8,128)(2,1)S(1)}, bf16[1,7168,128]{2,1,0:T(8,128)(2,1)}, u32[]{:S(2)}) copy-start(bf16[1,7168,128]{2,1,0:T(8,128)(2,1)} %param.15) | copy-start | bytes 5505028
  184.8 4.2 %copy-start.1 = (bf16[384,7168]{0,1:T(8,128)(2,1)S(1)}, bf16[384,7168]{0,1:T(8,128)(2,1)}, u32[]{:S(2)}) copy-start(bf16[384,7168]{0,1:T(8,128)(2,1)} %all-gather.3.cloned.1.call-done) | copy-start | bytes 16515076
  189.0 2.5 %copy-start.9 = (bf16[1,7168,128]{2,1,0:T(8,128)(2,1)S(1)}, bf16[1,7168,128]{2,1,0:T(8,128)(2,1)}, u32[]{:S(2)}) copy-start(bf16[1,7168,128]{2,1,0:T(8,128)(2,1)} %param.15) | copy-start | bytes 5505028
  206.4 0.7 copy-start.3
Sparse Core Ops, SparseCore 0:
  90.0 47.2 all-gather.4
  139.4 45.4 all-gather.2

commit v6 on v4

--- a/solution.py
+++ b/solution.py
@@ -15,7 +15,7 @@
 MESH_ID = pl.DeviceIdType.MESH
 
 
-def exchange(arrays, axis, n, cid):
+def exchange(arrays, axis, cid, size, stride=1):
     count = len(arrays)
     modes = [gather for _, gather in arrays]
 
@@ -24,26 +24,32 @@
         o_refs = refs[count:2 * count]
         local_sem, send_sem, recv_sem = refs[2 * count:]
         me = lax.axis_index(axis)
+        pos = lax.rem(lax.div(me, stride), size)
+        base = me - pos * stride
+
+        def member(k):
+            return base + lax.rem(pos + k, size) * stride
+
         barrier = pltpu.get_barrier_semaphore()
-        for k in range(1, n):
-            pl.semaphore_signal(barrier, inc=1, device_id={axis: lax.rem(me + k, n)}, device_id_type=MESH_ID)
-        pl.semaphore_wait(barrier, n - 1)
+        for k in range(1, size):
+            pl.semaphore_signal(barrier, inc=1, device_id={axis: member(k)}, device_id_type=MESH_ID)
+        pl.semaphore_wait(barrier, size - 1)
         copies = []
         for a in range(count):
             x_ref, o_ref, gather = x_refs[a], o_refs[a], modes[a]
-            local = pltpu.make_async_copy(x_ref if gather else x_ref.at[me], o_ref.at[me], local_sem.at[a])
+            local = pltpu.make_async_copy(x_ref if gather else x_ref.at[pos], o_ref.at[pos], local_sem.at[a])
             local.start()
             copies.append(local)
-        for k in range(1, n):
-            peer = lax.rem(me + k, n)
+        for k in range(1, size):
+            peer_pos = lax.rem(pos + k, size)
             for a in range(count):
                 x_ref, o_ref, gather = x_refs[a], o_refs[a], modes[a]
                 copy = pltpu.make_async_remote_copy(
-                    src_ref=x_ref if gather else x_ref.at[peer],
-                    dst_ref=o_ref.at[me],
+                    src_ref=x_ref if gather else x_ref.at[peer_pos],
+                    dst_ref=o_ref.at[pos],
                     send_sem=send_sem.at[a, k],
                     recv_sem=recv_sem.at[a, k],
-                    device_id={axis: peer},
+                    device_id={axis: member(k)},
                     device_id_type=MESH_ID,
                 )
                 copy.start()
@@ -52,7 +58,7 @@
             copy.wait()
 
     out_shape = [
-        jax.ShapeDtypeStruct((n,) + tuple(x.shape if gather else x.shape[1:]), x.dtype)
+        jax.ShapeDtypeStruct((size,) + tuple(x.shape if gather else x.shape[1:]), x.dtype)
         for x, gather in arrays
     ]
     return pl.pallas_call(
@@ -62,8 +68,8 @@
         out_specs=[pl.BlockSpec(memory_space=pltpu.VMEM)] * count,
         scratch_shapes=[
             pltpu.SemaphoreType.DMA((count,)),
-            pltpu.SemaphoreType.DMA((count, n)),
-            pltpu.SemaphoreType.DMA((count, n)),
+            pltpu.SemaphoreType.DMA((count, size)),
+            pltpu.SemaphoreType.DMA((count, size)),
         ],
         compiler_params=pltpu.CompilerParams(collective_id=cid, has_side_effects=True),
     )(*[x for x, _ in arrays])
@@ -76,8 +82,11 @@
     local_cols = residual.shape[1]
     top_count = routes.shape[1]
     gain_local = norm_gain.astype(jnp.float32)[None, :]
-    column_parts = attn_parts[0].reshape(tok_count, n_tensor, local_cols).transpose(1, 0, 2)
-    parts_in, gain_in = exchange([(column_parts, False), (norm_gain.reshape(1, local_cols), True)], "tensor", n_tensor, 0)
+    n_chip = n_tensor // 2
+    column_parts = attn_parts[0].reshape(tok_count, n_chip, 2, local_cols).transpose(2, 1, 0, 3)
+    pair_in, gain_pair = exchange([(column_parts, False), (norm_gain.reshape(1, local_cols), True)], "tensor", 0, 2)
+    pair_sum = (pair_in[0].astype(jnp.float32) + pair_in[1].astype(jnp.float32)).astype(jnp.bfloat16)
+    parts_in, gain_in = exchange([(pair_sum, False), (gain_pair, True)], "tensor", 4, n_chip, 2)
     gain_full = gain_in.reshape(1, n_tensor * local_cols).astype(jnp.float32)
     summed = jnp.sum(parts_in.astype(jnp.float32), axis=0)
     hidden = (residual.astype(jnp.float32) + summed).astype(jnp.bfloat16)
@@ -96,7 +105,7 @@
     outgoing = outgoing.reshape(n_expert, lane_rows, 128)
     count_rows = jnp.broadcast_to(load_counts.astype(jnp.bfloat16)[:, None, None], (n_expert, 1, 128))
     outgoing = jnp.concatenate([outgoing, count_rows], axis=1)
-    (arrived,) = exchange([(outgoing, False)], "expert", n_expert, 1)
+    (arrived,) = exchange([(outgoing, False)], "expert", 1, n_expert)
     arrived_counts = arrived[:, lane_rows, 0].astype(jnp.float32)
     own_block = arrived[:, :lane_rows, :].reshape(n_expert * CAP, local_cols)
     column_block = lax.all_gather(own_block, "tensor", axis=1, tiled=True)
@@ -113,10 +122,10 @@
     err_part = jnp.sum(difference * difference, axis=1) / FF
     pow_part = jnp.sum(full_acc * full_acc, axis=1) / FF
     partial = jnp.concatenate([err_part, pow_part]).reshape(-1, 128)
-    (gathered,) = exchange([(partial, True)], "tensor", n_tensor, 2)
+    (gathered,) = exchange([(partial, True)], "tensor", 2, n_tensor)
     slots = jnp.sum(gathered, axis=0).reshape(2, n_expert, CAP).transpose(1, 0, 2)
     expert_total = jnp.sum(slots[:, 0]) / (jnp.sum(slots[:, 1]) + epsilon)
-    (back,) = exchange([(slots, False)], "expert", n_expert, 3)
+    (back,) = exchange([(slots, False)], "expert", 3, n_expert)
     token_err = jnp.take(back[:, 0].reshape(-1), target).reshape(tok_count, top_count)
     token_pow = jnp.take(back[:, 1].reshape(-1), target).reshape(tok_count, top_count)
     ratios = token_err / (token_pow + epsilon)

time: 221 us -> 216 us (0.977)
  Pallas kernels: 89.6 us -> 81 us
    pallas_call x4 -> x5, Pallas kernels: 89.6 us -> 81 us  [exchange(): pl.pallas_call(kernel, out_shape=out_shape, in_specs=[pl.BlockSpec(memory...]
where the time goes in v6:
time: 216 us; the launch traced here: 215 us
  Pallas kernels  81 us (38%)
  waiting for transfers between devices  69.8 us (32%)
  other arithmetic  20.5 us (9%)
  local copies, waits for them, and re-layouts  19.2 us (9%)
  between operations  16.8 us (8%)
  matrix products  7.81 us (4%)
    pallas_call x5, Pallas kernels, exchange(): pl.pallas_call(kernel, out_shape=out_shape, in_specs=[pl.BlockSpec(memory...  81 us
    all_gather x1, waiting for transfers between devices, per_device(): column_block = lax.all_gather(own_block, 'tensor', axis=1, tiled=True)  69.8 us
    reduce_sum x1, other arithmetic, per_device(): jnp.sum(wide * wide, axis=1, keepdims=True) / D + epsilon  6.51 us
    another operation x2, local copies, waits for them, and re-layouts, per_device(): attn_parts[0].reshape(tok_count, n_chip, 2, local_cols)  5.11 us
  transfers between devices with their start and end apart: 1, of which 1 were waited for; matrix products, arithmetic and copies ran while one was open for 1% of the time, Pallas kernels for 0%

profile of v6, /device:TPU:1, one launch (start us, length us, event | category | flops | bytes accessed | tf_op | source)
XLA Modules:
  0.0 215.2 jit_solution(8656783360263503792)
XLA Ops:
  7.2 0.9 copy.41
  8.1 0.1 eq.40
  8.2 0.1 eq.44
  8.3 1.3 reshape.108.refs_1_
  9.6 1.2 reduce-window.6
  10.8 0.2 slice_reduce_fusion
  11.0 0.2 fusion.29
  11.2 0.1 reduce_sum.111
  11.3 0.7 multiply_add_fusion
  12.0 0.1 copy.45
  12.1 0.5 convert_reduce_fusion
  12.7 3.5 %reshape_squeeze.9 = bf16[64,8,2,448]{3,2,1,0:T(2,128)(2,1)S(1)} reshape(bf16[1,64,7168]{2,1,0:T(8,128)(2,1)} %param.10) | data formatting | bytes 1835008 | tf_op jit(solution)/shard_map/reshape;squeeze | solution.py:86
  16.2 1.6 copy.61
  17.8 11.5 %shard_map.94 = (bf16[2,8,64,448]{3,2,1,0:T(8,128)(2,1)}, bf16[2,1,448]{2,1,0:T(2,128)(2,1)}) custom-call(bf16[2,8,64,448]{3,2,1,0:T(8,128)(2,1)} %bitcast.45, bf16[1,448]{1,0:T(2,128)(2,1)} %reshape.108.refs_1_), custom_call_target="tpu_custom_call" | custom-call | tf_op jit(solution)/shard_map/pallas_call | solution.py:64
  29.2 2.2 %fusion.26.refs_0_ = bf16[8,64,448]{2,1,0:T(8,128)(2,1)} fusion(bf16[2,8,64,448]{3,2,1,0:T(8,128)(2,1)} %get-tuple-element.8), kind=kLoop, calls=%fused_computation.25 | loop fusion | flops 917504 | bytes 1376256 | tf_op jit(solution)/shard_map/convert_element_type | solution.py:88
  31.4 19.6 %shard_map.95 = (bf16[8,64,448]{2,1,0:T(8,128)(2,1)}, bf16[8,2,1,448]{3,2,1,0:T(2,128)(2,1)}) custom-call(bf16[8,64,448]{2,1,0:T(8,128)(2,1)} %fusion.26.refs_0_, bf16[2,1,448]{2,1,0:T(2,128)(2,1)} %get-tuple-element.9.refs_1_), custom_call_target="tpu_custom_call" | custom-call | tf_op jit(solution)/shard_map/pallas_call | solution.py:64
  51.0 1.1 convert_reduce_fusion.1
  52.2 1.2 convolution_convert_fusion
  53.4 0.3 copy.47
  53.7 1.0 reshape.109
  54.7 0.1 broadcast_in_dim.6
  54.8 0.9 pad_maximum_fusion.refs_0_
  55.8 27.0 %shard_map.96 = bf16[32,85,128]{2,1,0:T(8,128)(2,1)} custom-call(bf16[32,85,128]{2,1,0:T(8,128)(2,1)} %pad_maximum_fusion.refs_0_), custom_call_target="tpu_custom_call" | custom-call | tf_op jit(solution)/shard_map/pallas_call | solution.py:64
  82.8 2.0 reshape.110
  84.7 1.1 copy.48
  85.9 0.1 copy.50
  86.0 0.1 convert_reduce_fusion.3
  86.1 0.1 reshape.114
  86.2 1.5 convert_reduce_fusion.4
  87.8 69.8 %all-gather.2.cloned.1.call-done = bf16[768,7168]{0,1:T(8,128)(2,1)} async-done(((bf16[768,448]{0,1:T(8,128)(2,1)}), bf16[768,7168]{0,1:T(8,128)(2,1)}) %all-gather.2.cloned.1.call-update) | async-done | bytes 11010064 | tf_op jit(solution)/shard_map/all_gather | solution.py:111
  157.6 6.5 %fusion = f32[768]{0:T(1024)S(1)} fusion(bf16[768,7168]{0,1:T(8,128)(2,1)} %all-gather.2.cloned.1.call-done), kind=kLoop, calls=%fused_computation.4 | loop fusion | flops 16514304 | bytes 11013120 | tf_op jit(solution)/shard_map/reduce_sum | solution.py:113
  164.1 0.7 copy-done.1
  164.8 3.3 %multiply_reduce_fusion = (f32[768]{0:T(1024)S(1)}, f32[768,128]{0,1:T(8,128)S(1)}) fusion(bf16[1,7168,128]{2,1,0:T(8,128)(2,1)S(1)} %copy-done, bf16[768,7168]{0,1:T(8,128)(2,1)S(1)} %copy-done.1, f32[7168]{0:T(1024)S(1)} %reshape.114, f32[768]{0:T(1024)S(1)} %add_rsqrt_fusion), kind=kOutput, calls=%fused_computation.26 | convolution fusion | flops 1431502080 | bytes 13273088 | tf_op jit(solution)/shard_map/dot_general | solution.py:116
  168.1 3.3 %fusion.20 = f32[768]{0:T(1024)S(1)} fusion(f32[768,128]{0,1:T(8,128)S(1)} %get-tuple-element.19, bf16[1,7168,128]{2,1,0:T(8,128)(2,1)S(1)} %copy-done.7, bf16[768,7168]{0,1:T(8,128)(2,1)S(1)} %copy-done.1, f32[7168]{0:T(1024)S(1)} %reshape.114, f32[768]{0:T(1024)S(1)} %add_rsqrt_fusion), kind=kOutput, calls=%fused_computation.19 | convolution fusion | flops 1431600384 | bytes 13273088 | tf_op jit(solution)/shard_map/dot_general | solution.py:117
  171.4 0.6 pad_maximum_fusion.1.refs_0_
  172.0 10.4 %shard_map.97 = f32[16,12,128]{2,1,0:T(8,128)} custom-call(f32[12,128]{1,0:T(8,128)} %pad_maximum_fusion.1.refs_0_), custom_call_target="tpu_custom_call" | custom-call | tf_op jit(solution)/shard_map/pallas_call | solution.py:64
  182.4 0.9 reduce_sum.118
  183.5 0.6 slice_reduce_fusion.1
  184.2 12.6 %shard_map.98 = f32[32,2,24]{2,1,0:T(2,128)} custom-call(f32[32,2,24]{2,1,0:T(2,128)} %bitcast.48), custom_call_target="tpu_custom_call" | custom-call | tf_op jit(solution)/shard_map/pallas_call | solution.py:64
  196.8 1.5 fusion.9
  198.2 0.9 slice_reduce_fusion.4
  199.2 0.1 reshape_squeeze.10
  199.3 0.1 reshape_squeeze.11
  199.4 2.3 %gather_fusion = f32[512]{0:T(512)S(1)} fusion(f32[768]{0:T(1024)S(1)} %reshape_squeeze.10, s32[1024]{0:T(1024)S(1)} %pad_clamp_fusion), kind=kCustom, calls=%fused_computation.clone | custom fusion | bytes 6144 | tf_op jit(solution)/shard_map/jit(_take)/gather | solution.py:129
  201.6 2.3 %gather_fusion.1 = f32[512]{0:T(512)S(1)} fusion(f32[768]{0:T(1024)S(1)} %reshape_squeeze.11, s32[1024]{0:T(1024)S(1)} %pad_clamp_fusion), kind=kCustom, calls=%fused_computation.1.clone | custom fusion | bytes 6144 | tf_op jit(solution)/shard_map/jit(_take)/gather | solution.py:130
  204.0 0.1 div.38
  204.1 1.2 multiply_divide_fusion
  206.6 0.6 multiply_reduce_fusion.1
  (30 shorter events, 0.3 us)
Async XLA Ops:
  7.2 156.9 %copy-start = (bf16[1,7168,128]{2,1,0:T(8,128)(2,1)S(1)}, bf16[1,7168,128]{2,1,0:T(8,128)(2,1)}, u32[]{:S(2)}) copy-start(bf16[1,7168,128]{2,1,0:T(8,128)(2,1)} %param.14) | copy-start | bytes 5505028
  7.2 78.7 %copy-start.6 = (bf16[448]{0:T(512)(128)(2,1)S(1)}, bf16[448]{0:T(512)(128)(2,1)}, u32[]{:S(2)}) copy-start(bf16[448]{0:T(512)(128)(2,1)} %param.11) | copy-start | bytes 2692
  7.2 78.7 %copy-start.5 = (f32[64,8]{0,1:T(8,128)S(1)}, f32[64,8]{0,1:T(8,128)}, u32[]{:S(2)}) copy-start(f32[64,8]{0,1:T(8,128)} %param.13) | copy-start | bytes 6148
  7.2 150.4 %all-gather.2.cloned.1.call-start = ((), (), s32[]{:S(2)}) async-start(), calls=%async_computation | async-start | bytes 11698176 | tf_op jit(solution)/shard_map/all_gather | solution.py:111
  51.0 35.0 %copy-start.4 = (bf16[8,2,1,448]{3,2,1,0:T(2,128)(2,1)S(1)}, bf16[8,2,1,448]{3,2,1,0:T(2,128)(2,1)}, u32[]{:S(2)}) copy-start(bf16[8,2,1,448]{3,2,1,0:T(2,128)(2,1)} %get-tuple-element.11) | copy-start | bytes 43012
  84.7 3.1 %copy-start.2 = (bf16[768,448]{1,0:T(8,128)(2,1)}, bf16[768,448]{1,0:T(8,128)(2,1)S(1)}, u32[]{:S(2)}) copy-start(bf16[768,448]{1,0:T(8,128)(2,1)S(1)} %reshape.110) | copy-start | bytes 2064388
  157.6 7.3 %copy-start.1 = (bf16[768,7168]{0,1:T(8,128)(2,1)S(1)}, bf16[768,7168]{0,1:T(8,128)(2,1)}, u32[]{:S(2)}) copy-start(bf16[768,7168]{0,1:T(8,128)(2,1)} %all-gather.2.cloned.1.call-done) | copy-start | bytes 33030148
  164.8 3.3 %copy-start.7 = (bf16[1,7168,128]{2,1,0:T(8,128)(2,1)S(1)}, bf16[1,7168,128]{2,1,0:T(8,128)(2,1)}, u32[]{:S(2)}) copy-start(bf16[1,7168,128]{2,1,0:T(8,128)(2,1)} %param.15) | copy-start | bytes 5505028
  183.5 0.7 copy-start.3
Sparse Core Ops, SparseCore 0:
  86.0 71.4 all-gather.1

commit v7 on v6

--- a/solution.py
+++ b/solution.py
@@ -125,10 +125,9 @@
     (gathered,) = exchange([(partial, True)], "tensor", 2, n_tensor)
     slots = jnp.sum(gathered, axis=0).reshape(2, n_expert, CAP).transpose(1, 0, 2)
     expert_total = jnp.sum(slots[:, 0]) / (jnp.sum(slots[:, 1]) + epsilon)
-    (back,) = exchange([(slots, False)], "expert", 3, n_expert)
-    token_err = jnp.take(back[:, 0].reshape(-1), target).reshape(tok_count, top_count)
-    token_pow = jnp.take(back[:, 1].reshape(-1), target).reshape(tok_count, top_count)
-    ratios = token_err / (token_pow + epsilon)
+    slot_ratios = (slots[:, 0] / (slots[:, 1] + epsilon)).reshape(n_expert, 1, CAP)
+    (back,) = exchange([(slot_ratios, False)], "expert", 3, n_expert)
+    ratios = jnp.take(back.reshape(-1), target).reshape(tok_count, top_count)
     token_error = jnp.sum(route_weights * ratios, axis=1)
     return (token_error, expert_total.reshape(1), hess_local.reshape(1, local_cols))
 

time: 216 us -> 213 us (0.986)
  local copies, waits for them, and re-layouts: 19.2 us -> 15.7 us
    gather x2, local copies, waits for them, and re-layouts: 4.58 us -> 2.37 us  [per_device(): ratios = jnp.take(back.reshape(-1), target).reshape(tok_count, top_count)]
where the time goes in v7:
time: 213 us
  Pallas kernels  80.7 us (38%)
  waiting for transfers between devices  69.7 us (33%)
  other arithmetic  21.8 us (10%)
  between operations  16.8 us (8%)
  local copies, waits for them, and re-layouts  15.7 us (7%)
  matrix products  7.86 us (4%)
    pallas_call x5, Pallas kernels, exchange(): pl.pallas_call(kernel, out_shape=out_shape, in_specs=[pl.BlockSpec(memory...  80.7 us
    all_gather x1, waiting for transfers between devices, per_device(): column_block = lax.all_gather(own_block, 'tensor', axis=1, tiled=True)  69.7 us
    reduce_sum x1, other arithmetic, per_device(): jnp.sum(wide * wide, axis=1, keepdims=True) / D + epsilon  6.51 us
    another operation x2, local copies, waits for them, and re-layouts, per_device(): attn_parts[0].reshape(tok_count, n_chip, 2, local_cols)  5.11 us
  transfers between devices with their start and end apart: 1, of which 1 were waited for; matrix products, arithmetic and copies ran while one was open for 1% of the time, Pallas kernels for 0%

profile of v7, /device:TPU:1, one launch (start us, length us, event | category | flops | bytes accessed | tf_op | source)
XLA Modules:
  0.0 212.6 jit_solution(7649448211709617194)
XLA Ops:
  7.2 0.0 all-gather.2.cloned.1.call-start
  7.2 0.9 copy.29
  8.1 0.1 eq.43
  8.2 0.1 eq.39
  8.3 1.3 reshape.140.refs_1_
  9.6 1.2 reduce-window.6
  10.8 0.2 slice_reduce_fusion
  11.0 0.2 fusion.29
  11.2 0.1 reduce_sum.113
  11.3 0.5 convert_reduce_fusion
  11.8 3.5 %reshape_squeeze.3 = bf16[64,8,2,448]{3,2,1,0:T(2,128)(2,1)S(1)} reshape(bf16[1,64,7168]{2,1,0:T(8,128)(2,1)} %param.8) | data formatting | bytes 1835008 | tf_op jit(solution)/shard_map/reshape;squeeze | solution.py:86
  15.3 1.6 copy.48
  16.9 11.5 %shard_map.94 = (bf16[2,8,64,448]{3,2,1,0:T(8,128)(2,1)}, bf16[2,1,448]{2,1,0:T(2,128)(2,1)}) custom-call(bf16[2,8,64,448]{3,2,1,0:T(8,128)(2,1)} %bitcast.47, bf16[1,448]{1,0:T(2,128)(2,1)} %reshape.140.refs_1_), custom_call_target="tpu_custom_call" | custom-call | tf_op jit(solution)/shard_map/pallas_call | solution.py:64
  28.4 2.2 %fusion.26.refs_0_ = bf16[8,64,448]{2,1,0:T(8,128)(2,1)} fusion(bf16[2,8,64,448]{3,2,1,0:T(8,128)(2,1)} %get-tuple-element.7), kind=kLoop, calls=%fused_computation.24 | loop fusion | flops 917504 | bytes 1376256 | tf_op jit(solution)/shard_map/convert_element_type | solution.py:88
  30.6 19.6 %shard_map.95 = (bf16[8,64,448]{2,1,0:T(8,128)(2,1)}, bf16[8,2,1,448]{3,2,1,0:T(2,128)(2,1)}) custom-call(bf16[8,64,448]{2,1,0:T(8,128)(2,1)} %fusion.26.refs_0_, bf16[2,1,448]{2,1,0:T(2,128)(2,1)} %get-tuple-element.8.refs_1_), custom_call_target="tpu_custom_call" | custom-call | tf_op jit(solution)/shard_map/pallas_call | solution.py:64
  50.2 1.1 convert_reduce_fusion.1
  51.3 1.2 convolution_convert_fusion
  52.6 0.3 copy.34
  52.8 1.0 reshape.141
  53.9 0.1 broadcast_in_dim.6
  54.0 0.9 pad_maximum_fusion.refs_0_
  54.9 27.0 %shard_map.96 = bf16[32,85,128]{2,1,0:T(8,128)(2,1)} custom-call(bf16[32,85,128]{2,1,0:T(8,128)(2,1)} %pad_maximum_fusion.refs_0_), custom_call_target="tpu_custom_call" | custom-call | tf_op jit(solution)/shard_map/pallas_call | solution.py:64
  81.9 2.0 reshape.142
  83.9 1.1 copy.35
  85.0 0.0 all-gather.2.cloned.1.call-update
  85.1 0.1 copy.37
  85.2 0.1 mul.86
  85.3 0.1 convert_reduce_fusion.3
  85.4 0.1 reshape.147
  85.5 1.5 convert_reduce_fusion.4
  87.1 69.7 %all-gather.2.cloned.1.call-done = bf16[768,7168]{0,1:T(8,128)(2,1)} async-done(((bf16[768,448]{0,1:T(8,128)(2,1)}), bf16[768,7168]{0,1:T(8,128)(2,1)}) %all-gather.2.cloned.1.call-update) | async-done | bytes 11010064 | tf_op jit(solution)/shard_map/all_gather | solution.py:111
  156.7 6.5 %fusion = f32[768]{0:T(1024)S(1)} fusion(bf16[768,7168]{0,1:T(8,128)(2,1)} %all-gather.2.cloned.1.call-done), kind=kLoop, calls=%fused_computation.3 | loop fusion | flops 16514304 | bytes 11013120 | tf_op jit(solution)/shard_map/reduce_sum | solution.py:113
  163.3 1.5 fusion.9
  164.8 3.3 %multiply_reduce_fusion = (f32[768]{0:T(1024)S(1)}, f32[768,128]{0,1:T(8,128)S(1)}) fusion(bf16[1,7168,128]{2,1,0:T(8,128)(2,1)S(1)} %copy-done, bf16[768,7168]{0,1:T(8,128)(2,1)S(1)} %copy-done.1, f32[7168]{0:T(1024)S(1)} %reshape.147, f32[768]{0:T(1024)S(1)} %add_rsqrt_fusion), kind=kOutput, calls=%fused_computation.25 | convolution fusion | flops 1431502080 | bytes 13273088 | tf_op jit(solution)/shard_map/dot_general | solution.py:116
  168.1 3.3 %fusion.20 = f32[768]{0:T(1024)S(1)} fusion(f32[768,128]{0,1:T(8,128)S(1)} %get-tuple-element.19, bf16[1,7168,128]{2,1,0:T(8,128)(2,1)S(1)} %copy-done.6, bf16[768,7168]{0,1:T(8,128)(2,1)S(1)} %copy-done.1, f32[7168]{0:T(1024)S(1)} %reshape.147, f32[768]{0:T(1024)S(1)} %add_rsqrt_fusion), kind=kOutput, calls=%fused_computation.18 | convolution fusion | flops 1431600384 | bytes 13273088 | tf_op jit(solution)/shard_map/dot_general | solution.py:117
  171.4 0.6 pad_maximum_fusion.1.refs_0_
  172.0 10.4 %shard_map.97 = f32[16,12,128]{2,1,0:T(8,128)} custom-call(f32[12,128]{1,0:T(8,128)} %pad_maximum_fusion.1.refs_0_), custom_call_target="tpu_custom_call" | custom-call | tf_op jit(solution)/shard_map/pallas_call | solution.py:64
  182.4 0.9 reduce_sum.120
  183.4 0.1 reshape.143
  183.5 1.3 slice_reduce_fusion.1
  184.8 12.3 %shard_map.98 = f32[32,1,24]{2,1,0:T(1,128)} custom-call(f32[32,1,24]{2,1,0:T(1,128)} %get-tuple-element.15.refs_0_), custom_call_target="tpu_custom_call" | custom-call | tf_op jit(solution)/shard_map/pallas_call | solution.py:64
  197.0 0.5 broadcast.105
  197.6 1.4 reduce.12
  199.0 0.1 reshape.144
  199.0 2.3 %gather_fusion = f32[512]{0:T(512)S(1)} fusion(f32[768]{0:T(1024)S(1)} %reshape.144, s32[1024]{0:T(1024)S(1)} %pad_clamp_fusion), kind=kCustom, calls=%fused_computation | custom fusion | bytes 6144 | tf_op jit(solution)/shard_map/jit(_take)/gather | solution.py:130
  201.3 0.1 gather.7
  201.4 1.2 multiply_divide_fusion
  203.9 0.6 multiply_reduce_fusion.1
  (25 shorter events, 0.2 us)
Async XLA Ops:
  7.2 157.6 %copy-start = (bf16[1,7168,128]{2,1,0:T(8,128)(2,1)S(1)}, bf16[1,7168,128]{2,1,0:T(8,128)(2,1)}, u32[]{:S(2)}) copy-start(bf16[1,7168,128]{2,1,0:T(8,128)(2,1)} %param.12) | copy-start | bytes 5505028
  7.2 77.9 %copy-start.5 = (bf16[448]{0:T(512)(128)(2,1)S(1)}, bf16[448]{0:T(512)(128)(2,1)}, u32[]{:S(2)}) copy-start(bf16[448]{0:T(512)(128)(2,1)} %param.9) | copy-start | bytes 2692
  7.2 77.9 %copy-start.4 = (f32[64,8]{0,1:T(8,128)S(1)}, f32[64,8]{0,1:T(8,128)}, u32[]{:S(2)}) copy-start(f32[64,8]{0,1:T(8,128)} %param.11) | copy-start | bytes 6148
  7.2 149.5 %all-gather.2.cloned.1.call-start = ((), (), s32[]{:S(2)}) async-start(), calls=%async_computation | async-start | bytes 11698176 | tf_op jit(solution)/shard_map/all_gather | solution.py:111
  50.2 35.1 %copy-start.3 = (bf16[8,2,1,448]{3,2,1,0:T(2,128)(2,1)S(1)}, bf16[8,2,1,448]{3,2,1,0:T(2,128)(2,1)}, u32[]{:S(2)}) copy-start(bf16[8,2,1,448]{3,2,1,0:T(2,128)(2,1)} %get-tuple-element.10) | copy-start | bytes 43012
  83.9 3.2 %copy-start.2 = (bf16[768,448]{1,0:T(8,128)(2,1)}, bf16[768,448]{1,0:T(8,128)(2,1)S(1)}, u32[]{:S(2)}) copy-start(bf16[768,448]{1,0:T(8,128)(2,1)S(1)} %reshape.142) | copy-start | bytes 2064388
  156.7 8.0 %copy-start.1 = (bf16[768,7168]{0,1:T(8,128)(2,1)S(1)}, bf16[768,7168]{0,1:T(8,128)(2,1)}, u32[]{:S(2)}) copy-start(bf16[768,7168]{0,1:T(8,128)(2,1)} %all-gather.2.cloned.1.call-done) | copy-start | bytes 33030148
  164.8 3.3 %copy-start.6 = (bf16[1,7168,128]{2,1,0:T(8,128)(2,1)S(1)}, bf16[1,7168,128]{2,1,0:T(8,128)(2,1)}, u32[]{:S(2)}) copy-start(bf16[1,7168,128]{2,1,0:T(8,128)(2,1)} %param.13) | copy-start | bytes 5505028
Sparse Core Ops, SparseCore 0:
  85.2 71.4 all-gather.1

commit v8 on v7

--- a/solution.py
+++ b/solution.py
@@ -108,10 +108,22 @@
     (arrived,) = exchange([(outgoing, False)], "expert", 1, n_expert)
     arrived_counts = arrived[:, lane_rows, 0].astype(jnp.float32)
     own_block = arrived[:, :lane_rows, :].reshape(n_expert * CAP, local_cols)
-    column_block = lax.all_gather(own_block, "tensor", axis=1, tiled=True)
-    wide = column_block.astype(jnp.float32)
-    scaling = lax.rsqrt(jnp.sum(wide * wide, axis=1, keepdims=True) / D + epsilon)
-    normed = (wide * scaling * gain_full).astype(jnp.bfloat16)
+    slot_count = n_expert * CAP
+    own_wide = own_block.astype(jnp.float32)
+    own_squares = jnp.sum(own_wide * own_wide, axis=1)
+    squares_hi = own_squares.astype(jnp.bfloat16)
+    squares_lo = (own_squares - squares_hi.astype(jnp.float32)).astype(jnp.bfloat16)
+    extra_rows = 16
+    packed = jnp.concatenate([squares_hi, squares_lo])
+    packed = jnp.pad(packed, (0, extra_rows * local_cols - 2 * slot_count)).reshape(extra_rows, local_cols)
+    payload = jnp.concatenate([own_block, packed], axis=0)
+    gathered_block = lax.all_gather(payload, "tensor", axis=1, tiled=True)
+    column_block = gathered_block[:slot_count]
+    packed_all = gathered_block[slot_count:].reshape(extra_rows, n_tensor, local_cols).transpose(1, 0, 2)
+    packed_all = packed_all.reshape(n_tensor, extra_rows * local_cols)[:, :2 * slot_count].astype(jnp.float32)
+    row_squares = jnp.sum(packed_all[:, :slot_count] + packed_all[:, slot_count:], axis=0)
+    scaling = lax.rsqrt(row_squares[:, None] / D + epsilon)
+    normed = (column_block.astype(jnp.float32) * scaling * gain_full).astype(jnp.bfloat16)
     normed_local = (own_block.astype(jnp.float32) * scaling * gain_local).astype(jnp.bfloat16)
     full_acc = jnp.dot(normed, w_gate[0], preferred_element_type=jnp.float32)
     quant_acc = jnp.dot(normed, w_gate_q[0], preferred_element_type=jnp.float32)

time: 213 us -> 224 us (1.052)
  waiting for transfers between devices: 69.7 us -> 78.3 us
  other arithmetic: 21.8 us -> 14.6 us
  local copies, waits for them, and re-layouts: 15.7 us -> 20.6 us
  matrix products: 7.86 us -> 12.1 us
    all_gather x1, waiting for transfers between devices: 69.7 us -> 78.3 us  [per_device(): gathered_block = lax.all_gather(payload, 'tensor', axis=1, tiled=True)]
    reduce_sum x1 -> x2, other arithmetic: 6.51 us -> 0.25 us  [the longest x1 0.23 us: per_device(): own_squares = jnp.sum(own_wide * own_wide, axis=1)]
    dot_general x1, matrix products: 3.29 us -> 8.19 us  [per_device(): full_acc = jnp.dot(normed, w_gate[0], preferred_element_type=jnp.float32)]
    slice x1 -> x2, local copies, waits for them, and re-layouts: 0.22 us -> 3.1 us  [the longest x1 2.88 us: per_device(): gathered_block[slot_count:].reshape(extra_rows, n_tensor, local_cols)]
where the time goes in v8:
time: 224 us; the launch traced here: 223 us
  Pallas kernels  80.8 us (36%)
  waiting for transfers between devices  78.3 us (35%)
  local copies, waits for them, and re-layouts  20.6 us (9%)
  between operations  16.9 us (8%)
  other arithmetic  14.6 us (7%)
  matrix products  12.1 us (5%)
    pallas_call x5, Pallas kernels, exchange(): pl.pallas_call(kernel, out_shape=out_shape, in_specs=[pl.BlockSpec(memory...  80.8 us
    all_gather x1, waiting for transfers between devices, per_device(): gathered_block = lax.all_gather(payload, 'tensor', axis=1, tiled=True)  78.3 us
    dot_general x1, matrix products, per_device(): full_acc = jnp.dot(normed, w_gate[0], preferred_element_type=jnp.float32)  8.19 us
    another operation x2, local copies, waits for them, and re-layouts, per_device(): attn_parts[0].reshape(tok_count, n_chip, 2, local_cols)  5.11 us
  transfers between devices with their start and end apart: 1, of which 1 were waited for; matrix products, arithmetic and copies ran while one was open for 1% of the time, Pallas kernels for 0%

profile of v8, /device:TPU:1, one launch (start us, length us, event | category | flops | bytes accessed | tf_op | source)
XLA Modules:
  0.0 223.4 jit_solution(952545433349703377)
XLA Ops:
  7.2 0.9 copy.31
  8.1 0.1 eq.43
  8.2 0.1 eq.39
  8.3 1.3 reshape.149.refs_1_
  9.6 1.2 reduce-window.6
  10.7 0.2 slice_reduce_fusion
  11.0 0.2 fusion.21
  11.2 0.1 reduce_sum.122
  11.3 0.5 convert_reduce_fusion
  11.8 3.5 %reshape_squeeze.3 = bf16[64,8,2,448]{3,2,1,0:T(2,128)(2,1)S(1)} reshape(bf16[1,64,7168]{2,1,0:T(8,128)(2,1)} %param.8) | data formatting | bytes 1835008 | tf_op jit(solution)/shard_map/reshape;squeeze | solution.py:86
  15.3 1.6 copy.51
  16.9 11.6 %shard_map.94 = (bf16[2,8,64,448]{3,2,1,0:T(8,128)(2,1)}, bf16[2,1,448]{2,1,0:T(2,128)(2,1)}) custom-call(bf16[2,8,64,448]{3,2,1,0:T(8,128)(2,1)} %bitcast.50, bf16[1,448]{1,0:T(2,128)(2,1)} %reshape.149.refs_1_), custom_call_target="tpu_custom_call" | custom-call | tf_op jit(solution)/shard_map/pallas_call | solution.py:64
  28.5 2.2 fusion.18.refs_0_
  30.7 19.6 %shard_map.95 = (bf16[8,64,448]{2,1,0:T(8,128)(2,1)}, bf16[8,2,1,448]{3,2,1,0:T(2,128)(2,1)}) custom-call(bf16[8,64,448]{2,1,0:T(8,128)(2,1)} %fusion.18.refs_0_, bf16[2,1,448]{2,1,0:T(2,128)(2,1)} %get-tuple-element.8.refs_1_), custom_call_target="tpu_custom_call" | custom-call | tf_op jit(solution)/shard_map/pallas_call | solution.py:64
  50.3 1.1 convert_reduce_fusion.1
  51.4 0.4 convolution_convert_fusion
  51.8 0.3 copy.36
  52.1 1.0 reshape.150
  53.2 0.1 broadcast_in_dim.6
  53.3 0.9 pad_maximum_fusion.1.refs_0_
  54.2 27.0 %shard_map.96 = bf16[32,85,128]{2,1,0:T(8,128)(2,1)} custom-call(bf16[32,85,128]{2,1,0:T(8,128)(2,1)} %pad_maximum_fusion.1.refs_0_), custom_call_target="tpu_custom_call" | custom-call | tf_op jit(solution)/shard_map/pallas_call | solution.py:64
  81.2 1.8 reshape.151
  83.0 0.2 fusion.4
  83.2 0.1 reshape.152
  83.3 0.1 pad_maximum_fusion
  83.5 1.2 copy.37
  84.8 0.1 copy.40
  84.8 0.1 mul.86
  84.9 0.1 convert_reduce_fusion.3
  85.0 0.1 reshape.159
  85.2 1.5 convert_reduce_fusion.4
  86.7 78.3 %all-gather.2.cloned.1.call-done = bf16[784,7168]{0,1:T(8,128)(2,1)} async-done(((bf16[784,448]{0,1:T(8,128)(2,1)}), bf16[784,7168]{0,1:T(8,128)(2,1)}) %all-gather.2.cloned.1.call-update) | async-done | bytes 11239440 | tf_op jit(solution)/shard_map/all_gather | solution.py:120
  165.0 2.9 %slice.58 = bf16[16,7168]{0,1:T(8,128)(2,1)} slice(bf16[784,7168]{0,1:T(8,128)(2,1)} %all-gather.2.cloned.1.call-done), slice={[768:784], [0:7168]} | slice | bytes 458752 | tf_op jit(solution)/shard_map/slice | solution.py:122
  167.9 1.8 copy.38
  169.7 0.3 reshape.154
  170.1 0.3 fusion.7
  170.5 8.2 %multiply_reduce_fusion = (f32[768]{0:T(1024)S(1)}, f32[768,128]{0,1:T(8,128)S(1)}) fusion(bf16[1,7168,128]{2,1,0:T(8,128)(2,1)S(1)} %copy-done, bf16[784,7168]{0,1:T(8,128)(2,1)} %all-gather.2.cloned.1.call-done, f32[7168]{0:T(1024)S(1)} %reshape.159, f32[768]{0:T(1024)S(1)} %add_rsqrt_fusion), kind=kOutput, calls=%fused_computation.26 | convolution fusion | flops 1431502080 | bytes 13273088 | tf_op jit(solution)/shard_map/dot_general | solution.py:128
  178.7 3.6 %fusion.14 = f32[768]{0:T(1024)S(1)} fusion(f32[768,128]{0,1:T(8,128)S(1)} %get-tuple-element.21, bf16[1,7168,128]{2,1,0:T(8,128)(2,1)S(1)} %copy-done.5, bf16[784,7168]{0,1:T(8,128)(2,1)S(1)} %bitcast.54, f32[7168]{0:T(1024)S(1)} %reshape.159, f32[768]{0:T(1024)S(1)} %add_rsqrt_fusion), kind=kOutput, calls=%fused_computation.18 | convolution fusion | flops 1431600384 | bytes 13274112 | tf_op jit(solution)/shard_map/dot_general | solution.py:129
  182.3 0.6 pad_maximum_fusion.2.refs_0_
  182.9 10.4 %shard_map.97 = f32[16,12,128]{2,1,0:T(8,128)} custom-call(f32[12,128]{1,0:T(8,128)} %pad_maximum_fusion.2.refs_0_), custom_call_target="tpu_custom_call" | custom-call | tf_op jit(solution)/shard_map/pallas_call | solution.py:64
  193.3 0.9 reduce_sum.130
  194.4 1.3 slice_reduce_fusion.1
  195.6 12.3 %shard_map.98 = f32[32,1,24]{2,1,0:T(1,128)} custom-call(f32[32,1,24]{2,1,0:T(1,128)} %get-tuple-element.17.refs_0_), custom_call_target="tpu_custom_call" | custom-call | tf_op jit(solution)/shard_map/pallas_call | solution.py:64
  207.9 0.5 broadcast.113
  208.4 1.4 reduce.12
  209.9 2.3 %gather_fusion = f32[512]{0:T(512)S(1)} fusion(f32[768]{0:T(1024)S(1)} %reshape.156, s32[1024]{0:T(1024)S(1)} %pad_clamp_fusion), kind=kCustom, calls=%fused_computation | custom fusion | bytes 6144 | tf_op jit(solution)/shard_map/jit(_take)/gather | solution.py:142
  212.3 1.2 multiply_divide_fusion
  214.8 0.6 multiply_reduce_fusion.1
  (41 shorter events, 0.5 us)
Async XLA Ops:
  7.2 163.2 %copy-start = (bf16[1,7168,128]{2,1,0:T(8,128)(2,1)S(1)}, bf16[1,7168,128]{2,1,0:T(8,128)(2,1)}, u32[]{:S(2)}) copy-start(bf16[1,7168,128]{2,1,0:T(8,128)(2,1)} %param.12) | copy-start | bytes 5505028
  7.2 157.9 %all-gather.2.cloned.1.call-start = ((), (), s32[]{:S(2)}) async-start(), calls=%async_computation | async-start | bytes 13647872 | tf_op jit(solution)/shard_map/all_gather | solution.py:120
  16.9 34.5 %copy-start.1 = (bf16[64,448]{1,0:T(8,128)(2,1)S(1)}, bf16[64,448]{1,0:T(8,128)(2,1)}, u32[]{:S(2)}) copy-start(bf16[64,448]{1,0:T(8,128)(2,1)} %param.7) | copy-start | bytes 172036
  83.3 1.4 copy-start.4
  83.3 1.4 copy-start.3
  83.3 1.6 copy-start.2
  170.1 8.6 %slice-start = ((s8[12845056]{0:T(1024)(128)(4,1)}), s8[4194304]{0:T(1024)(128)(4,1)S(1)}, s32[]{:S(2)}) async-start(s8[12845056]{0:T(1024)(128)(4,1)} %bitcast.53), calls=%async_computation.1 | async-start | bytes 8388608
  170.4 8.3 %slice-start.1 = ((s8[12845056]{0:T(1024)(128)(4,1)}), s8[4194304]{0:T(1024)(128)(4,1)S(1)}, s32[]{:S(2)}) async-start(s8[12845056]{0:T(1024)(128)(4,1)} %bitcast.53), calls=%async_computation.2 | async-start | bytes 8388608
  170.4 8.2 %slice-start.2 = ((s8[12845056]{0:T(1024)(128)(4,1)}), s8[4194304]{0:T(1024)(128)(4,1)S(1)}, s32[]{:S(2)}) async-start(s8[12845056]{0:T(1024)(128)(4,1)} %bitcast.53), calls=%async_computation.3 | async-start | bytes 8388608
  170.4 8.2 %slice-start.3 = ((s8[12845056]{0:T(1024)(128)(4,1)}), s8[262144]{0:T(1024)(128)(4,1)S(1)}, s32[]{:S(2)}) async-start(s8[12845056]{0:T(1024)(128)(4,1)} %bitcast.53), calls=%async_computation.4 | async-start | bytes 524288
  170.5 8.2 %copy-start.5 = (bf16[1,7168,128]{2,1,0:T(8,128)(2,1)S(1)}, bf16[1,7168,128]{2,1,0:T(8,128)(2,1)}, u32[]{:S(2)}) copy-start(bf16[1,7168,128]{2,1,0:T(8,128)(2,1)} %param.13) | copy-start | bytes 5505028
Sparse Core Ops, SparseCore 0:
  84.8 80.1 all-gather.1

commit v9 on v7

--- a/solution.py
+++ b/solution.py
@@ -113,8 +113,11 @@
     scaling = lax.rsqrt(jnp.sum(wide * wide, axis=1, keepdims=True) / D + epsilon)
     normed = (wide * scaling * gain_full).astype(jnp.bfloat16)
     normed_local = (own_block.astype(jnp.float32) * scaling * gain_local).astype(jnp.bfloat16)
-    full_acc = jnp.dot(normed, w_gate[0], preferred_element_type=jnp.float32)
-    quant_acc = jnp.dot(normed, w_gate_q[0], preferred_element_type=jnp.float32)
+    weight_cols = w_gate.shape[2]
+    both_weights = jnp.concatenate([w_gate[0], w_gate_q[0]], axis=1)
+    both_acc = jnp.dot(normed, both_weights, preferred_element_type=jnp.float32)
+    full_acc = both_acc[:, :weight_cols]
+    quant_acc = both_acc[:, weight_cols:]
     block_squares = jnp.einsum("rc,rc->c", normed_local, normed_local, preferred_element_type=jnp.float32)
     total_load = jnp.sum(arrived_counts)
     hess_local = 2.0 * block_squares / total_load

time: 213 us -> 211 us (level)
    dot_general x2 -> x1, matrix products: 6.63 us -> 5.82 us  [per_device(): both_acc = jnp.dot(normed, both_weights, preferred_element_type=jnp.float32)]
where the time goes in v9:
time: 211 us; the launch traced here: 210 us
  Pallas kernels  80.7 us (38%)
  waiting for transfers between devices  69.7 us (33%)
  other arithmetic  20.7 us (10%)
  between operations  16.7 us (8%)
  local copies, waits for them, and re-layouts  15.9 us (8%)
  matrix products  6.21 us (3%)
    pallas_call x5, Pallas kernels, exchange(): pl.pallas_call(kernel, out_shape=out_shape, in_specs=[pl.BlockSpec(memory...  80.7 us
    all_gather x1, waiting for transfers between devices, per_device(): column_block = lax.all_gather(own_block, 'tensor', axis=1, tiled=True)  69.7 us
    reduce_sum x1, other arithmetic, per_device(): jnp.sum(wide * wide, axis=1, keepdims=True) / D + epsilon  6.51 us
    dot_general x1, matrix products, per_device(): both_acc = jnp.dot(normed, both_weights, preferred_element_type=jnp.float32)  5.82 us
    another operation x2, local copies, waits for them, and re-layouts, per_device(): attn_parts[0].reshape(tok_count, n_chip, 2, local_cols)  5.14 us
  transfers between devices with their start and end apart: 1, of which 1 were waited for; matrix products, arithmetic and copies ran while one was open for 1% of the time, Pallas kernels for 0%

profile of v9, /device:TPU:1, one launch (start us, length us, event | category | flops | bytes accessed | tf_op | source)
XLA Modules:
  0.0 210.0 jit_solution(2498127447205933936)
XLA Ops:
  7.2 0.0 all-gather.2.cloned.1.call-start
  7.2 0.8 copy.29
  8.0 0.1 eq.43
  8.1 0.1 eq.39
  8.2 1.3 reshape.140.refs_1_
  9.4 1.2 reduce-window.6
  10.6 0.2 slice_reduce_fusion
  10.9 0.2 fusion.17
  11.0 0.1 reduce_sum.113
  11.1 0.5 convert_reduce_fusion
  11.7 3.5 %reshape_squeeze.3 = bf16[64,8,2,448]{3,2,1,0:T(2,128)(2,1)S(1)} reshape(bf16[1,64,7168]{2,1,0:T(8,128)(2,1)} %param.8) | data formatting | bytes 1835008 | tf_op jit(solution)/shard_map/reshape;squeeze | solution.py:86
  15.2 1.6 copy.48
  16.8 11.5 %shard_map.94 = (bf16[2,8,64,448]{3,2,1,0:T(8,128)(2,1)}, bf16[2,1,448]{2,1,0:T(2,128)(2,1)}) custom-call(bf16[2,8,64,448]{3,2,1,0:T(8,128)(2,1)} %bitcast.35, bf16[1,448]{1,0:T(2,128)(2,1)} %reshape.140.refs_1_), custom_call_target="tpu_custom_call" | custom-call | tf_op jit(solution)/shard_map/pallas_call | solution.py:64
  28.3 2.2 %fusion.12.refs_0_ = bf16[8,64,448]{2,1,0:T(8,128)(2,1)} fusion(bf16[2,8,64,448]{3,2,1,0:T(8,128)(2,1)} %get-tuple-element.7), kind=kLoop, calls=%fused_computation.23 | loop fusion | flops 917504 | bytes 1376256 | tf_op jit(solution)/shard_map/convert_element_type | solution.py:88
  30.5 19.6 %shard_map.95 = (bf16[8,64,448]{2,1,0:T(8,128)(2,1)}, bf16[8,2,1,448]{3,2,1,0:T(2,128)(2,1)}) custom-call(bf16[8,64,448]{2,1,0:T(8,128)(2,1)} %fusion.12.refs_0_, bf16[2,1,448]{2,1,0:T(2,128)(2,1)} %get-tuple-element.8.refs_1_), custom_call_target="tpu_custom_call" | custom-call | tf_op jit(solution)/shard_map/pallas_call | solution.py:64
  50.1 1.1 convert_reduce_fusion.1
  51.2 0.4 convolution_convert_fusion
  51.6 0.3 copy.34
  51.9 1.0 reshape.141
  53.0 0.1 broadcast_in_dim.6
  53.1 0.9 pad_maximum_fusion.refs_0_
  54.0 27.0 %shard_map.96 = bf16[32,85,128]{2,1,0:T(8,128)(2,1)} custom-call(bf16[32,85,128]{2,1,0:T(8,128)(2,1)} %pad_maximum_fusion.refs_0_), custom_call_target="tpu_custom_call" | custom-call | tf_op jit(solution)/shard_map/pallas_call | solution.py:64
  81.0 2.0 reshape.142
  83.0 1.1 copy.35
  84.1 0.1 copy.37
  84.2 0.1 mul.86
  84.3 0.1 convert_reduce_fusion.3
  84.4 0.1 reshape.147
  84.5 1.5 convert_reduce_fusion.4
  86.0 69.7 %all-gather.2.cloned.1.call-done = bf16[768,7168]{0,1:T(8,128)(2,1)} async-done(((bf16[768,448]{0,1:T(8,128)(2,1)}), bf16[768,7168]{0,1:T(8,128)(2,1)}) %all-gather.2.cloned.1.call-update) | async-done | bytes 11010064 | tf_op jit(solution)/shard_map/all_gather | solution.py:111
  155.7 6.5 %fusion = f32[768]{0:T(1024)S(1)} fusion(bf16[768,7168]{0,1:T(8,128)(2,1)} %all-gather.2.cloned.1.call-done), kind=kLoop, calls=%fused_computation.3 | loop fusion | flops 16514304 | bytes 11013120 | tf_op jit(solution)/shard_map/reduce_sum | solution.py:113
  162.3 0.4 fusion.10
  162.6 0.4 copy-done
  163.0 5.8 %fusion.3 = f32[768,256]{0,1:T(8,128)S(1)} fusion(bf16[768,7168]{0,1:T(8,128)(2,1)S(1)} %copy-done, f32[7168]{0:T(1024)S(1)} %reshape.147, f32[768]{0:T(1024)S(1)} %add_rsqrt_fusion, bf16[7168,128]{1,0:T(8,128)(2,1)} %bitcast.41, bf16[7168,128]{1,0:T(8,128)(2,1)} %bitcast.42), kind=kOutput, calls=%fused_computation.6 | convolution fusion | flops 2847932416 | bytes 15498240 | tf_op jit(solution)/shard_map/dot_general | solution.py:118
  168.8 0.1 fusion.14
  168.9 0.6 pad_maximum_fusion.1.refs_0_
  169.5 10.4 %shard_map.97 = f32[16,12,128]{2,1,0:T(8,128)} custom-call(f32[12,128]{1,0:T(8,128)} %pad_maximum_fusion.1.refs_0_), custom_call_target="tpu_custom_call" | custom-call | tf_op jit(solution)/shard_map/pallas_call | solution.py:64
  179.9 0.9 reduce_sum.120
  180.9 0.1 reshape.143
  181.0 1.3 slice_reduce_fusion.1
  182.2 12.3 %shard_map.98 = f32[32,1,24]{2,1,0:T(1,128)} custom-call(f32[32,1,24]{2,1,0:T(1,128)} %get-tuple-element.17.refs_0_), custom_call_target="tpu_custom_call" | custom-call | tf_op jit(solution)/shard_map/pallas_call | solution.py:64
  194.5 0.5 broadcast.105
  195.0 1.4 reduce.12
  196.5 0.1 reshape.144
  196.5 2.3 %gather_fusion = f32[512]{0:T(512)S(1)} fusion(f32[768]{0:T(1024)S(1)} %reshape.144, s32[1024]{0:T(1024)S(1)} %pad_clamp_fusion), kind=kCustom, calls=%fused_computation | custom fusion | bytes 6144 | tf_op jit(solution)/shard_map/jit(_take)/gather | solution.py:133
  198.8 0.1 gather.7
  198.9 1.2 multiply_divide_fusion
  201.4 0.6 multiply_reduce_fusion.1
  (21 shorter events, 0.2 us)
Async XLA Ops:
  7.2 148.6 %all-gather.2.cloned.1.call-start = ((), (), s32[]{:S(2)}) async-start(), calls=%async_computation | async-start | bytes 11698176 | tf_op jit(solution)/shard_map/all_gather | solution.py:111
  11.7 39.5 %copy-start.1 = (bf16[64,448]{1,0:T(8,128)(2,1)S(1)}, bf16[64,448]{1,0:T(8,128)(2,1)}, u32[]{:S(2)}) copy-start(bf16[64,448]{1,0:T(8,128)(2,1)} %param.7) | copy-start | bytes 172036
  52.9 31.1 %copy-start.4 = (bf16[448]{0:T(512)(128)(2,1)S(1)}, bf16[448]{0:T(512)(128)(2,1)}, u32[]{:S(2)}) copy-start(bf16[448]{0:T(512)(128)(2,1)} %param.9) | copy-start | bytes 2692
  52.9 31.2 %copy-start.3 = (f32[64,8]{0,1:T(8,128)S(1)}, f32[64,8]{0,1:T(8,128)}, u32[]{:S(2)}) copy-start(f32[64,8]{0,1:T(8,128)} %param.11) | copy-start | bytes 6148
  53.0 31.3 %copy-start.2 = (bf16[8,2,1,448]{3,2,1,0:T(2,128)(2,1)S(1)}, bf16[8,2,1,448]{3,2,1,0:T(2,128)(2,1)}, u32[]{:S(2)}) copy-start(bf16[8,2,1,448]{3,2,1,0:T(2,128)(2,1)} %get-tuple-element.10) | copy-start | bytes 43012
  155.7 7.3 %copy-start = (bf16[768,7168]{0,1:T(8,128)(2,1)S(1)}, bf16[768,7168]{0,1:T(8,128)(2,1)}, u32[]{:S(2)}) copy-start(bf16[768,7168]{0,1:T(8,128)(2,1)} %all-gather.2.cloned.1.call-done) | copy-start | bytes 33030148
Sparse Core Ops, SparseCore 0:
  84.2 71.4 all-gather.1

commit v10 on v9

--- a/solution.py
+++ b/solution.py
@@ -109,9 +109,12 @@
     arrived_counts = arrived[:, lane_rows, 0].astype(jnp.float32)
     own_block = arrived[:, :lane_rows, :].reshape(n_expert * CAP, local_cols)
     column_block = lax.all_gather(own_block, "tensor", axis=1, tiled=True)
-    wide = column_block.astype(jnp.float32)
-    scaling = lax.rsqrt(jnp.sum(wide * wide, axis=1, keepdims=True) / D + epsilon)
-    normed = (wide * scaling * gain_full).astype(jnp.bfloat16)
+    own_wide = own_block.astype(jnp.float32)
+    own_squares = jnp.sum(own_wide * own_wide, axis=1).reshape(-1, 128)
+    (squares_in,) = exchange([(own_squares, True)], "tensor", 6, n_tensor)
+    row_squares = jnp.sum(squares_in, axis=0).reshape(-1, 1)
+    scaling = lax.rsqrt(row_squares / D + epsilon)
+    normed = (column_block.astype(jnp.float32) * scaling * gain_full).astype(jnp.bfloat16)
     normed_local = (own_block.astype(jnp.float32) * scaling * gain_local).astype(jnp.bfloat16)
     weight_cols = w_gate.shape[2]
     both_weights = jnp.concatenate([w_gate[0], w_gate_q[0]], axis=1)

time: 211 us -> 205 us (0.972)
  waiting for transfers between devices: 69.7 us -> 53.9 us
  Pallas kernels: 80.7 us -> 93.4 us
  other arithmetic: 20.7 us -> 15.8 us
  matrix products: 6.21 us -> 8.83 us
    all_gather x1, waiting for transfers between devices: 69.7 us -> 53.9 us  [per_device(): column_block = lax.all_gather(own_block, 'tensor', axis=1, tiled=True)]
    pallas_call x5 -> x6, Pallas kernels: 80.7 us -> 93.4 us  [exchange(): pl.pallas_call(kernel, out_shape=out_shape, in_specs=[pl.BlockSpec(memory...]
    reduce_sum x1 -> x2, other arithmetic: 6.51 us -> 1.7 us  [the longest x1 0.87 us: per_device(): row_squares = jnp.sum(squares_in, axis=0).reshape(-1, 1)]
    dot_general x1, matrix products: 5.82 us -> 8.45 us  [per_device(): both_acc = jnp.dot(normed, both_weights, preferred_element_type=jnp.float32)]
  transfers between devices with their start and end apart: 1 -> 1, of which waited for: 1 -> 1; matrix products, arithmetic and copies ran while one was open for 1% -> 3% of each run, Pallas kernels for 0% -> 6%
where the time goes in v10:
time: 205 us; the launch traced here: 204 us
  Pallas kernels  93.4 us (46%)
  waiting for transfers between devices  53.9 us (26%)
  between operations  16.7 us (8%)
  other arithmetic  15.8 us (8%)
  local copies, waits for them, and re-layouts  15.5 us (8%)
  matrix products  8.83 us (4%)
    pallas_call x6, Pallas kernels, exchange(): pl.pallas_call(kernel, out_shape=out_shape, in_specs=[pl.BlockSpec(memory...  93.4 us
    all_gather x1, waiting for transfers between devices, per_device(): column_block = lax.all_gather(own_block, 'tensor', axis=1, tiled=True)  53.9 us
    dot_general x1, matrix products, per_device(): both_acc = jnp.dot(normed, both_weights, preferred_element_type=jnp.float32)  8.45 us
    another operation x2, local copies, waits for them, and re-layouts, per_device(): attn_parts[0].reshape(tok_count, n_chip, 2, local_cols)  5.11 us
  transfers between devices with their start and end apart: 1, of which 1 were waited for; matrix products, arithmetic and copies ran while one was open for 3% of the time, Pallas kernels for 6%

profile of v10, /device:TPU:1, one launch (start us, length us, event | category | flops | bytes accessed | tf_op | source)
XLA Modules:
  0.0 204.2 jit_solution(10688052181773603162)
XLA Ops:
  7.2 0.8 copy.29
  8.0 0.1 eq.43
  8.1 0.1 eq.39
  8.2 1.3 reshape.152.refs_1_
  9.4 1.2 reduce-window.6
  10.6 0.2 slice_reduce_fusion
  10.9 0.2 fusion.16
  11.0 0.1 reduce_sum.122
  11.1 0.5 convert_reduce_fusion
  11.7 3.5 %reshape_squeeze.3 = bf16[64,8,2,448]{3,2,1,0:T(2,128)(2,1)S(1)} reshape(bf16[1,64,7168]{2,1,0:T(8,128)(2,1)} %param.8) | data formatting | bytes 1835008 | tf_op jit(solution)/shard_map/reshape;squeeze | solution.py:86
  15.2 1.6 copy.48
  16.8 11.6 %shard_map.94 = (bf16[2,8,64,448]{3,2,1,0:T(8,128)(2,1)}, bf16[2,1,448]{2,1,0:T(2,128)(2,1)}) custom-call(bf16[2,8,64,448]{3,2,1,0:T(8,128)(2,1)} %bitcast.38, bf16[1,448]{1,0:T(2,128)(2,1)} %reshape.152.refs_1_), custom_call_target="tpu_custom_call" | custom-call | tf_op jit(solution)/shard_map/pallas_call | solution.py:64
  28.4 2.2 %fusion.11.refs_0_ = bf16[8,64,448]{2,1,0:T(8,128)(2,1)} fusion(bf16[2,8,64,448]{3,2,1,0:T(8,128)(2,1)} %get-tuple-element.7), kind=kLoop, calls=%fused_computation.23 | loop fusion | flops 917504 | bytes 1376256 | tf_op jit(solution)/shard_map/convert_element_type | solution.py:88
  30.5 19.6 %shard_map.95 = (bf16[8,64,448]{2,1,0:T(8,128)(2,1)}, bf16[8,2,1,448]{3,2,1,0:T(2,128)(2,1)}) custom-call(bf16[8,64,448]{2,1,0:T(8,128)(2,1)} %fusion.11.refs_0_, bf16[2,1,448]{2,1,0:T(2,128)(2,1)} %get-tuple-element.8.refs_1_), custom_call_target="tpu_custom_call" | custom-call | tf_op jit(solution)/shard_map/pallas_call | solution.py:64
  50.1 1.1 convert_reduce_fusion.1
  51.3 0.4 convolution_convert_fusion
  51.7 0.3 copy.34
  52.0 1.0 reshape.153
  53.0 0.1 broadcast_in_dim.6
  53.1 0.9 pad_maximum_fusion.refs_0_
  54.1 27.0 %shard_map.96 = bf16[32,85,128]{2,1,0:T(8,128)(2,1)} custom-call(bf16[32,85,128]{2,1,0:T(8,128)(2,1)} %pad_maximum_fusion.refs_0_), custom_call_target="tpu_custom_call" | custom-call | tf_op jit(solution)/shard_map/pallas_call | solution.py:64
  81.1 2.0 reshape.154
  83.1 1.1 copy.35
  84.2 0.1 copy.37
  84.3 0.1 mul.86
  84.4 0.1 convert_reduce_fusion.3
  84.5 0.1 reshape.160
  84.6 0.8 fusion.6
  85.4 12.6 %shard_map.97 = f32[16,6,128]{2,1,0:T(8,128)} custom-call(f32[6,128]{1,0:T(8,128)} %bitcast.42), custom_call_target="tpu_custom_call" | custom-call | tf_op jit(solution)/shard_map/pallas_call | solution.py:64
  98.0 0.9 reduce_sum.127
  98.9 1.5 convert_reduce_fusion.4
  100.4 0.4 fusion.9
  100.8 1.2 multiply_divide_fusion
  102.0 53.9 %all-gather.2.cloned.1.call-done = bf16[768,7168]{0,1:T(8,128)(2,1)} async-done(((bf16[768,448]{0,1:T(8,128)(2,1)}), bf16[768,7168]{0,1:T(8,128)(2,1)}) %all-gather.2.cloned.1.call-update) | async-done | bytes 11010064 | tf_op jit(solution)/shard_map/all_gather | solution.py:111
  155.9 8.4 %fusion = f32[768,256]{0,1:T(8,128)S(1)} fusion(bf16[768,7168]{0,1:T(8,128)(2,1)} %all-gather.2.cloned.1.call-done, f32[7168]{0:T(1024)S(1)} %reshape.160, f32[768]{0:T(1024)S(1)} %rsqrt_bitcast_fusion, bf16[7168,128]{1,0:T(8,128)(2,1)S(1)} %bitcast.45, bf16[7168,128]{1,0:T(8,128)(2,1)} %bitcast.46), kind=kOutput, calls=%fused_computation.2 | convolution fusion | flops 2847932416 | bytes 15498240 | tf_op jit(solution)/shard_map/dot_general | solution.py:121
  164.3 0.1 fusion.13
  164.4 0.6 pad_maximum_fusion.1.refs_0_
  165.0 10.4 %shard_map.98 = f32[16,12,128]{2,1,0:T(8,128)} custom-call(f32[12,128]{1,0:T(8,128)} %pad_maximum_fusion.1.refs_0_), custom_call_target="tpu_custom_call" | custom-call | tf_op jit(solution)/shard_map/pallas_call | solution.py:64
  175.4 0.9 reduce_sum.130
  176.4 0.1 reshape.156
  176.5 1.3 slice_reduce_fusion.1
  177.7 12.3 %shard_map.99 = f32[32,1,24]{2,1,0:T(1,128)} custom-call(f32[32,1,24]{2,1,0:T(1,128)} %get-tuple-element.17.refs_0_), custom_call_target="tpu_custom_call" | custom-call | tf_op jit(solution)/shard_map/pallas_call | solution.py:64
  190.0 0.5 broadcast.109
  190.5 1.3 reduce.12
  191.8 0.1 reshape.157
  191.9 2.3 %gather_fusion = f32[512]{0:T(512)S(1)} fusion(f32[768]{0:T(1024)S(1)} %reshape.157, s32[1024]{0:T(1024)S(1)} %pad_clamp_fusion), kind=kCustom, calls=%fused_computation | custom fusion | bytes 6144 | tf_op jit(solution)/shard_map/jit(_take)/gather | solution.py:136
  194.2 0.1 gather.7
  195.6 0.6 multiply_reduce_fusion.1
  (23 shorter events, 0.2 us)
Async XLA Ops:
  7.2 148.7 %all-gather.2.cloned.1.call-start = ((), (), s32[]{:S(2)}) async-start(), calls=%async_computation | async-start | bytes 11698176 | tf_op jit(solution)/shard_map/all_gather | solution.py:111
  16.8 34.5 %copy-start = (bf16[64,448]{1,0:T(8,128)(2,1)S(1)}, bf16[64,448]{1,0:T(8,128)(2,1)}, u32[]{:S(2)}) copy-start(bf16[64,448]{1,0:T(8,128)(2,1)} %param.7) | copy-start | bytes 172036
  81.1 3.1 %copy-start.3 = (bf16[448]{0:T(512)(128)(2,1)S(1)}, bf16[448]{0:T(512)(128)(2,1)}, u32[]{:S(2)}) copy-start(bf16[448]{0:T(512)(128)(2,1)} %param.9) | copy-start | bytes 2692
  81.1 3.2 %copy-start.2 = (f32[64,8]{0,1:T(8,128)S(1)}, f32[64,8]{0,1:T(8,128)}, u32[]{:S(2)}) copy-start(f32[64,8]{0,1:T(8,128)} %param.11) | copy-start | bytes 6148
  81.1 3.3 %copy-start.1 = (bf16[8,2,1,448]{3,2,1,0:T(2,128)(2,1)S(1)}, bf16[8,2,1,448]{3,2,1,0:T(2,128)(2,1)}, u32[]{:S(2)}) copy-start(bf16[8,2,1,448]{3,2,1,0:T(2,128)(2,1)} %get-tuple-element.10) | copy-start | bytes 43012
  83.1 72.8 %copy-start.4 = (bf16[1,7168,128]{2,1,0:T(8,128)(2,1)S(1)}, bf16[1,7168,128]{2,1,0:T(8,128)(2,1)}, u32[]{:S(2)}) copy-start(bf16[1,7168,128]{2,1,0:T(8,128)(2,1)} %param.13) | copy-start | bytes 5505028
Sparse Core Ops, SparseCore 0:
  84.3 71.5 all-gather.1

commit v11 on v10

--- a/solution.py
+++ b/solution.py
@@ -30,10 +30,6 @@
         def member(k):
             return base + lax.rem(pos + k, size) * stride
 
-        barrier = pltpu.get_barrier_semaphore()
-        for k in range(1, size):
-            pl.semaphore_signal(barrier, inc=1, device_id={axis: member(k)}, device_id_type=MESH_ID)
-        pl.semaphore_wait(barrier, size - 1)
         copies = []
         for a in range(count):
             x_ref, o_ref, gather = x_refs[a], o_refs[a], modes[a]
@@ -71,7 +67,7 @@
             pltpu.SemaphoreType.DMA((count, size)),
             pltpu.SemaphoreType.DMA((count, size)),
         ],
-        compiler_params=pltpu.CompilerParams(collective_id=cid, has_side_effects=True),
+        compiler_params=pltpu.CompilerParams(has_side_effects=True),
     )(*[x for x, _ in arrays])
 
 

time: 205 us -> 264 us (1.29)
  Pallas kernels: 93.4 us -> 163 us
  waiting for transfers between devices: 53.9 us -> 43.1 us
    pallas_call x6, Pallas kernels: 93.4 us -> 163 us  [exchange(): pl.pallas_call(kernel, out_shape=out_shape, in_specs=[pl.BlockSpec(memory...]
    all_gather x1, waiting for transfers between devices: 53.9 us -> 43 us  [per_device(): column_block = lax.all_gather(own_block, 'tensor', axis=1, tiled=True)]
  transfers between devices with their start and end apart: 1 -> 1, of which waited for: 1 -> 1; matrix products, arithmetic and copies ran while one was open for 3% -> 2% of each run, Pallas kernels for 6% -> 10%
where the time goes in v11:
time: 264 us; the launch traced here: 263 us
  Pallas kernels  163 us (62%)
  waiting for transfers between devices  43.1 us (16%)
  between operations  16.7 us (6%)
  other arithmetic  15.8 us (6%)
  local copies, waits for them, and re-layouts  15.3 us (6%)
  matrix products  8.83 us (3%)
    pallas_call x6, Pallas kernels, exchange(): pl.pallas_call(kernel, out_shape=out_shape, in_specs=[pl.BlockSpec(memory...  163 us
    all_gather x1, waiting for transfers between devices, per_device(): column_block = lax.all_gather(own_block, 'tensor', axis=1, tiled=True)  43 us
    dot_general x1, matrix products, per_device(): both_acc = jnp.dot(normed, both_weights, preferred_element_type=jnp.float32)  8.45 us
  transfers between devices with their start and end apart: 1, of which 1 were waited for; matrix products, arithmetic and copies ran while one was open for 2% of the time, Pallas kernels for 10%

profile of v11, /device:TPU:1, one launch (start us, length us, event | category | flops | bytes accessed | tf_op | source)
XLA Modules:
  0.0 263.3 jit_solution(1650560829075368421)
XLA Ops:
  7.2 0.8 copy.29
  8.0 0.1 eq.43
  8.1 0.1 eq.39
  8.2 1.3 reshape.152.refs_1_
  9.4 1.2 reduce-window.6
  10.6 0.2 slice_reduce_fusion
  10.9 0.2 fusion.16
  11.0 0.1 reduce_sum.122
  11.1 0.5 convert_reduce_fusion
  11.7 3.5 %reshape_squeeze.3 = bf16[64,8,2,448]{3,2,1,0:T(2,128)(2,1)S(1)} reshape(bf16[1,64,7168]{2,1,0:T(8,128)(2,1)} %param.8) | data formatting | bytes 1835008 | tf_op jit(solution)/shard_map/reshape;squeeze | solution.py:82
  15.2 1.6 copy.48
  16.8 27.0 %shard_map.94 = (bf16[2,8,64,448]{3,2,1,0:T(8,128)(2,1)}, bf16[2,1,448]{2,1,0:T(2,128)(2,1)}) custom-call(bf16[2,8,64,448]{3,2,1,0:T(8,128)(2,1)} %bitcast.38, bf16[1,448]{1,0:T(2,128)(2,1)} %reshape.152.refs_1_), custom_call_target="tpu_custom_call" | custom-call | tf_op jit(solution)/shard_map/pallas_call | solution.py:60
  43.8 2.2 fusion.11.refs_0_
  46.0 31.5 %shard_map.95 = (bf16[8,64,448]{2,1,0:T(8,128)(2,1)}, bf16[8,2,1,448]{3,2,1,0:T(2,128)(2,1)}) custom-call(bf16[8,64,448]{2,1,0:T(8,128)(2,1)} %fusion.11.refs_0_, bf16[2,1,448]{2,1,0:T(2,128)(2,1)} %get-tuple-element.8.refs_1_), custom_call_target="tpu_custom_call" | custom-call | tf_op jit(solution)/shard_map/pallas_call | solution.py:60
  77.5 1.1 convert_reduce_fusion.1
  78.7 0.4 convolution_convert_fusion
  79.1 0.3 copy.34
  79.3 1.0 reshape.153
  80.4 0.1 broadcast_in_dim.6
  80.5 0.9 pad_maximum_fusion.refs_0_
  81.4 35.0 %shard_map.96 = bf16[32,85,128]{2,1,0:T(8,128)(2,1)} custom-call(bf16[32,85,128]{2,1,0:T(8,128)(2,1)} %pad_maximum_fusion.refs_0_), custom_call_target="tpu_custom_call" | custom-call | tf_op jit(solution)/shard_map/pallas_call | solution.py:60
  116.5 1.8 reshape.154
  118.3 1.1 copy.35
  119.4 0.1 copy.37
  119.5 0.1 mul.86
  119.6 0.1 convert_reduce_fusion.3
  119.7 0.1 reshape.160
  119.8 0.8 fusion.6
  120.7 26.1 %shard_map.97 = f32[16,6,128]{2,1,0:T(8,128)} custom-call(f32[6,128]{1,0:T(8,128)} %bitcast.42), custom_call_target="tpu_custom_call" | custom-call | tf_op jit(solution)/shard_map/pallas_call | solution.py:60
  146.8 0.9 reduce_sum.127
  147.7 1.5 convert_reduce_fusion.4
  149.1 0.4 fusion.9
  149.5 1.2 multiply_divide_fusion
  150.7 43.0 %all-gather.2.cloned.1.call-done = bf16[768,7168]{0,1:T(8,128)(2,1)} async-done(((bf16[768,448]{0,1:T(8,128)(2,1)}), bf16[768,7168]{0,1:T(8,128)(2,1)}) %all-gather.2.cloned.1.call-update) | async-done | bytes 11010064 | tf_op jit(solution)/shard_map/all_gather | solution.py:107
  193.8 8.4 %fusion = f32[768,256]{0,1:T(8,128)S(1)} fusion(bf16[768,7168]{0,1:T(8,128)(2,1)} %all-gather.2.cloned.1.call-done, f32[7168]{0:T(1024)S(1)} %reshape.160, f32[768]{0:T(1024)S(1)} %rsqrt_bitcast_fusion, bf16[7168,128]{1,0:T(8,128)(2,1)S(1)} %bitcast.45, bf16[7168,128]{1,0:T(8,128)(2,1)} %bitcast.46), kind=kOutput, calls=%fused_computation.2 | convolution fusion | flops 2847932416 | bytes 15498240 | tf_op jit(solution)/shard_map/dot_general | solution.py:117
  202.2 0.1 fusion.13
  202.3 0.6 pad_maximum_fusion.1.refs_0_
  202.9 23.0 %shard_map.98 = f32[16,12,128]{2,1,0:T(8,128)} custom-call(f32[12,128]{1,0:T(8,128)} %pad_maximum_fusion.1.refs_0_), custom_call_target="tpu_custom_call" | custom-call | tf_op jit(solution)/shard_map/pallas_call | solution.py:60
  225.9 0.9 reduce_sum.130
  226.8 0.1 reshape.156
  226.9 1.3 slice_reduce_fusion.1
  228.2 20.9 %shard_map.99 = f32[32,1,24]{2,1,0:T(1,128)} custom-call(f32[32,1,24]{2,1,0:T(1,128)} %get-tuple-element.17.refs_0_), custom_call_target="tpu_custom_call" | custom-call | tf_op jit(solution)/shard_map/pallas_call | solution.py:60
  249.1 0.5 broadcast.109
  249.6 1.3 reduce.12
  250.9 0.1 reshape.157
  251.0 2.3 gather_fusion
  253.3 0.1 gather.7
  254.7 0.6 multiply_reduce_fusion.1
  (23 shorter events, 0.2 us)
Async XLA Ops:
  7.2 186.6 %all-gather.2.cloned.1.call-start = ((), (), s32[]{:S(2)}) async-start(), calls=%async_computation | async-start | bytes 11698176 | tf_op jit(solution)/shard_map/all_gather | solution.py:107
  16.8 61.9 %copy-start = (bf16[64,448]{1,0:T(8,128)(2,1)S(1)}, bf16[64,448]{1,0:T(8,128)(2,1)}, u32[]{:S(2)}) copy-start(bf16[64,448]{1,0:T(8,128)(2,1)} %param.7) | copy-start | bytes 172036
  116.4 3.0 %copy-start.3 = (bf16[448]{0:T(512)(128)(2,1)S(1)}, bf16[448]{0:T(512)(128)(2,1)}, u32[]{:S(2)}) copy-start(bf16[448]{0:T(512)(128)(2,1)} %param.9) | copy-start | bytes 2692
  116.5 3.0 %copy-start.2 = (f32[64,8]{0,1:T(8,128)S(1)}, f32[64,8]{0,1:T(8,128)}, u32[]{:S(2)}) copy-start(f32[64,8]{0,1:T(8,128)} %param.11) | copy-start | bytes 6148
  116.5 3.2 %copy-start.1 = (bf16[8,2,1,448]{3,2,1,0:T(2,128)(2,1)S(1)}, bf16[8,2,1,448]{3,2,1,0:T(2,128)(2,1)}, u32[]{:S(2)}) copy-start(bf16[8,2,1,448]{3,2,1,0:T(2,128)(2,1)} %get-tuple-element.10) | copy-start | bytes 43012
  118.3 75.5 %copy-start.4 = (bf16[1,7168,128]{2,1,0:T(8,128)(2,1)S(1)}, bf16[1,7168,128]{2,1,0:T(8,128)(2,1)}, u32[]{:S(2)}) copy-start(bf16[1,7168,128]{2,1,0:T(8,128)(2,1)} %param.13) | copy-start | bytes 5505028
Sparse Core Ops, SparseCore 0:
  119.5 74.2 all-gather.1

commit v12 on v10

--- a/solution.py
+++ b/solution.py
@@ -83,12 +83,14 @@
     top_count = routes.shape[1]
     gain_local = norm_gain.astype(jnp.float32)[None, :]
     n_chip = n_tensor // 2
+    dense_rows = tok_count * local_cols // 128
     column_parts = attn_parts[0].reshape(tok_count, n_chip, 2, local_cols).transpose(2, 1, 0, 3)
+    column_parts = column_parts.reshape(2, n_chip, dense_rows, 128)
     pair_in, gain_pair = exchange([(column_parts, False), (norm_gain.reshape(1, local_cols), True)], "tensor", 0, 2)
     pair_sum = (pair_in[0].astype(jnp.float32) + pair_in[1].astype(jnp.float32)).astype(jnp.bfloat16)
     parts_in, gain_in = exchange([(pair_sum, False), (gain_pair, True)], "tensor", 4, n_chip, 2)
     gain_full = gain_in.reshape(1, n_tensor * local_cols).astype(jnp.float32)
-    summed = jnp.sum(parts_in.astype(jnp.float32), axis=0)
+    summed = jnp.sum(parts_in.astype(jnp.float32), axis=0).reshape(tok_count, local_cols)
     hidden = (residual.astype(jnp.float32) + summed).astype(jnp.bfloat16)
     expert_ids = jnp.arange(n_expert, dtype=jnp.int32)
     flat_routes = routes.reshape(-1)

time: 205 us -> 205 us (level)
    reshape x0 -> x2, local copies, waits for them, and re-layouts: none -> 2.25 us  [the longest x1 2.16 us: per_device(): column_parts = column_parts.reshape(2, n_chip, dense_rows, 128)]
where the time goes in v12:
time: 205 us; the launch traced here: 204 us
  Pallas kernels  92 us (45%)
  waiting for transfers between devices  54 us (26%)
  between operations  16.8 us (8%)
  local copies, waits for them, and re-layouts  16.7 us (8%)
  other arithmetic  15.7 us (8%)
  matrix products  8.83 us (4%)
    pallas_call x6, Pallas kernels, exchange(): pl.pallas_call(kernel, out_shape=out_shape, in_specs=[pl.BlockSpec(memory...  92 us
    all_gather x1, waiting for transfers between devices, per_device(): column_block = lax.all_gather(own_block, 'tensor', axis=1, tiled=True)  54 us
    dot_general x1, matrix products, per_device(): both_acc = jnp.dot(normed, both_weights, preferred_element_type=jnp.float32)  8.45 us
  transfers between devices with their start and end apart: 1, of which 1 were waited for; matrix products, arithmetic and copies ran while one was open for 3% of the time, Pallas kernels for 6%

profile of v12, /device:TPU:1, one launch (start us, length us, event | category | flops | bytes accessed | tf_op | source)
XLA Modules:
  0.0 204.0 jit_solution(13177925566471694966)
XLA Ops:
  7.2 0.8 copy.30
  8.0 0.1 eq.43
  8.1 0.1 eq.39
  8.2 1.3 reshape.159.refs_1_
  9.4 1.2 reduce-window.6
  10.6 0.2 slice_reduce_fusion
  10.9 0.2 fusion.16
  11.0 0.1 reduce_sum.122
  11.1 0.5 convert_reduce_fusion
  11.7 3.5 %reshape_squeeze.3 = bf16[64,8,2,448]{3,2,1,0:T(2,128)(2,1)S(1)} reshape(bf16[1,64,7168]{2,1,0:T(8,128)(2,1)} %param.8) | data formatting | bytes 1835008 | tf_op jit(solution)/shard_map/reshape;squeeze | solution.py:87
  15.2 0.6 copy.49
  15.8 2.2 %reshape.158.refs_0_ = bf16[2,8,224,128]{3,2,1,0:T(8,128)(2,1)} reshape(bf16[2,8,64,448]{3,2,1,0:T(8,128)(2,1)S(1)} %bitcast.40) | data formatting | bytes 1835008 | tf_op jit(solution)/shard_map/reshape | solution.py:88
  17.9 11.6 %shard_map.94 = (bf16[2,8,224,128]{3,2,1,0:T(8,128)(2,1)}, bf16[2,1,448]{2,1,0:T(2,128)(2,1)}) custom-call(bf16[2,8,224,128]{3,2,1,0:T(8,128)(2,1)} %reshape.158.refs_0_, bf16[1,448]{1,0:T(2,128)(2,1)} %reshape.159.refs_1_), custom_call_target="tpu_custom_call" | custom-call | tf_op jit(solution)/shard_map/pallas_call | solution.py:64
  29.6 2.1 %fusion.11.refs_0_ = bf16[8,224,128]{2,1,0:T(8,128)(2,1)} fusion(bf16[2,8,224,128]{3,2,1,0:T(8,128)(2,1)} %get-tuple-element.7), kind=kLoop, calls=%fused_computation.23 | loop fusion | flops 917504 | bytes 1376256 | tf_op jit(solution)/shard_map/convert_element_type | solution.py:90
  31.6 17.9 %shard_map.95 = (bf16[8,224,128]{2,1,0:T(8,128)(2,1)}, bf16[8,2,1,448]{3,2,1,0:T(2,128)(2,1)}) custom-call(bf16[8,224,128]{2,1,0:T(8,128)(2,1)} %fusion.11.refs_0_, bf16[2,1,448]{2,1,0:T(2,128)(2,1)} %get-tuple-element.8.refs_1_), custom_call_target="tpu_custom_call" | custom-call | tf_op jit(solution)/shard_map/pallas_call | solution.py:64
  49.5 1.1 convert_reduce_fusion.1
  50.6 0.1 reshape.160
  50.7 0.4 convolution_convert_fusion
  51.1 0.3 copy.35
  51.4 1.0 reshape.161
  52.4 0.1 broadcast_in_dim.6
  52.5 0.9 pad_maximum_fusion.refs_0_
  53.4 27.0 %shard_map.96 = bf16[32,85,128]{2,1,0:T(8,128)(2,1)} custom-call(bf16[32,85,128]{2,1,0:T(8,128)(2,1)} %pad_maximum_fusion.refs_0_), custom_call_target="tpu_custom_call" | custom-call | tf_op jit(solution)/shard_map/pallas_call | solution.py:64
  80.5 2.0 reshape.162
  82.5 1.1 copy.36
  83.6 0.1 copy.38
  83.7 0.1 mul.86
  83.8 0.1 convert_reduce_fusion.3
  83.9 0.1 reshape.168
  84.0 0.8 fusion.6
  84.8 12.9 %shard_map.97 = f32[16,6,128]{2,1,0:T(8,128)} custom-call(f32[6,128]{1,0:T(8,128)} %bitcast.44), custom_call_target="tpu_custom_call" | custom-call | tf_op jit(solution)/shard_map/pallas_call | solution.py:64
  97.7 0.9 reduce_sum.127
  98.6 1.5 convert_reduce_fusion.4
  100.1 0.4 fusion.9
  100.4 1.2 multiply_divide_fusion
  101.7 54.0 %all-gather.2.cloned.1.call-done = bf16[768,7168]{0,1:T(8,128)(2,1)} async-done(((bf16[768,448]{0,1:T(8,128)(2,1)}), bf16[768,7168]{0,1:T(8,128)(2,1)}) %all-gather.2.cloned.1.call-update) | async-done | bytes 11010064 | tf_op jit(solution)/shard_map/all_gather | solution.py:113
  155.6 8.4 %fusion = f32[768,256]{0,1:T(8,128)S(1)} fusion(bf16[768,7168]{0,1:T(8,128)(2,1)} %all-gather.2.cloned.1.call-done, f32[7168]{0:T(1024)S(1)} %reshape.168, f32[768]{0:T(1024)S(1)} %rsqrt_bitcast_fusion, bf16[7168,128]{1,0:T(8,128)(2,1)S(1)} %bitcast.47, bf16[7168,128]{1,0:T(8,128)(2,1)} %bitcast.48), kind=kOutput, calls=%fused_computation.2 | convolution fusion | flops 2847932416 | bytes 15498240 | tf_op jit(solution)/shard_map/dot_general | solution.py:123
  164.2 0.6 pad_maximum_fusion.1.refs_0_
  164.8 10.4 %shard_map.98 = f32[16,12,128]{2,1,0:T(8,128)} custom-call(f32[12,128]{1,0:T(8,128)} %pad_maximum_fusion.1.refs_0_), custom_call_target="tpu_custom_call" | custom-call | tf_op jit(solution)/shard_map/pallas_call | solution.py:64
  175.2 0.9 reduce_sum.130
  176.3 1.3 slice_reduce_fusion.1
  177.5 12.3 %shard_map.99 = f32[32,1,24]{2,1,0:T(1,128)} custom-call(f32[32,1,24]{2,1,0:T(1,128)} %get-tuple-element.17.refs_0_), custom_call_target="tpu_custom_call" | custom-call | tf_op jit(solution)/shard_map/pallas_call | solution.py:64
  189.8 0.5 broadcast.109
  190.3 1.3 reduce.12
  191.6 0.1 reshape.165
  191.7 2.3 %gather_fusion = f32[512]{0:T(512)S(1)} fusion(f32[768]{0:T(1024)S(1)} %reshape.165, s32[1024]{0:T(1024)S(1)} %pad_clamp_fusion), kind=kCustom, calls=%fused_computation | custom fusion | bytes 6144 | tf_op jit(solution)/shard_map/jit(_take)/gather | solution.py:138
  194.0 0.1 gather.7
  195.4 0.6 multiply_reduce_fusion.1
  (25 shorter events, 0.4 us)
Async XLA Ops:
  7.2 148.5 %all-gather.2.cloned.1.call-start = ((), (), s32[]{:S(2)}) async-start(), calls=%async_computation | async-start | bytes 11698176 | tf_op jit(solution)/shard_map/all_gather | solution.py:113
  17.9 32.8 %copy-start = (bf16[64,448]{1,0:T(8,128)(2,1)S(1)}, bf16[64,448]{1,0:T(8,128)(2,1)}, u32[]{:S(2)}) copy-start(bf16[64,448]{1,0:T(8,128)(2,1)} %param.7) | copy-start | bytes 172036
  80.4 3.1 %copy-start.3 = (bf16[448]{0:T(512)(128)(2,1)S(1)}, bf16[448]{0:T(512)(128)(2,1)}, u32[]{:S(2)}) copy-start(bf16[448]{0:T(512)(128)(2,1)} %param.9) | copy-start | bytes 2692
  80.4 3.2 %copy-start.2 = (f32[64,8]{0,1:T(8,128)S(1)}, f32[64,8]{0,1:T(8,128)}, u32[]{:S(2)}) copy-start(f32[64,8]{0,1:T(8,128)} %param.11) | copy-start | bytes 6148
  80.5 3.3 %copy-start.1 = (bf16[8,2,1,448]{3,2,1,0:T(2,128)(2,1)S(1)}, bf16[8,2,1,448]{3,2,1,0:T(2,128)(2,1)}, u32[]{:S(2)}) copy-start(bf16[8,2,1,448]{3,2,1,0:T(2,128)(2,1)} %get-tuple-element.10) | copy-start | bytes 43012
  82.4 73.2 %copy-start.4 = (bf16[1,7168,128]{2,1,0:T(8,128)(2,1)S(1)}, bf16[1,7168,128]{2,1,0:T(8,128)(2,1)}, u32[]{:S(2)}) copy-start(bf16[1,7168,128]{2,1,0:T(8,128)(2,1)} %param.13) | copy-start | bytes 5505028
Sparse Core Ops, SparseCore 0:
  83.7 71.8 all-gather.1

commit v13 on v10

--- a/solution.py
+++ b/solution.py
@@ -100,6 +100,7 @@
     slot_ids = jnp.arange(n_expert * CAP, dtype=jnp.int32)
     placing = (slot_ids[:, None] == target[None, :]).reshape(n_expert * CAP, tok_count, top_count)
     dispatch = jnp.sum(placing.astype(jnp.int32), axis=2).astype(jnp.bfloat16)
+    weighted_slots = jnp.sum(jnp.where(placing, route_weights[None, :, :], 0.0), axis=2)
     outgoing = jnp.dot(dispatch, hidden, preferred_element_type=jnp.float32).astype(jnp.bfloat16)
     lane_rows = CAP * local_cols // 128
     outgoing = outgoing.reshape(n_expert, lane_rows, 128)
@@ -133,8 +134,7 @@
     expert_total = jnp.sum(slots[:, 0]) / (jnp.sum(slots[:, 1]) + epsilon)
     slot_ratios = (slots[:, 0] / (slots[:, 1] + epsilon)).reshape(n_expert, 1, CAP)
     (back,) = exchange([(slot_ratios, False)], "expert", 3, n_expert)
-    ratios = jnp.take(back.reshape(-1), target).reshape(tok_count, top_count)
-    token_error = jnp.sum(route_weights * ratios, axis=1)
+    token_error = jnp.dot(back.reshape(1, -1), weighted_slots, precision=lax.Precision.HIGHEST).reshape(tok_count)
     return (token_error, expert_total.reshape(1), hess_local.reshape(1, local_cols))
 
 

time: 205 us -> 204 us (level)
  local copies, waits for them, and re-layouts: 15.5 us -> 13.2 us
    gather x2 -> x0, local copies, waits for them, and re-layouts: 2.37 us -> none  [per_device(): ratios = jnp.take(back.reshape(-1), target).reshape(tok_count, top_count)]
where the time goes in v13:
time: 204 us; the launch traced here: 203 us
  Pallas kernels  93.4 us (46%)
  waiting for transfers between devices  53.5 us (26%)
  between operations  16.7 us (8%)
  other arithmetic  16.4 us (8%)
  local copies, waits for them, and re-layouts  13.2 us (6%)
  matrix products  9.53 us (5%)
    pallas_call x6, Pallas kernels, exchange(): pl.pallas_call(kernel, out_shape=out_shape, in_specs=[pl.BlockSpec(memory...  93.4 us
    all_gather x1, waiting for transfers between devices, per_device(): column_block = lax.all_gather(own_block, 'tensor', axis=1, tiled=True)  53.5 us
    dot_general x1, matrix products, per_device(): both_acc = jnp.dot(normed, both_weights, preferred_element_type=jnp.float32)  8.35 us
    another operation x2, local copies, waits for them, and re-layouts, per_device(): attn_parts[0].reshape(tok_count, n_chip, 2, local_cols)  5.11 us
  transfers between devices with their start and end apart: 1, of which 1 were waited for; matrix products, arithmetic and copies ran while one was open for 3% of the time, Pallas kernels for 6%

profile of v13, /device:TPU:1, one launch (start us, length us, event | category | flops | bytes accessed | tf_op | source)
XLA Modules:
  0.0 202.7 jit_solution(1706790306441505961)
XLA Ops:
  7.2 0.8 copy.42
  8.0 0.1 eq.44
  8.1 0.1 eq.40
  8.2 1.3 reshape.120.refs_1_
  9.4 1.2 reduce-window.6
  10.6 0.2 slice_reduce_fusion
  10.9 0.2 fusion.16
  11.0 0.1 reduce_sum.120
  11.2 0.7 multiply_add_fusion
  11.9 0.1 copy.46
  12.0 0.5 convert_reduce_fusion
  12.5 3.5 %reshape_squeeze.3 = bf16[64,8,2,448]{3,2,1,0:T(2,128)(2,1)S(1)} reshape(bf16[1,64,7168]{2,1,0:T(8,128)(2,1)} %param.8) | data formatting | bytes 1835008 | tf_op jit(solution)/shard_map/reshape;squeeze | solution.py:86
  16.0 1.6 copy.62
  17.6 11.6 %shard_map.94 = (bf16[2,8,64,448]{3,2,1,0:T(8,128)(2,1)}, bf16[2,1,448]{2,1,0:T(2,128)(2,1)}) custom-call(bf16[2,8,64,448]{3,2,1,0:T(8,128)(2,1)} %bitcast.40, bf16[1,448]{1,0:T(2,128)(2,1)} %reshape.120.refs_1_), custom_call_target="tpu_custom_call" | custom-call | tf_op jit(solution)/shard_map/pallas_call | solution.py:64
  29.2 2.2 %fusion.11.refs_0_ = bf16[8,64,448]{2,1,0:T(8,128)(2,1)} fusion(bf16[2,8,64,448]{3,2,1,0:T(8,128)(2,1)} %get-tuple-element.7), kind=kLoop, calls=%fused_computation.24 | loop fusion | flops 917504 | bytes 1376256 | tf_op jit(solution)/shard_map/convert_element_type | solution.py:88
  31.4 19.6 %shard_map.95 = (bf16[8,64,448]{2,1,0:T(8,128)(2,1)}, bf16[8,2,1,448]{3,2,1,0:T(2,128)(2,1)}) custom-call(bf16[8,64,448]{2,1,0:T(8,128)(2,1)} %fusion.11.refs_0_, bf16[2,1,448]{2,1,0:T(2,128)(2,1)} %get-tuple-element.8.refs_1_), custom_call_target="tpu_custom_call" | custom-call | tf_op jit(solution)/shard_map/pallas_call | solution.py:64
  51.0 1.1 convert_reduce_fusion.1
  52.1 0.4 convolution_convert_fusion
  52.5 0.3 copy.48
  52.8 1.0 reshape.121
  53.9 0.1 broadcast_in_dim.14
  54.0 0.9 pad_maximum_fusion.refs_0_
  54.9 27.0 %shard_map.96 = bf16[32,85,128]{2,1,0:T(8,128)(2,1)} custom-call(bf16[32,85,128]{2,1,0:T(8,128)(2,1)} %pad_maximum_fusion.refs_0_), custom_call_target="tpu_custom_call" | custom-call | tf_op jit(solution)/shard_map/pallas_call | solution.py:64
  81.9 2.0 reshape.122
  83.9 1.1 copy.49
  85.1 0.1 copy.51
  85.1 0.1 convert_reduce_fusion.3
  85.3 0.1 reshape.128
  85.4 0.8 fusion.6
  86.2 12.6 %shard_map.97 = f32[16,6,128]{2,1,0:T(8,128)} custom-call(f32[6,128]{1,0:T(8,128)} %bitcast.43), custom_call_target="tpu_custom_call" | custom-call | tf_op jit(solution)/shard_map/pallas_call | solution.py:64
  98.7 0.9 reduce_sum.125
  99.6 1.5 convert_reduce_fusion.4
  101.1 0.5 select_reduce_fusion
  101.7 0.3 fusion.9
  102.0 1.2 multiply_divide_fusion
  103.2 53.5 %all-gather.2.cloned.1.call-done = bf16[768,7168]{0,1:T(8,128)(2,1)} async-done(((bf16[768,448]{0,1:T(8,128)(2,1)}), bf16[768,7168]{0,1:T(8,128)(2,1)}) %all-gather.2.cloned.1.call-update) | async-done | bytes 11010064 | tf_op jit(solution)/shard_map/all_gather | solution.py:112
  156.7 8.4 %fusion = f32[768,256]{0,1:T(8,128)S(1)} fusion(bf16[768,7168]{0,1:T(8,128)(2,1)} %all-gather.2.cloned.1.call-done, f32[7168]{0:T(1024)S(1)} %reshape.128, f32[768]{0:T(1024)S(1)} %rsqrt_bitcast_fusion, bf16[7168,128]{1,0:T(8,128)(2,1)S(1)} %bitcast.45, bf16[7168,128]{1,0:T(8,128)(2,1)} %bitcast.46), kind=kOutput, calls=%fused_computation.1 | convolution fusion | flops 2847932416 | bytes 15498240 | tf_op jit(solution)/shard_map/dot_general | solution.py:122
  165.1 0.1 fusion.13
  165.2 0.6 pad_maximum_fusion.1.refs_0_
  165.8 10.4 %shard_map.98 = f32[16,12,128]{2,1,0:T(8,128)} custom-call(f32[12,128]{1,0:T(8,128)} %pad_maximum_fusion.1.refs_0_), custom_call_target="tpu_custom_call" | custom-call | tf_op jit(solution)/shard_map/pallas_call | solution.py:64
  176.2 0.9 reduce_sum.128
  177.1 0.1 reshape.124
  177.2 1.3 slice_reduce_fusion.1
  178.5 12.3 %shard_map.99 = f32[32,1,24]{2,1,0:T(1,128)} custom-call(f32[32,1,24]{2,1,0:T(1,128)} %get-tuple-element.17.refs_0_), custom_call_target="tpu_custom_call" | custom-call | tf_op jit(solution)/shard_map/pallas_call | solution.py:64
  190.8 0.5 broadcast.65
  191.3 1.3 reduce.12
  192.6 0.1 reshape.129
  194.0 0.8 convolution_bitcast_fusion
  (21 shorter events, 0.2 us)
Async XLA Ops:
  7.2 149.5 %all-gather.2.cloned.1.call-start = ((), (), s32[]{:S(2)}) async-start(), calls=%async_computation | async-start | bytes 11698176 | tf_op jit(solution)/shard_map/all_gather | solution.py:112
  17.6 34.5 %copy-start = (bf16[64,448]{1,0:T(8,128)(2,1)S(1)}, bf16[64,448]{1,0:T(8,128)(2,1)}, u32[]{:S(2)}) copy-start(bf16[64,448]{1,0:T(8,128)(2,1)} %param.7) | copy-start | bytes 172036
  81.9 3.1 %copy-start.3 = (bf16[448]{0:T(512)(128)(2,1)S(1)}, bf16[448]{0:T(512)(128)(2,1)}, u32[]{:S(2)}) copy-start(bf16[448]{0:T(512)(128)(2,1)} %param.9) | copy-start | bytes 2692
  81.9 3.2 %copy-start.2 = (f32[64,8]{0,1:T(8,128)S(1)}, f32[64,8]{0,1:T(8,128)}, u32[]{:S(2)}) copy-start(f32[64,8]{0,1:T(8,128)} %param.11) | copy-start | bytes 6148
  81.9 3.2 %copy-start.1 = (bf16[8,2,1,448]{3,2,1,0:T(2,128)(2,1)S(1)}, bf16[8,2,1,448]{3,2,1,0:T(2,128)(2,1)}, u32[]{:S(2)}) copy-start(bf16[8,2,1,448]{3,2,1,0:T(2,128)(2,1)} %get-tuple-element.10) | copy-start | bytes 43012
  83.9 72.8 %copy-start.4 = (bf16[1,7168,128]{2,1,0:T(8,128)(2,1)S(1)}, bf16[1,7168,128]{2,1,0:T(8,128)(2,1)}, u32[]{:S(2)}) copy-start(bf16[1,7168,128]{2,1,0:T(8,128)(2,1)} %param.13) | copy-start | bytes 5505028
Sparse Core Ops, SparseCore 0:
  85.2 71.4 all-gather.1

commit v14 on v13

--- a/solution.py
+++ b/solution.py
@@ -130,9 +130,10 @@
     pow_part = jnp.sum(full_acc * full_acc, axis=1) / FF
     partial = jnp.concatenate([err_part, pow_part]).reshape(-1, 128)
     (gathered,) = exchange([(partial, True)], "tensor", 2, n_tensor)
-    slots = jnp.sum(gathered, axis=0).reshape(2, n_expert, CAP).transpose(1, 0, 2)
-    expert_total = jnp.sum(slots[:, 0]) / (jnp.sum(slots[:, 1]) + epsilon)
-    slot_ratios = (slots[:, 0] / (slots[:, 1] + epsilon)).reshape(n_expert, 1, CAP)
+    slots = jnp.sum(gathered, axis=0)
+    half = slots.shape[0] // 2
+    expert_total = jnp.sum(slots[:half]) / (jnp.sum(slots[half:]) + epsilon)
+    slot_ratios = (slots[:half] / (slots[half:] + epsilon)).reshape(n_expert, 1, CAP)
     (back,) = exchange([(slot_ratios, False)], "expert", 3, n_expert)
     token_error = jnp.dot(back.reshape(1, -1), weighted_slots, precision=lax.Precision.HIGHEST).reshape(tok_count)
     return (token_error, expert_total.reshape(1), hess_local.reshape(1, local_cols))

time: 204 us -> 204 us (level)
  no operation moved by 1% of the time
where the time goes in v14:
time: 204 us; the launch traced here: 203 us
  Pallas kernels  93.4 us (46%)
  waiting for transfers between devices  53.5 us (26%)
  between operations  16.7 us (8%)
  other arithmetic  15.8 us (8%)
  local copies, waits for them, and re-layouts  13.8 us (7%)
  matrix products  9.53 us (5%)
    pallas_call x6, Pallas kernels, exchange(): pl.pallas_call(kernel, out_shape=out_shape, in_specs=[pl.BlockSpec(memory...  93.4 us
    all_gather x1, waiting for transfers between devices, per_device(): column_block = lax.all_gather(own_block, 'tensor', axis=1, tiled=True)  53.5 us
    dot_general x1, matrix products, per_device(): both_acc = jnp.dot(normed, both_weights, preferred_element_type=jnp.float32)  8.35 us
    another operation x2, local copies, waits for them, and re-layouts, per_device(): attn_parts[0].reshape(tok_count, n_chip, 2, local_cols)  5.11 us
  transfers between devices with their start and end apart: 1, of which 1 were waited for; matrix products, arithmetic and copies ran while one was open for 3% of the time, Pallas kernels for 6%

profile of v14, /device:TPU:1, one launch (start us, length us, event | category | flops | bytes accessed | tf_op | source)
XLA Modules:
  0.0 202.7 jit_solution(11864263785165347503)
XLA Ops:
  7.2 0.8 copy.42
  8.0 0.1 eq.44
  8.1 0.1 eq.40
  8.2 1.3 reshape.119.refs_1_
  9.4 1.2 reduce-window.6
  10.6 0.2 slice_reduce_fusion
  10.9 0.2 fusion.16
  11.0 0.1 reduce_sum.120
  11.2 0.7 multiply_add_fusion
  11.9 0.1 copy.46
  12.0 0.5 convert_reduce_fusion
  12.5 3.5 %reshape_squeeze.3 = bf16[64,8,2,448]{3,2,1,0:T(2,128)(2,1)S(1)} reshape(bf16[1,64,7168]{2,1,0:T(8,128)(2,1)} %param.8) | data formatting | bytes 1835008 | tf_op jit(solution)/shard_map/reshape;squeeze | solution.py:86
  16.0 1.6 copy.61
  17.6 11.6 %shard_map.94 = (bf16[2,8,64,448]{3,2,1,0:T(8,128)(2,1)}, bf16[2,1,448]{2,1,0:T(2,128)(2,1)}) custom-call(bf16[2,8,64,448]{3,2,1,0:T(8,128)(2,1)} %bitcast.38, bf16[1,448]{1,0:T(2,128)(2,1)} %reshape.119.refs_1_), custom_call_target="tpu_custom_call" | custom-call | tf_op jit(solution)/shard_map/pallas_call | solution.py:64
  29.2 2.2 %fusion.11.refs_0_ = bf16[8,64,448]{2,1,0:T(8,128)(2,1)} fusion(bf16[2,8,64,448]{3,2,1,0:T(8,128)(2,1)} %get-tuple-element.7), kind=kLoop, calls=%fused_computation.24 | loop fusion | flops 917504 | bytes 1376256 | tf_op jit(solution)/shard_map/convert_element_type | solution.py:88
  31.4 19.6 %shard_map.95 = (bf16[8,64,448]{2,1,0:T(8,128)(2,1)}, bf16[8,2,1,448]{3,2,1,0:T(2,128)(2,1)}) custom-call(bf16[8,64,448]{2,1,0:T(8,128)(2,1)} %fusion.11.refs_0_, bf16[2,1,448]{2,1,0:T(2,128)(2,1)} %get-tuple-element.8.refs_1_), custom_call_target="tpu_custom_call" | custom-call | tf_op jit(solution)/shard_map/pallas_call | solution.py:64
  51.0 1.1 convert_reduce_fusion.1
  52.1 0.4 convolution_convert_fusion
  52.5 0.3 copy.48
  52.8 1.0 reshape.120
  53.9 0.1 broadcast_in_dim.14
  54.0 0.9 pad_maximum_fusion.refs_0_
  54.9 27.0 %shard_map.96 = bf16[32,85,128]{2,1,0:T(8,128)(2,1)} custom-call(bf16[32,85,128]{2,1,0:T(8,128)(2,1)} %pad_maximum_fusion.refs_0_), custom_call_target="tpu_custom_call" | custom-call | tf_op jit(solution)/shard_map/pallas_call | solution.py:64
  81.9 2.0 reshape.121
  83.9 1.1 copy.49
  85.1 0.1 copy.51
  85.1 0.1 convert_reduce_fusion.3
  85.3 0.1 reshape.127
  85.4 0.8 fusion.6
  86.2 12.6 %shard_map.97 = f32[16,6,128]{2,1,0:T(8,128)} custom-call(f32[6,128]{1,0:T(8,128)} %bitcast.41), custom_call_target="tpu_custom_call" | custom-call | tf_op jit(solution)/shard_map/pallas_call | solution.py:64
  98.7 0.9 reduce_sum.125
  99.6 1.5 convert_reduce_fusion.4
  101.1 0.5 select_reduce_fusion
  101.7 0.3 fusion.9
  102.0 1.2 multiply_divide_fusion
  103.2 53.5 %all-gather.2.cloned.1.call-done = bf16[768,7168]{0,1:T(8,128)(2,1)} async-done(((bf16[768,448]{0,1:T(8,128)(2,1)}), bf16[768,7168]{0,1:T(8,128)(2,1)}) %all-gather.2.cloned.1.call-update) | async-done | bytes 11010064 | tf_op jit(solution)/shard_map/all_gather | solution.py:112
  156.7 8.4 %fusion = f32[768,256]{0,1:T(8,128)S(1)} fusion(bf16[768,7168]{0,1:T(8,128)(2,1)} %all-gather.2.cloned.1.call-done, f32[7168]{0:T(1024)S(1)} %reshape.127, f32[768]{0:T(1024)S(1)} %rsqrt_bitcast_fusion, bf16[7168,128]{1,0:T(8,128)(2,1)S(1)} %bitcast.43, bf16[7168,128]{1,0:T(8,128)(2,1)} %bitcast.44), kind=kOutput, calls=%fused_computation.1 | convolution fusion | flops 2847932416 | bytes 15498240 | tf_op jit(solution)/shard_map/dot_general | solution.py:122
  165.1 0.1 fusion.13
  165.2 0.6 pad_maximum_fusion.1.refs_0_
  165.8 10.4 %shard_map.98 = f32[16,12,128]{2,1,0:T(8,128)} custom-call(f32[12,128]{1,0:T(8,128)} %pad_maximum_fusion.1.refs_0_), custom_call_target="tpu_custom_call" | custom-call | tf_op jit(solution)/shard_map/pallas_call | solution.py:64
  176.2 0.9 reduce_sum.128
  177.1 0.6 slice_reduce_fusion.1
  177.7 0.7 reshape.123
  178.4 12.3 %shard_map.99 = f32[32,1,24]{2,1,0:T(1,128)} custom-call(f32[32,1,24]{2,1,0:T(1,128)} %bitcast.40), custom_call_target="tpu_custom_call" | custom-call | tf_op jit(solution)/shard_map/pallas_call | solution.py:64
  190.7 0.5 broadcast.64
  191.2 1.3 reduce.10
  192.5 0.1 reshape.128
  193.9 0.8 convolution_bitcast_fusion
  (20 shorter events, 0.2 us)
Async XLA Ops:
  7.2 149.5 %all-gather.2.cloned.1.call-start = ((), (), s32[]{:S(2)}) async-start(), calls=%async_computation | async-start | bytes 11698176 | tf_op jit(solution)/shard_map/all_gather | solution.py:112
  17.6 34.5 %copy-start = (bf16[64,448]{1,0:T(8,128)(2,1)S(1)}, bf16[64,448]{1,0:T(8,128)(2,1)}, u32[]{:S(2)}) copy-start(bf16[64,448]{1,0:T(8,128)(2,1)} %param.7) | copy-start | bytes 172036
  81.9 3.1 %copy-start.3 = (bf16[448]{0:T(512)(128)(2,1)S(1)}, bf16[448]{0:T(512)(128)(2,1)}, u32[]{:S(2)}) copy-start(bf16[448]{0:T(512)(128)(2,1)} %param.9) | copy-start | bytes 2692
  81.9 3.2 %copy-start.2 = (f32[64,8]{0,1:T(8,128)S(1)}, f32[64,8]{0,1:T(8,128)}, u32[]{:S(2)}) copy-start(f32[64,8]{0,1:T(8,128)} %param.11) | copy-start | bytes 6148
  81.9 3.2 %copy-start.1 = (bf16[8,2,1,448]{3,2,1,0:T(2,128)(2,1)S(1)}, bf16[8,2,1,448]{3,2,1,0:T(2,128)(2,1)}, u32[]{:S(2)}) copy-start(bf16[8,2,1,448]{3,2,1,0:T(2,128)(2,1)} %get-tuple-element.10) | copy-start | bytes 43012
  83.9 72.8 %copy-start.4 = (bf16[1,7168,128]{2,1,0:T(8,128)(2,1)S(1)}, bf16[1,7168,128]{2,1,0:T(8,128)(2,1)}, u32[]{:S(2)}) copy-start(bf16[1,7168,128]{2,1,0:T(8,128)(2,1)} %param.13) | copy-start | bytes 5505028
Sparse Core Ops, SparseCore 0:
  85.2 71.4 all-gather.1
